TPU v7x, 128 devices: a whole 4x4x4 slice. The times are simulated.
128 devices in a mesh: gx: 2 (over core), gy: 2 (over x_lo), gz: 32 (over z, y, x_hi).
Axes of the slice: x: 4 (x_hi: 2, x_lo: 2; x = x_hi * 2 + x_lo), y: 4, z: 4, core: 2. Of those that a mesh axis runs over, the one named last changes fastest.
Arguments:
- a_diag: bfloat16 [8, 12, 256, 4096], P('gx', 'gy', 'gz'), may hold values from -0.75 to 0.75
- a_face: bfloat16 [3, 8, 12, 256, 4096], P(None, 'gx', 'gy', 'gz'), may hold values from -0.75 to 0.75
- prolong: bfloat16 [8, 12, 256, 4096], P('gx', 'gy', 'gz'), may hold values from -0.75 to 0.75
- aggregate: int32 [8, 12, 256], P('gx', 'gy', 'gz'), may hold values from 0 to 23
- pair_slot: int32 [7, 8, 12, 256], P(None, 'gx', 'gy', 'gz'), may hold values from 0 to 6
- row_owner: int32 [3072], P(('gx', 'gy', 'gz')), may hold values from 0 to 31, as said below
Outputs:
- coarse: bfloat16 [2, 2, 32, 64, 7, 4096], P('gx', 'gy', 'gz')
Inputs may be any that keep to these rules, and one draw needn't show every extreme that they name: `row_owner`: all rows of a device go to owners in its own (gx, gy) column. From each device at most 2 rows go to one owner, and in each column one owner receives exactly 2 rows from every device, so at most 64 rows reach one owner.
All inputs are finite; a program needn't handle non-finite values.
Results may differ from a plain program's by a relative error of at most 0.0049.
Values may be sent and summed in bfloat16 or wider, within the bound.
A program may use at most 256 MiB of HBM per device.

v0:
```python
import jax
import jax.numpy as jnp
from jax import lax
from jax.sharding import PartitionSpec as P

NODES = 64
SLOTS = 7
AGG_DEV = 24


def with_halo(cells, sides, width):
    for axis, dim in sides:
        count = lax.axis_size(axis)
        ends = count - 1
        head = lax.slice_in_dim(cells, 0, width, axis=dim)
        tail = lax.slice_in_dim(cells, cells.shape[dim] - width, cells.shape[dim], axis=dim)
        cells = jnp.concatenate(
            [
                lax.ppermute(tail, axis, [(i, (i + 1) % count) for i in range(ends)]),
                cells,
                lax.ppermute(head, axis, [((i + 1) % count, i) for i in range(ends)]),
            ],
            axis=dim,
        )
    return cells


def passed_along(block, axis, distance):
    devices = range(lax.axis_size(axis))
    route = [(i - distance, i) for i in devices if i - distance in devices]
    return lax.ppermute(block, axis, route)


def pick_rows(match, source_rows):
    count = match.shape[1]
    source = jnp.sum(match * jnp.arange(count, dtype=jnp.int32)[None, :], axis=1)
    present = jnp.sum(match, axis=1) > 0
    taken = jnp.take(source_rows, source, axis=0)
    return (jnp.where(present[:, None, None], taken, jnp.zeros_like(taken)), present)


def shards(a_diag, a_face, prolong, aggregate, pair_slot, row_owner):
    size_x, size_y, size_z, block = a_diag.shape
    depth = lax.axis_size("gz")
    capacity = max(2, (AGG_DEV + depth - 1) // depth)
    holding = capacity * depth
    padded = with_halo(prolong, (("gx", 0), ("gy", 1), ("gz", 2)), 1)
    rim_x = passed_along(a_face[0, size_x - 1 :], "gx", 1)
    back_x = jnp.concatenate([rim_x, a_face[0, : size_x - 1]], axis=0)
    rim_y = passed_along(a_face[1, :, size_y - 1 :], "gy", 1)
    back_y = jnp.concatenate([rim_y, a_face[1, :, : size_y - 1]], axis=1)
    rim_z = passed_along(a_face[2, :, :, size_z - 1 :], "gz", 1)
    back_z = jnp.concatenate([rim_z, a_face[2, :, :, : size_z - 1]], axis=2)

    def blocks(value):
        return value.reshape(size_x, size_y, size_z, NODES, NODES)

    def forward(left, right):
        return jnp.einsum(
            "xyzab,xyzbc->xyzac", blocks(left), blocks(right), preferred_element_type=jnp.float32
        ).astype(jnp.bfloat16)

    def backward(left, right):
        return jnp.einsum(
            "xyzba,xyzbc->xyzac", blocks(left), blocks(right), preferred_element_type=jnp.float32
        ).astype(jnp.bfloat16)

    center = padded[1:-1, 1:-1, 1:-1]
    pairs = [
        (forward, a_diag, center),
        (backward, back_x, padded[:-2, 1:-1, 1:-1]),
        (forward, a_face[0], padded[2:, 1:-1, 1:-1]),
        (backward, back_y, padded[1:-1, :-2, 1:-1]),
        (forward, a_face[1], padded[1:-1, 2:, 1:-1]),
        (backward, back_z, padded[1:-1, 1:-1, :-2]),
        (forward, a_face[2], padded[1:-1, 1:-1, 2:]),
    ]
    key_ids = jnp.arange(AGG_DEV * SLOTS, dtype=jnp.int32)[:, None]
    summed = jnp.zeros((AGG_DEV * SLOTS, block), jnp.float32)
    for number, (product, left, right) in enumerate(pairs):
        couple = product(left, right)
        term = jnp.einsum(
            "xyzba,xyzbc->xyzac", blocks(center), couple, preferred_element_type=jnp.float32
        ).reshape(-1, block)
        keys = (aggregate * SLOTS + pair_slot[number]).reshape(1, -1)
        select = (key_ids == keys).astype(jnp.float32)
        summed = summed + jnp.dot(
            select, term, precision=lax.Precision.HIGHEST, preferred_element_type=jnp.float32
        )
    rows = summed.reshape(AGG_DEV, SLOTS, block).astype(jnp.bfloat16)
    incoming, owner_all = (
        lax.all_gather(rows, "gz", axis=0, tiled=True),
        lax.all_gather(row_owner, "gz", axis=0, tiled=True),
    )
    valid = (owner_all == lax.axis_index("gz")).astype(jnp.int32)
    rank = jnp.cumsum(valid) - 1
    targets = jnp.arange(holding, dtype=jnp.int32)[:, None]
    match = ((valid[None, :] > 0) & (rank[None, :] == targets)).astype(jnp.int32)
    result, _ = pick_rows(match, incoming)
    return result.reshape(1, 1, 1, holding, SLOTS, block)


def solution(mesh):
    return jax.shard_map(
        shards,
        mesh=mesh,
        in_specs=(
            P("gx", "gy", "gz", None),
            P(None, "gx", "gy", "gz", None),
            P("gx", "gy", "gz", None),
            P("gx", "gy", "gz"),
            P(None, "gx", "gy", "gz"),
            P(("gx", "gy", "gz")),
        ),
        out_specs=P("gx", "gy", "gz", None, None, None),
        check_vma=False,
    )
```

profile of v0, /device:TPU:0, one launch (start us, length us, event | category | flops | bytes accessed | tf_op | source)
XLA Modules:
  0.0 761.5 jit_solution(11696326981371261283)
XLA Ops:
  12.9 4.7 collective-permute-start.3
  26.4 5.3 collective-permute-start.6
  36.0 4.7 fusion.85
  40.7 5.5 reshape.142
  46.2 6.4 fusion.28
  61.7 4.8 concatenate.55
  70.9 4.7 concatenate.50
  79.9 6.6 copy.136
  86.4 5.8 reshape.144
  94.9 5.5 reshape_squeeze.9
  103.2 5.5 reshape_squeeze.10
  110.0 5.1 reshape.170
  115.1 4.5 copy.157
  120.9 5.7 reshape_squeeze.11
  128.0 5.2 fusion.70
  141.5 4.5 constant_dynamic-update-slice_fusion.1
  152.0 5.5 reshape.145
  162.4 7.5 fusion.31
  169.9 6.6 copy.141
  176.5 5.8 reshape.146
  182.3 5.6 reshape.147
  187.9 8.2 %fusion.34 = f32[4,6,8,64,64]{3,4,2,1,0:T(8,128)} fusion(bf16[4,6,8,64,64]{4,3,2,1,0:T(8,128)(2,1)S(1)} %reshape.143, bf16[4,6,8,64,64]{4,3,2,1,0:T(8,128)(2,1)} %reshape.147, bf16[4,6,8,64,64]{4,3,2,1,0:T(8,128)(2,1)} %reshape_squeeze.9), kind=kOutput, calls=%fused_computation.38 | convolution fusion | flops 202113024 | bytes 7864320 | tf_op jit(solution)/shard_map/xyzba,xyzbc->xyzac/dot_general | solution.py:82
  196.1 6.6 copy.144
  202.6 5.8 reshape.148
  208.5 4.6 convolution_add_fusion.5
  216.6 13.4 %collective-permute-start.7 = (bf16[6,8,1,4096]{3,1,2,0:T(8,128)(2,1)S(1)}, bf16[6,8,1,4096]{3,1,2,0:T(8,128)(2,1)S(1)}, u32[]{:S(2)}, u32[]{:S(2)}) collective-permute-start(bf16[6,8,1,4096]{3,1,2,0:T(8,128)(2,1)S(1)} %copy.158), channel_id=1, source_target_pairs={{0,1},{1,2},{2,3},{3,4},{4,5},{5,6},{6,7},{7,8},{8,9},{9,10},{10,1... | collective-permute-start | bytes 1179656 | tf_op jit(solution)/shard_map/ppermute | solution.py:19
  236.0 6.8 collective-permute-done.8
  243.6 6.5 pad_maximum_fusion
  250.1 5.5 reshape.149
  255.6 7.5 fusion.37
  263.1 6.6 copy.149
  269.6 5.8 reshape.150
  275.5 5.6 reshape.151
  281.0 8.2 %fusion.40 = f32[4,6,8,64,64]{3,4,2,1,0:T(8,128)} fusion(bf16[4,6,8,64,64]{4,3,2,1,0:T(8,128)(2,1)S(1)} %reshape.143, bf16[4,6,8,64,64]{4,3,2,1,0:T(8,128)(2,1)} %reshape.151, bf16[4,6,8,64,64]{4,3,2,1,0:T(8,128)(2,1)} %reshape_squeeze.10), kind=kOutput, calls=%fused_computation.40 | convolution fusion | flops 202113024 | bytes 7864320 | tf_op jit(solution)/shard_map/xyzba,xyzbc->xyzac/dot_general | solution.py:82
  289.2 6.6 copy.152
  295.8 5.8 reshape.152
  301.6 5.8 reshape.153
  307.4 7.4 fusion.43
  314.8 6.6 copy.161
  321.3 5.9 reshape.154
  327.2 5.6 reshape.155
  332.7 8.2 %fusion.46 = f32[4,6,8,64,64]{3,4,2,1,0:T(8,128)} fusion(bf16[4,6,8,64,64]{4,3,2,1,0:T(8,128)(2,1)S(1)} %reshape.143, bf16[4,6,8,64,64]{4,3,2,1,0:T(8,128)(2,1)} %reshape.155, bf16[4,6,8,64,64]{4,3,2,1,0:T(8,128)(2,1)} %reshape_squeeze.11), kind=kOutput, calls=%fused_computation.42 | convolution fusion | flops 202113024 | bytes 7864320 | tf_op jit(solution)/shard_map/xyzba,xyzbc->xyzac/dot_general | solution.py:82
  340.9 6.6 copy.166
  347.5 6.2 reshape.156
  367.5 20.9 %all-reduce = s32[768]{0:T(1024)S(1)} all-reduce(s32[768]{0:T(1024)S(1)} %dynamic-update-slice), channel_id=1, replica_groups=mesh['gx'=2,'gy'=2,'gz'=32] {'gz'}, use_global_device_ids=true, to_apply=%add | all-reduce | flops 768 | bytes 6144
  389.1 312.2 %all-gather.2.cloned.1.call-done = bf16[768,7,4096]{2,0,1:T(8,128)(2,1)} async-done(((bf16[24,7,4096]{2,0,1:T(8,128)(2,1)}), bf16[768,7,4096]{2,0,1:T(8,128)(2,1)}) %all-gather.2.cloned.1.call-update) | async-done | bytes 44040208 | tf_op jit(solution)/shard_map/all_gather | solution.py:92
  701.3 39.6 %copy.168 = bf16[768,7,4096]{2,1,0:T(8,128)(2,1)} copy(bf16[768,7,4096]{2,0,1:T(8,128)(2,1)} %all-gather.2.cloned.1.call-done) | data formatting | bytes 88080384 | tf_op jit(solution)/shard_map/all_gather | solution.py:92
  740.9 6.4 gather_fusion
  (113 shorter events, 96.5 us)
Async XLA Ops:
  6.5 694.8 %all-gather.2.cloned.1.call-start = ((), (), s32[]{:S(2)}) async-start(), calls=%async_computation | async-start | bytes 45416448 | tf_op jit(solution)/shard_map/all_gather | solution.py:92
  8.6 132.8 %collective-permute-start.1 = (bf16[1,6,8,4096]{3,2,1,0:T(8,128)(2,1)}, bf16[1,6,8,4096]{3,2,1,0:T(8,128)(2,1)S(1)}, u32[]{:S(2)}, u32[]{:S(2)}) collective-permute-start(bf16[1,6,8,4096]{3,2,1,0:T(8,128)(2,1)} %get-tuple-element.24), channel_id=1, source_target_pairs={{0,64},{1,65},{2,66},{3,67},{4,68},{5,69},{6,70},{7,71},{8,72},{9,... | collective-permute-start | bytes 1179656 | tf_op jit(solution)/shard_map/ppermute | solution.py:19
  9.9 131.6 %collective-permute-start.2 = (bf16[1,6,8,4096]{3,2,1,0:T(8,128)(2,1)}, bf16[1,6,8,4096]{3,2,1,0:T(8,128)(2,1)}, u32[]{:S(2)}, u32[]{:S(2)}) collective-permute-start(bf16[1,6,8,4096]{3,2,1,0:T(8,128)(2,1)} %get-tuple-element.23), channel_id=1, source_target_pairs={{64,0},{65,1},{66,2},{67,3},{68,4},{69,5},{70,6},{71,7},{72,8},{73... | collective-permute-start | bytes 1179656 | tf_op jit(solution)/shard_map/ppermute | solution.py:21
  12.9 124.3 %collective-permute-start.3 = (bf16[4,1,8,4096]{3,2,0,1:T(8,128)(2,1)}, bf16[4,1,8,4096]{3,2,0,1:T(8,128)(2,1)}, u32[]{:S(2)}, u32[]{:S(2)}) collective-permute-start(bf16[4,1,8,4096]{3,2,0,1:T(8,128)(2,1)} %slice_bitcast_fusion.1), channel_id=1, source_target_pairs={{0,32},{1,33},{2,34},{3,35},{4,36},{5,37},{6,38},{7,39},{8,40},{9,... | collective-permute-start | bytes 786440 | tf_op jit(solution)/shard_map/ppermute | solution.py:31
  19.3 138.1 %collective-permute-start = (bf16[1,6,8,4096]{3,2,1,0:T(8,128)(2,1)}, bf16[1,6,8,4096]{3,2,1,0:T(8,128)(2,1)}, u32[]{:S(2)}, u32[]{:S(2)}) collective-permute-start(bf16[1,6,8,4096]{3,2,1,0:T(8,128)(2,1)} %slice_bitcast_fusion), channel_id=1, source_target_pairs={{0,64},{1,65},{2,66},{3,67},{4,68},{5,69},{6,70},{7,71},{8,72},{9,... | collective-permute-start | bytes 1179656 | tf_op jit(solution)/shard_map/ppermute | solution.py:31
  26.4 106.8 %collective-permute-start.6 = (bf16[4,6,1,4096]{3,0,1,2:T(4,128)(2,1)}, bf16[4,6,1,4096]{3,0,1,2:T(4,128)(2,1)}, u32[]{:S(2)}, u32[]{:S(2)}) collective-permute-start(bf16[4,6,1,4096]{3,0,1,2:T(4,128)(2,1)} %bitcast.120), channel_id=1, source_target_pairs={{0,1},{1,2},{2,3},{3,4},{4,5},{5,6},{6,7},{7,8},{8,9},{9,10},{10,1... | collective-permute-start | bytes 589832 | tf_op jit(solution)/shard_map/ppermute | solution.py:31
  46.2 6.4 copy-start.8
  147.1 1.4 copy-start
  149.3 63.7 %collective-permute-start.4 = (bf16[6,1,8,4096]{3,2,1,0:T(8,128)(2,1)}, bf16[6,1,8,4096]{3,2,1,0:T(8,128)(2,1)S(1)}, u32[]{:S(2)}, u32[]{:S(2)}) collective-permute-start(bf16[6,1,8,4096]{3,2,1,0:T(8,128)(2,1)} %get-tuple-element.19), channel_id=1, source_target_pairs={{0,32},{1,33},{2,34},{3,35},{4,36},{5,37},{6,38},{7,39},{8,40},{9,... | collective-permute-start | bytes 1179656 | tf_op jit(solution)/shard_map/ppermute | solution.py:19
  150.7 62.4 %collective-permute-start.5 = (bf16[6,1,8,4096]{3,2,1,0:T(8,128)(2,1)}, bf16[6,1,8,4096]{3,2,1,0:T(8,128)(2,1)}, u32[]{:S(2)}, u32[]{:S(2)}) collective-permute-start(bf16[6,1,8,4096]{3,2,1,0:T(8,128)(2,1)} %get-tuple-element.18), channel_id=1, source_target_pairs={{32,0},{33,1},{34,2},{35,3},{36,4},{37,5},{38,6},{39,7},{40,8},{41... | collective-permute-start | bytes 1179656 | tf_op jit(solution)/shard_map/ppermute | solution.py:21
  202.6 5.8 copy-start.13
  208.4 4.7 copy-start.1
  213.1 18.7 %copy-start.3 = (f32[192,4096]{1,0:T(8,128)S(1)}, f32[192,4096]{1,0:T(8,128)}, u32[]{:S(2)}) copy-start(f32[192,4096]{1,0:T(8,128)} %reshape.148) | copy-start | bytes 9437188
  213.1 18.7 %copy-start.12 = (s32[192]{0:T(256)S(1)}, s32[192]{0:T(256)}, u32[]{:S(2)}) copy-start(s32[192]{0:T(256)} %eq.138) | copy-start | bytes 2308
  216.6 18.6 %collective-permute-start.7 = (bf16[6,8,1,4096]{3,1,2,0:T(8,128)(2,1)S(1)}, bf16[6,8,1,4096]{3,1,2,0:T(8,128)(2,1)S(1)}, u32[]{:S(2)}, u32[]{:S(2)}) collective-permute-start(bf16[6,8,1,4096]{3,1,2,0:T(8,128)(2,1)S(1)} %copy.158), channel_id=1, source_target_pairs={{0,1},{1,2},{2,3},{3,4},{4,5},{5,6},{6,7},{7,8},{8,9},{9,10},{10,1... | collective-permute-start | bytes 1179656 | tf_op jit(solution)/shard_map/ppermute | solution.py:19
  230.5 12.3 %collective-permute-start.8 = (bf16[6,8,1,4096]{3,1,2,0:T(8,128)(2,1)S(1)}, bf16[6,8,1,4096]{3,1,2,0:T(8,128)(2,1)S(1)}, u32[]{:S(2)}, u32[]{:S(2)}) collective-permute-start(bf16[6,8,1,4096]{3,1,2,0:T(8,128)(2,1)S(1)} %copy.163), channel_id=1, source_target_pairs={{1,0},{2,1},{3,2},{4,3},{5,4},{6,5},{7,6},{8,7},{9,8},{10,9},{11,1... | collective-permute-start | bytes 1179656 | tf_op jit(solution)/shard_map/ppermute | solution.py:21
  301.6 5.8 copy-start.7
  347.5 6.3 copy-start.2
  347.5 6.3 copy-start.9
  353.7 3.9 copy-start.4
  353.8 3.9 copy-start.10
  357.6 1.9 copy-start.5
  357.6 1.9 copy-start.11
  359.6 1.9 copy-start.6
  359.6 1.9 copy-start.14
  363.5 2.5 copy-start.16
  363.5 3.7 copy-start.15
Sparse Core Ops, SparseCore 0:
  366.1 335.2 all-gather.1
where the time goes:
time: 774 us; the launch traced here: 762 us
  waiting for transfers between devices  319 us (41%)
  local copies, waits for them, and re-layouts  278 us (36%)
  matrix products  76.1 us (10%)
  starting transfers between devices  34.2 us (4%)
  blocking collectives  20.9 us (3%)
  other arithmetic  18.7 us (2%)
  between operations  15 us (2%)
    all_gather x1, waiting for transfers between devices, shards(): lax.all_gather(rows, 'gz', axis=0, tiled=True)  312 us
    dot_general x7, matrix products, shards(): jnp.einsum('xyzba,xyzbc->xyzac', blocks(center), couple, preferred_elemen...  53.3 us
    dot_general x7, local copies, waits for them, and re-layouts, shards(): jnp.einsum('xyzba,xyzbc->xyzac', blocks(center), couple, preferred_elemen...  45.9 us
    reshape x8, local copies, waits for them, and re-layouts, blocks(): return value.reshape(size_x, size_y, size_z, NODES, NODES)  43.2 us
    reshape x7, local copies, waits for them, and re-layouts, shards(): term = jnp.einsum('xyzba,xyzbc->xyzac', blocks(center), couple, preferred...  41.2 us
    all_gather x1, local copies, waits for them, and re-layouts, shards(): lax.all_gather(rows, 'gz', axis=0, tiled=True)  39.6 us
    dot_general x7, matrix products, shards(): jnp.dot(select, term, precision=lax.Precision.HIGHEST, preferred_element_...  22.8 us
    unnamed x1, blocking collectives  20.9 us
  transfers between devices with their start and end apart: 10, of which 2 were waited for; matrix products, arithmetic and copies ran while one was open for 25% of the time, Pallas kernels for 0%

commit v1 on v0

v1 whole, which is shorter than its diff:
```python
import jax
import jax.numpy as jnp
from jax import lax
from jax.experimental import pallas as pl
from jax.experimental.pallas import tpu as pltpu
from jax.sharding import PartitionSpec as P

NODES = 64
SLOTS = 7
AGG_DEV = 24
BX, BY, BZ = 4, 6, 8
LINES = BX * BY
PLACES = 2
ROW = SLOTS * NODES * NODES // 128
PACK = PLACES * ROW + 16
KEYS = AGG_DEV * SLOTS
F32 = jnp.float32
BF16 = jnp.bfloat16


def lane_low(shape):
    return lax.broadcasted_iota(jnp.int32, shape, 1) < 64


def spread(line, scratch):
    values = line.astype(F32)
    for tile in range(32):
        scratch[pl.ds(tile, 8, stride=32), :] = values[:, tile * 128 : tile * 128 + 128]


def spread_twice(line, natural, by_parity):
    values = line.astype(F32)
    low = lane_low((8, 128))
    for tile in range(32):
        here = values[:, tile * 128 : tile * 128 + 128]
        swapped = pltpu.roll(here, 64, axis=1)
        even = jnp.where(low, here, swapped)
        odd = jnp.where(low, swapped, here)
        if natural is not None:
            natural[pl.ds(2 * tile, 8, stride=64), :] = even
            natural[pl.ds(2 * tile + 1, 8, stride=64), :] = odd
        if by_parity is not None:
            by_parity[pl.ds(tile, 8, stride=64), :] = even
            by_parity[pl.ds(32 + tile, 8, stride=64), :] = odd


def compute_kernel(
    agg, slot, owner,
    a_diag, a_face, prolong, rim_x, rim_y, rim_z,
    p_xm, p_xp, p_ym, p_yp, p_zm, p_zp,
    send,
    ra_d, ra_x, ra_y, ra_z, right, left, work_a, work_b, work_c,
    acc_f, acc_b, rows, counts, tally, sems, count_sem,
):
    def store_spread(line, dest, base):
        spread(line, work_a)
        dest[pl.ds(pl.multiple_of(base, 32), 256), :] = work_a[...].astype(BF16)

    right_xp, right_yp, right_zp = LINES, LINES + BY, LINES + BY + BX
    left_xm, left_ym, left_zm = LINES, LINES + BY, LINES + BY + BX

    def store_right(base):
        right[pl.ds(pl.multiple_of(base * 512, 512), 512), :] = work_b[...].astype(BF16)

    def store_left(base):
        low = lane_low((64, 128))
        for pair in range(4):
            first = work_c[pair * 128 : pair * 128 + 64, :]
            second = work_c[pair * 128 + 64 : pair * 128 + 128, :]
            flipped = jnp.where(low, first, second).T
            left[pl.ds(pl.multiple_of(base * 512 + pair * 128, 128), 128), :] = flipped.astype(BF16)

    acc_f[...] = jnp.zeros_like(acc_f)
    acc_b[...] = jnp.zeros_like(acc_b)

    @pl.loop(0, LINES)
    def _(line):
        spread_twice(prolong[line], work_b, work_c)
        store_right(line)
        store_left(line)
        store_spread(a_diag[line], ra_d, line * 256)
        store_spread(a_face[0, line], ra_x, (line + BY) * 256)
        store_spread(a_face[1, line], ra_y, (line + line // BY + 1) * 256)
        store_spread(a_face[2, line], ra_z, line * 288 + 32)

    @pl.loop(0, BY)
    def _(line):
        store_spread(rim_x[line], ra_x, line * 256)
        spread_twice(p_xm[line], None, work_c)
        store_left(left_xm + line)
        spread_twice(p_xp[line], work_b, None)
        store_right(right_xp + line)

    @pl.loop(0, BX)
    def _(line):
        store_spread(rim_y[line], ra_y, line * (BY + 1) * 256)
        spread_twice(p_ym[line], None, work_c)
        store_left(left_ym + line)
        spread_twice(p_yp[line], work_b, None)
        store_right(right_yp + line)

    @pl.loop(0, LINES // 8)
    def _(line):
        spread(rim_z[line], work_a)
        for k in range(8):
            at = (line * 8 + k) * 288
            ra_z[pl.ds(pl.multiple_of(at, 32), 32), :] = work_a[k * 32 : k * 32 + 32, :].astype(BF16)
        spread_twice(p_zm[line], None, work_c)
        store_left(left_zm + line)
        spread_twice(p_zp[line], work_b, None)
        store_right(right_zp + line)

    def products(cell, blocks):
        low = lane_low((64, 128))
        block = right[pl.ds(pl.multiple_of(cell * 64, 64), 64), :]
        zero = jnp.zeros_like(block)
        weight = jnp.concatenate([jnp.where(low, block, zero), jnp.where(low, zero, block)], axis=0)
        stack = [ref[pl.ds(pl.multiple_of(at, 32), 32), :] for ref, at, _, _, _ in blocks]
        stack = jnp.concatenate(stack, axis=0) if len(stack) > 1 else stack[0]
        both = jnp.dot(stack, weight, preferred_element_type=F32)
        turned = pltpu.roll(both, 64, axis=1)
        for number, (_, _, flip, key_f, key_b) in enumerate(blocks):
            part = slice(number * 32, number * 32 + 32)
            couple = jnp.concatenate([both[part], turned[part]], axis=0).astype(BF16)
            lhs = left[pl.ds(pl.multiple_of(flip * 64, 64), 64), :]
            term = jnp.dot(lhs, couple, preferred_element_type=F32)
            if key_f is not None:
                acc_f[key_f] += term
            if key_b is not None:
                acc_b[key_b] += term

    def key(e, number):
        return agg[e] * SLOTS + slot[number, e]

    @pl.loop(0, LINES)
    def _(line):
        x, y = line // BY, line % BY
        flip_x = jnp.where(x > 0, (line - BY) * 8, (left_xm + y) * 8)
        flip_y = jnp.where(y > 0, (line - 1) * 8, (left_ym + x) * 8)
        for z in range(BZ):
            n = line * BZ + z
            back_x = jnp.where(x > 0, n - BY * BZ, 0)
            back_y = jnp.where(y > 0, n - BZ, 0)
            key_x = jnp.where(x > 0, key(back_x, 2), KEYS)
            key_y = jnp.where(y > 0, key(back_y, 4), KEYS)
            products(
                n,
                [
                    (ra_d, n * 32, n, key(n, 0), None),
                    (ra_x, n * 32, flip_x + z, key_x, key(n, 1)),
                    (ra_y, (line + x) * 256 + z * 32, flip_y + z, key_y, key(n, 3)),
                    (
                        ra_z,
                        line * 288 + z * 32,
                        left_zm * 8 + line if z == 0 else n - 1,
                        None if z == 0 else key(n - 1, 6),
                        key(n, 5),
                    ),
                ],
            )
        e = line * BZ + BZ - 1
        products(right_zp * 8 + line, [(ra_z, line * 288 + BZ * 32, e, key(e, 6), None)])

    @pl.loop(0, BY)
    def _(y):
        for z in range(BZ):
            e = ((BX - 1) * BY + y) * BZ + z
            at = (BX * BY + y) * 256 + z * 32
            products((right_xp + y) * 8 + z, [(ra_x, at, e, key(e, 2), None)])

    @pl.loop(0, BX)
    def _(x):
        for z in range(BZ):
            e = (x * BY + BY - 1) * BZ + z
            at = (x * (BY + 1) + BY) * 256 + z * 32
            products((right_yp + x) * 8 + z, [(ra_y, at, e, key(e, 4), None)])

    depth = send.shape[0]

    @pl.loop(0, depth)
    def _(c):
        tally[c] = 0

    @pl.loop(0, AGG_DEV)
    def _(r):
        low = lane_low((32, 128))
        for s in range(SLOTS):
            k = r * SLOTS + s
            work_b[0:64, 0:64] = acc_f[k, :, 0:64] + acc_b[k].T[0:64, :]
            even = work_b[pl.ds(0, 32, stride=2), :]
            odd = work_b[pl.ds(1, 32, stride=2), :]
            row = jnp.where(low, even, pltpu.roll(odd, 64, axis=1)).astype(BF16)
            rows[pl.ds(pl.multiple_of(r * ROW + s * 32, 32), 32), :] = row
        c = owner[r]
        place = tally[c]
        tally[c] = place + 1
        pltpu.make_async_copy(
            rows.at[pl.ds(pl.multiple_of(r * ROW, 32), ROW)],
            send.at[c, pl.ds(pl.multiple_of(place * ROW, 32), ROW)],
            sems.at[r],
        ).start()

    @pl.loop(0, depth)
    def _(c):
        counts[c] = jnp.full((16, 128), tally[c], jnp.int32).astype(F32).astype(BF16)

    told = pltpu.make_async_copy(counts, send.at[:, pl.ds(PLACES * ROW, 16)], count_sem)
    told.start()
    told.wait()

    @pl.loop(0, AGG_DEV)
    def _(r):
        pltpu.make_async_copy(rows.at[pl.ds(0, ROW)], send.at[0, pl.ds(0, ROW)], sems.at[r]).wait()


def coarse_rows(agg, slot, owner, arrays, depth):
    smem = pl.BlockSpec(memory_space=pltpu.SMEM)
    vmem = pl.BlockSpec(memory_space=pltpu.VMEM)
    lines_right = LINES + BY + BX + LINES // 8
    return pl.pallas_call(
        compute_kernel,
        out_shape=jax.ShapeDtypeStruct((depth, PACK, 128), BF16),
        in_specs=[smem] * 3 + [vmem] * len(arrays),
        out_specs=pl.BlockSpec(memory_space=pl.ANY),
        scratch_shapes=[
            pltpu.VMEM((LINES * 256, 128), BF16),
            pltpu.VMEM(((LINES + BY) * 256, 128), BF16),
            pltpu.VMEM((BX * (BY + 1) * 256, 128), BF16),
            pltpu.VMEM((LINES * 288, 128), BF16),
            pltpu.VMEM((lines_right * 512, 128), BF16),
            pltpu.VMEM((lines_right * 512, 64), BF16),
            pltpu.VMEM((256, 128), F32),
            pltpu.VMEM((512, 128), F32),
            pltpu.VMEM((512, 128), F32),
            pltpu.VMEM((KEYS + 1, 64, 128), F32),
            pltpu.VMEM((KEYS + 1, 64, 128), F32),
            pltpu.VMEM((AGG_DEV * ROW, 128), BF16),
            pltpu.VMEM((depth, 16, 128), BF16),
            pltpu.SMEM((depth,), jnp.int32),
            pltpu.SemaphoreType.DMA((AGG_DEV,)),
            pltpu.SemaphoreType.DMA,
        ],
        compiler_params=pltpu.CompilerParams(vmem_limit_bytes=63 << 20),
        name="coarse_rows",
    )(agg, slot, owner, *arrays)


GROUP = 8


def place_kernel(source, total, taken, out, work):
    step = pl.program_id(0)
    for k in range(GROUP):
        t = step * GROUP + k

        @pl.when(t < total[0])
        def _():
            at = source[t]
            row = taken[at // PLACES, pl.ds(pl.multiple_of(at % PLACES * ROW, 32), ROW), :]
            work[k, 0:ROW, :] = row.astype(F32)
            for tile in range(32):
                piece = work[k, pl.ds(tile, SLOTS, stride=32), :]
                out[k, :, tile * 128 : tile * 128 + 128] = piece.astype(BF16)

        @pl.when(t >= total[0])
        def _():
            out[k] = jnp.zeros((SLOTS, NODES * NODES), BF16)


def place_rows(source, total, taken):
    count = source.shape[0]
    return pl.pallas_call(
        place_kernel,
        out_shape=jax.ShapeDtypeStruct((count, SLOTS, NODES * NODES), BF16),
        grid_spec=pltpu.PrefetchScalarGridSpec(
            num_scalar_prefetch=2,
            grid=(count // GROUP,),
            in_specs=[pl.BlockSpec(memory_space=pltpu.VMEM)],
            out_specs=pl.BlockSpec((GROUP, SLOTS, NODES * NODES), lambda i, s, n: (i, 0, 0)),
            scratch_shapes=[pltpu.VMEM((GROUP, 256, 128), F32)],
        ),
        compiler_params=pltpu.CompilerParams(vmem_limit_bytes=40 << 20),
        name="place_rows",
    )(source, total, taken)


def to_next(block, axis):
    count = lax.axis_size(axis)
    return lax.ppermute(block, axis, [(i, i + 1) for i in range(count - 1)])


def to_previous(block, axis):
    count = lax.axis_size(axis)
    return lax.ppermute(block, axis, [(i + 1, i) for i in range(count - 1)])


def shards(a_diag, a_face, prolong, aggregate, pair_slot, row_owner):
    block = a_diag.shape[-1]
    depth = lax.axis_size("gz")
    holding = PLACES * depth

    def face_z(cells):
        return cells.reshape(LINES // 8, 8, block)

    arrays = [
        a_diag.reshape(LINES, BZ, block),
        a_face.reshape(3, LINES, BZ, block),
        prolong.reshape(LINES, BZ, block),
        to_next(a_face[0, BX - 1], "gx"),
        to_next(a_face[1, :, BY - 1], "gy"),
        to_next(face_z(a_face[2, :, :, BZ - 1]), "gz"),
        to_next(prolong[BX - 1], "gx"),
        to_previous(prolong[0], "gx"),
        to_next(prolong[:, BY - 1], "gy"),
        to_previous(prolong[:, 0], "gy"),
        to_next(face_z(prolong[:, :, BZ - 1]), "gz"),
        to_previous(face_z(prolong[:, :, 0]), "gz"),
    ]
    send = coarse_rows(
        aggregate.reshape(-1), pair_slot.reshape(SLOTS, -1), row_owner, arrays, depth
    )
    taken = lax.all_to_all(send, "gz", 0, 0, tiled=True)
    count = taken[:, PLACES * ROW, 0].astype(jnp.int32)
    ends = jnp.cumsum(count)
    spot = jnp.arange(holding, dtype=jnp.int32)
    origin = jnp.sum((ends[None, :] <= spot[:, None]).astype(jnp.int32), axis=1)
    starts = jnp.sum(
        jnp.where(jnp.arange(depth)[None, :] < origin[:, None], count[None, :], 0), axis=1
    )
    source = jnp.minimum(origin * PLACES + (spot - starts), holding - 1)
    coarse = place_rows(source, ends[-1:], taken)
    return coarse.reshape(1, 1, 1, holding, SLOTS, block)


def solution(mesh):
    return jax.shard_map(
        shards,
        mesh=mesh,
        in_specs=(
            P("gx", "gy", "gz", None),
            P(None, "gx", "gy", "gz", None),
            P("gx", "gy", "gz", None),
            P("gx", "gy", "gz"),
            P(None, "gx", "gy", "gz"),
            P(("gx", "gy", "gz")),
        ),
        out_specs=P("gx", "gy", "gz", None, None, None),
        check_vma=False,
    )
```

time: 774 us -> 230 us (0.30); the launches traced: 762 us -> 227 us
  waiting for transfers between devices: 319 us -> 3.24 us
  local copies, waits for them, and re-layouts: 278 us -> 23.2 us
  Pallas kernels: 0 us -> 114 us
  matrix products: 76.1 us -> 0 us
  blocking collectives: 20.9 us -> 57 us
  other arithmetic: 18.7 us -> 1.88 us
  between operations: 15 us -> 0.19 us
    all_gather x1 -> x0, waiting for transfers between devices: 312 us -> none  [shards(): lax.all_gather(rows, 'gz', axis=0, tiled=True)]
    pallas_call x0 -> x2, Pallas kernels: none -> 114 us  [the longest x1 109 us: coarse_rows(): pl.pallas_call(compute_kernel, out_shape=jax.ShapeDtypeStruct((depth, PAC...]
    reshape x15 -> x3, local copies, waits for them, and re-layouts: 84.5 us -> 5.48 us  [the longest x1 4.12 us: shards(): return coarse.reshape(1, 1, 1, holding, SLOTS, block)]
    dot_general x14 -> x0, matrix products: 76.1 us -> none  [the longest x7 53.3 us: shards(): jnp.einsum('xyzba,xyzbc->xyzac', blocks(center), couple, preferred_elemen...]
    all_to_all x0 -> x1, blocking collectives: none -> 57 us  [shards(): taken = lax.all_to_all(send, 'gz', 0, 0, tiled=True)]
    dot_general x7 -> x0, local copies, waits for them, and re-layouts: 45.9 us -> none  [shards(): jnp.einsum('xyzba,xyzbc->xyzac', blocks(center), couple, preferred_elemen...]
    concatenate x13 -> x0, local copies, waits for them, and re-layouts: 42 us -> none  [the longest x4 13.9 us: shards(): back_x = jnp.concatenate([rim_x, a_face[0, :size_x - 1]], axis=0)]
    all_gather x1 -> x0, local copies, waits for them, and re-layouts: 39.6 us -> none  [shards(): lax.all_gather(rows, 'gz', axis=0, tiled=True)]
  transfers between devices with their start and end apart: 10 -> 9, of which waited for: 2 -> 3; matrix products, arithmetic and copies ran while one was open for 25% -> 5% of each run, Pallas kernels for 0% -> 0%
where the time goes in v1:
time: 230 us; the launch traced here: 227 us
  Pallas kernels  114 us (50%)
  blocking collectives  57 us (25%)
  starting transfers between devices  28.2 us (12%)
  local copies, waits for them, and re-layouts  23.2 us (10%)
  waiting for transfers between devices  3.24 us (1%)
    pallas_call x1, Pallas kernels, coarse_rows(): pl.pallas_call(compute_kernel, out_shape=jax.ShapeDtypeStruct((depth, PAC...  109 us
    all_to_all x1, blocking collectives, shards(): taken = lax.all_to_all(send, 'gz', 0, 0, tiled=True)  57 us
    ppermute x6, starting transfers between devices, to_next(): return lax.ppermute(block, axis, [(i, i + 1) for i in range(count - 1)])  24.3 us
    unnamed x18, local copies, waits for them, and re-layouts  5.61 us
  transfers between devices with their start and end apart: 9, of which 3 were waited for; matrix products, arithmetic and copies ran while one was open for 5% of the time, Pallas kernels for 0%

profile of v1, /device:TPU:0, one launch (start us, length us, event | category | flops | bytes accessed | tf_op | source)
XLA Modules:
  0.0 227.2 jit_solution(10616020371858623332)
XLA Ops:
  0.0 2.7 %slice_reduce_fusion.2 = bf16[4,6,4096]{2,1,0:T(8,128)(2,1)S(1)} fusion(bf16[3,4,6,8,4096]{4,3,2,1,0:T(8,128)(2,1)} %param.7), kind=kLoop, calls=%fused_computation.4 | loop fusion | bytes 393216 | tf_op jit(solution)/shard_map/slice | solution.py:311
  2.8 0.7 reshape_squeeze.9
  3.5 5.7 %collective-permute-start.2 = (bf16[3,8,4096]{2,1,0:T(8,128)(2,1)}, bf16[3,8,4096]{2,1,0:T(8,128)(2,1)}, u32[]{:S(2)}, u32[]{:S(2)}) collective-permute-start(bf16[3,8,4096]{2,1,0:T(8,128)(2,1)} %reshape_squeeze.9), channel_id=1, source_target_pairs={{0,1},{1,2},{2,3},{3,4},{4,5},{5,6},{6,7},{7,8},{8,9},{9,10},{10,1... | collective-permute-start | bytes 589832 | tf_op jit(solution)/shard_map/ppermute | solution.py:289
  9.2 1.0 slice_bitcast_fusion.5
  10.2 3.2 %collective-permute-start.1 = (bf16[4,8,4096]{2,1,0:T(8,128)(2,1)S(1)}, bf16[4,8,4096]{2,1,0:T(8,128)(2,1)}, u32[]{:S(2)}, u32[]{:S(2)}) collective-permute-start(bf16[4,8,4096]{2,1,0:T(8,128)(2,1)S(1)} %slice_bitcast_fusion.5), channel_id=1, source_target_pairs={{0,32},{1,33},{2,34},{3,35},{4,36},{5,37},{6,38},{7,39},{8,40},{9,... | collective-permute-start | bytes 786440 | tf_op jit(solution)/shard_map/ppermute | solution.py:289
  13.4 1.0 slice_bitcast_fusion.2
  14.4 1.3 collective-permute-start
  15.7 3.7 %slice_reduce_fusion = (bf16[4,6,4096]{2,1,0:T(8,128)(2,1)S(1)}, bf16[4,6,4096]{2,1,0:T(8,128)(2,1)S(1)}) fusion(bf16[4,6,8,4096]{3,2,1,0:T(8,128)(2,1)} %param.8), kind=kLoop, calls=%fused_computation | loop fusion | bytes 786432 | tf_op jit(solution)/shard_map/slice | solution.py:317
  19.5 0.8 reshape_squeeze.10
  20.2 5.0 %collective-permute-start.7 = (bf16[3,8,4096]{2,1,0:T(8,128)(2,1)}, bf16[3,8,4096]{2,1,0:T(8,128)(2,1)}, u32[]{:S(2)}, u32[]{:S(2)}) collective-permute-start(bf16[3,8,4096]{2,1,0:T(8,128)(2,1)} %reshape_squeeze.10), channel_id=1, source_target_pairs={{0,1},{1,2},{2,3},{3,4},{4,5},{5,6},{6,7},{7,8},{8,9},{9,10},{10,1... | collective-permute-start | bytes 589832 | tf_op jit(solution)/shard_map/ppermute | solution.py:289
  25.2 0.8 reshape_squeeze.11
  25.9 1.3 collective-permute-start.8
  27.2 0.0 copy-done.2
  27.2 0.1 slice_bitcast_fusion
  27.3 0.0 collective-permute-done.2.rim_z
  27.3 1.3 collective-permute-start.4
  28.6 0.0 collective-permute-done.7.p_zm
  28.6 4.5 %collective-permute-start.3 = (bf16[6,8,4096]{2,1,0:T(8,128)(2,1)S(1)}, bf16[6,8,4096]{2,1,0:T(8,128)(2,1)}, u32[]{:S(2)}, u32[]{:S(2)}) collective-permute-start(bf16[6,8,4096]{2,1,0:T(8,128)(2,1)S(1)} %get-tuple-element.10), channel_id=1, source_target_pairs={{0,64},{1,65},{2,66},{3,67},{4,68},{5,69},{6,70},{7,71},{8,72},{9,... | collective-permute-start | bytes 1179656 | tf_op jit(solution)/shard_map/ppermute | solution.py:289
  33.2 0.8 slice_bitcast_fusion.3
  34.0 1.3 collective-permute-done.8.p_zp
  35.3 1.3 collective-permute-start.6
  36.6 0.0 collective-permute-done.1.rim_y
  36.6 4.6 %collective-permute-start.5 = (bf16[4,8,4096]{2,1,0:T(8,128)(2,1)}, bf16[4,8,4096]{2,1,0:T(8,128)(2,1)S(1)}, u32[]{:S(2)}, u32[]{:S(2)}) collective-permute-start(bf16[4,8,4096]{2,1,0:T(8,128)(2,1)} %get-tuple-element.8), channel_id=1, source_target_pairs={{0,32},{1,33},{2,34},{3,35},{4,36},{5,37},{6,38},{7,39},{8,40},{9,... | collective-permute-start | bytes 786440 | tf_op jit(solution)/shard_map/ppermute | solution.py:289
  41.2 0.0 copy-done.7
  41.2 0.7 reshape.43.agg
  41.9 0.9 copy.21
  42.8 0.7 reshape.44.slot
  43.5 0.3 collective-permute-done.6.p_yp
  43.8 1.6 collective-permute-done.5.p_ym
  45.4 0.0 collective-permute-done.rim_x
  45.4 0.0 collective-permute-done.4.p_xp
  45.4 0.0 collective-permute-done.3.p_xm
  45.4 0.0 copy-done.4
  45.4 0.7 copy-done.5
  46.1 0.1 copy-done.3
  46.2 109.2 %coarse_rows.1 = bf16[32,464,128]{2,1,0:T(8,128)(2,1)} custom-call(s32[192]{0:T(256)} %reshape.43.agg, s32[7,192]{1,0:T(8,128)} %reshape.44.slot, s32[24]{0:T(128)} %owner.1, bf16[24,8,4096]{2,1,0:T(8,128)(2,1)} %bitcast.27, bf16[3,24,8,4096]{3,2,1,0:T(8,128)(2,1)} %bitcast.26, bf16[24,8,4096]{2,1,0:T(8,128)(2,1)} %bitcast.25, ...), custom_call_target="tpu_custom_call" | custom-call | tf_op jit(solution)/shard_map/coarse_rows/pallas_call | solution.py:220
  155.5 57.0 %all_to_all.5.taken = bf16[32,464,128]{2,1,0:T(8,128)(2,1)S(1)} all-to-all(bf16[32,464,128]{2,1,0:T(8,128)(2,1)} %coarse_rows.1), channel_id=1, replica_groups=mesh['gx'=2,'gy'=2,'gz'=32] {'gz'}, dimensions={0} | all-to-all | bytes 7602176 | tf_op jit(solution)/shard_map/all_to_all | solution.py:322
  212.5 1.8 copy-done
  214.3 0.1 reduce-window.4
  214.4 0.5 slice.49
  214.9 0.1 reduce.3
  215.0 0.1 convert_reduce_fusion
  215.1 1.5 fusion
  216.6 0.1 select_reduce_fusion
  216.7 0.0 copy-start.1
  216.7 2.1 copy-done.1
  218.8 4.3 %place_rows.1 = bf16[64,7,4096]{2,1,0:T(8,128)(2,1)S(1)} custom-call(s32[64]{0:T(128)S(1)} %add_minimum_fusion.source, s32[1]{0:T(128)} %bitcast.10.total, bf16[32,464,128]{2,1,0:T(8,128)(2,1)S(1)} %copy-done.1), custom_call_target="tpu_custom_call" | custom-call | tf_op jit(solution)/shard_map/place_rows/pallas_call | solution.py:272
  223.1 4.1 %copy.26 = bf16[1,1,1,64,7,4096]{5,3,4,2,1,0:T(8,128)(2,1)} copy(bf16[1,1,1,64,7,4096]{5,4,3,2,1,0:T(8,128)(2,1)S(1)} %bitcast.24) | data formatting | bytes 7340032 | tf_op jit(solution)/shard_map/reshape | solution.py:332
  (11 shorter events, 0.0 us)
Async XLA Ops:
  0.0 27.2 %copy-start.2 = (bf16[4,6,8,4096]{3,2,1,0:T(8,128)(2,1)S(1)}, bf16[4,6,8,4096]{3,2,1,0:T(8,128)(2,1)}, u32[]{:S(2)}) copy-start(bf16[4,6,8,4096]{3,2,1,0:T(8,128)(2,1)} %param.8) | copy-start | bytes 4718596
  0.0 41.2 %copy-start.7 = (s32[4,6,8]{2,0,1:T(4,128)S(1)}, s32[4,6,8]{2,0,1:T(4,128)}, u32[]{:S(2)}) copy-start(s32[4,6,8]{2,0,1:T(4,128)} %param.9) | copy-start | bytes 2308
  3.5 23.8 %collective-permute-start.2 = (bf16[3,8,4096]{2,1,0:T(8,128)(2,1)}, bf16[3,8,4096]{2,1,0:T(8,128)(2,1)}, u32[]{:S(2)}, u32[]{:S(2)}) collective-permute-start(bf16[3,8,4096]{2,1,0:T(8,128)(2,1)} %reshape_squeeze.9), channel_id=1, source_target_pairs={{0,1},{1,2},{2,3},{3,4},{4,5},{5,6},{6,7},{7,8},{8,9},{9,10},{10,1... | collective-permute-start | bytes 589832 | tf_op jit(solution)/shard_map/ppermute | solution.py:289
  10.2 26.4 %collective-permute-start.1 = (bf16[4,8,4096]{2,1,0:T(8,128)(2,1)S(1)}, bf16[4,8,4096]{2,1,0:T(8,128)(2,1)}, u32[]{:S(2)}, u32[]{:S(2)}) collective-permute-start(bf16[4,8,4096]{2,1,0:T(8,128)(2,1)S(1)} %slice_bitcast_fusion.5), channel_id=1, source_target_pairs={{0,32},{1,33},{2,34},{3,35},{4,36},{5,37},{6,38},{7,39},{8,40},{9,... | collective-permute-start | bytes 786440 | tf_op jit(solution)/shard_map/ppermute | solution.py:289
  14.4 31.0 %collective-permute-start = (bf16[6,8,4096]{2,1,0:T(8,128)(2,1)S(1)}, bf16[6,8,4096]{2,1,0:T(8,128)(2,1)S(1)}, u32[]{:S(2)}, u32[]{:S(2)}) collective-permute-start(bf16[6,8,4096]{2,1,0:T(8,128)(2,1)S(1)} %slice_bitcast_fusion.2), channel_id=1, source_target_pairs={{0,64},{1,65},{2,66},{3,67},{4,68},{5,69},{6,70},{7,71},{8,72},{9,... | collective-permute-start | bytes 1179656 | tf_op jit(solution)/shard_map/ppermute | solution.py:289
  20.2 8.4 %collective-permute-start.7 = (bf16[3,8,4096]{2,1,0:T(8,128)(2,1)}, bf16[3,8,4096]{2,1,0:T(8,128)(2,1)}, u32[]{:S(2)}, u32[]{:S(2)}) collective-permute-start(bf16[3,8,4096]{2,1,0:T(8,128)(2,1)} %reshape_squeeze.10), channel_id=1, source_target_pairs={{0,1},{1,2},{2,3},{3,4},{4,5},{5,6},{6,7},{7,8},{8,9},{9,10},{10,1... | collective-permute-start | bytes 589832 | tf_op jit(solution)/shard_map/ppermute | solution.py:289
  25.9 9.4 %collective-permute-start.8 = (bf16[3,8,4096]{2,1,0:T(8,128)(2,1)}, bf16[3,8,4096]{2,1,0:T(8,128)(2,1)S(1)}, u32[]{:S(2)}, u32[]{:S(2)}) collective-permute-start(bf16[3,8,4096]{2,1,0:T(8,128)(2,1)} %reshape_squeeze.11), channel_id=1, source_target_pairs={{1,0},{2,1},{3,2},{4,3},{5,4},{6,5},{7,6},{8,7},{9,8},{10,9},{11,1... | collective-permute-start | bytes 589832 | tf_op jit(solution)/shard_map/ppermute | solution.py:294
  27.3 18.1 %collective-permute-start.4 = (bf16[6,8,4096]{2,1,0:T(8,128)(2,1)S(1)}, bf16[6,8,4096]{2,1,0:T(8,128)(2,1)}, u32[]{:S(2)}, u32[]{:S(2)}) collective-permute-start(bf16[6,8,4096]{2,1,0:T(8,128)(2,1)S(1)} %get-tuple-element.9), channel_id=1, source_target_pairs={{64,0},{65,1},{66,2},{67,3},{68,4},{69,5},{70,6},{71,7},{72,8},{73... | collective-permute-start | bytes 1179656 | tf_op jit(solution)/shard_map/ppermute | solution.py:294
  28.6 16.8 %collective-permute-start.3 = (bf16[6,8,4096]{2,1,0:T(8,128)(2,1)S(1)}, bf16[6,8,4096]{2,1,0:T(8,128)(2,1)}, u32[]{:S(2)}, u32[]{:S(2)}) collective-permute-start(bf16[6,8,4096]{2,1,0:T(8,128)(2,1)S(1)} %get-tuple-element.10), channel_id=1, source_target_pairs={{0,64},{1,65},{2,66},{3,67},{4,68},{5,69},{6,70},{7,71},{8,72},{9,... | collective-permute-start | bytes 1179656 | tf_op jit(solution)/shard_map/ppermute | solution.py:289
  35.3 1.3 copy-start.6
  35.3 8.5 %collective-permute-start.6 = (bf16[4,8,4096]{2,1,0:T(8,128)(2,1)}, bf16[4,8,4096]{2,1,0:T(8,128)(2,1)S(1)}, u32[]{:S(2)}, u32[]{:S(2)}) collective-permute-start(bf16[4,8,4096]{2,1,0:T(8,128)(2,1)} %get-tuple-element.7), channel_id=1, source_target_pairs={{32,0},{33,1},{34,2},{35,3},{36,4},{37,5},{38,6},{39,7},{40,8},{41... | collective-permute-start | bytes 786440 | tf_op jit(solution)/shard_map/ppermute | solution.py:294
  36.6 8.8 %collective-permute-start.5 = (bf16[4,8,4096]{2,1,0:T(8,128)(2,1)}, bf16[4,8,4096]{2,1,0:T(8,128)(2,1)S(1)}, u32[]{:S(2)}, u32[]{:S(2)}) collective-permute-start(bf16[4,8,4096]{2,1,0:T(8,128)(2,1)} %get-tuple-element.8), channel_id=1, source_target_pairs={{0,32},{1,33},{2,34},{3,35},{4,36},{5,37},{6,38},{7,39},{8,40},{9,... | collective-permute-start | bytes 786440 | tf_op jit(solution)/shard_map/ppermute | solution.py:289
  43.8 1.6 copy-start.4
  45.4 0.7 copy-start.5
  45.4 0.8 copy-start.3
  212.5 1.8 copy-start
  216.7 2.1 copy-start.1

commit v2 on v1

--- a/solution.py
+++ b/solution.py
@@ -49,131 +49,215 @@
     a_diag, a_face, prolong, rim_x, rim_y, rim_z,
     p_xm, p_xp, p_ym, p_yp, p_zm, p_zp,
     send,
-    ra_d, ra_x, ra_y, ra_z, right, left, work_a, work_b, work_c,
+    ra_d, ra_x, ra_y, ra_z, right, left, couple, work_a, work_b, work_c,
     acc_f, acc_b, rows, counts, tally, sems, count_sem,
 ):
-    def store_spread(line, dest, base):
-        spread(line, work_a)
-        dest[pl.ds(pl.multiple_of(base, 32), 256), :] = work_a[...].astype(BF16)
+    def store_spread(line, dest, base, bench):
+        work = work_a.at[bench]
+        spread(line, work)
+        dest[pl.ds(pl.multiple_of(base, 32), 256), :] = work[...].astype(BF16)
 
     right_xp, right_yp, right_zp = LINES, LINES + BY, LINES + BY + BX
     left_xm, left_ym, left_zm = LINES, LINES + BY, LINES + BY + BX
 
-    def store_right(base):
-        right[pl.ds(pl.multiple_of(base * 512, 512), 512), :] = work_b[...].astype(BF16)
-
-    def store_left(base):
+    def store_right(base, work):
+        right[pl.ds(pl.multiple_of(base * 512, 512), 512), :] = work[...].astype(BF16)
+
+    def store_left(base, work):
         low = lane_low((64, 128))
+        zero = jnp.zeros((64, 128), F32)
         for pair in range(4):
-            first = work_c[pair * 128 : pair * 128 + 64, :]
-            second = work_c[pair * 128 + 64 : pair * 128 + 128, :]
-            flipped = jnp.where(low, first, second).T
-            left[pl.ds(pl.multiple_of(base * 512 + pair * 128, 128), 128), :] = flipped.astype(BF16)
+            first = work[pair * 128 : pair * 128 + 64, :]
+            second = work[pair * 128 + 64 : pair * 128 + 128, :]
+            block = jnp.concatenate([jnp.where(low, first, zero), jnp.where(low, zero, second)], axis=0)
+            at = pl.multiple_of(base * 512 + pair * 128, 128)
+            left[pl.ds(at, 128), :] = block.astype(BF16).T
 
     acc_f[...] = jnp.zeros_like(acc_f)
     acc_b[...] = jnp.zeros_like(acc_b)
 
-    @pl.loop(0, LINES)
-    def _(line):
-        spread_twice(prolong[line], work_b, work_c)
-        store_right(line)
-        store_left(line)
-        store_spread(a_diag[line], ra_d, line * 256)
-        store_spread(a_face[0, line], ra_x, (line + BY) * 256)
-        store_spread(a_face[1, line], ra_y, (line + line // BY + 1) * 256)
-        store_spread(a_face[2, line], ra_z, line * 288 + 32)
-
-    @pl.loop(0, BY)
-    def _(line):
-        store_spread(rim_x[line], ra_x, line * 256)
-        spread_twice(p_xm[line], None, work_c)
-        store_left(left_xm + line)
-        spread_twice(p_xp[line], work_b, None)
-        store_right(right_xp + line)
-
-    @pl.loop(0, BX)
-    def _(line):
-        store_spread(rim_y[line], ra_y, line * (BY + 1) * 256)
-        spread_twice(p_ym[line], None, work_c)
-        store_left(left_ym + line)
-        spread_twice(p_yp[line], work_b, None)
-        store_right(right_yp + line)
-
-    @pl.loop(0, LINES // 8)
-    def _(line):
-        spread(rim_z[line], work_a)
+    @pl.loop(0, LINES // 2)
+    def _(half):
+        for k in range(2):
+            line = half * 2 + k
+            natural, by_parity = work_b.at[k], work_c.at[k]
+            spread_twice(prolong[line], natural, by_parity)
+            store_right(line, natural)
+            store_left(line, by_parity)
+            store_spread(a_diag[line], ra_d, line * 256, 0)
+            store_spread(a_face[0, line], ra_x, (line + BY) * 256, 1)
+            store_spread(a_face[1, line], ra_y, (line + line // BY + 1) * 256, 2)
+            store_spread(a_face[2, line], ra_z, line * 288 + 32, 3)
+
+    @pl.loop(0, BY // 2)
+    def _(half):
+        for k in range(2):
+            line = half * 2 + k
+            store_spread(rim_x[line], ra_x, line * 256, k)
+            spread_twice(p_xm[line], None, work_c.at[k])
+            store_left(left_xm + line, work_c.at[k])
+            spread_twice(p_xp[line], work_b.at[k], None)
+            store_right(right_xp + line, work_b.at[k])
+
+    @pl.loop(0, BX // 2)
+    def _(half):
+        for k in range(2):
+            line = half * 2 + k
+            store_spread(rim_y[line], ra_y, line * (BY + 1) * 256, k)
+            spread_twice(p_ym[line], None, work_c.at[k])
+            store_left(left_ym + line, work_c.at[k])
+            spread_twice(p_yp[line], work_b.at[k], None)
+            store_right(right_yp + line, work_b.at[k])
+
+    for line in range(LINES // 8):
+        work = work_a.at[line]
+        spread(rim_z[line], work)
         for k in range(8):
             at = (line * 8 + k) * 288
-            ra_z[pl.ds(pl.multiple_of(at, 32), 32), :] = work_a[k * 32 : k * 32 + 32, :].astype(BF16)
-        spread_twice(p_zm[line], None, work_c)
-        store_left(left_zm + line)
-        spread_twice(p_zp[line], work_b, None)
-        store_right(right_zp + line)
-
-    def products(cell, blocks):
+            ra_z[at : at + 32, :] = work[k * 32 : k * 32 + 32, :].astype(BF16)
+        spread_twice(p_zm[line], None, work_c.at[line % 2])
+        store_left(left_zm + line, work_c.at[line % 2])
+        spread_twice(p_zp[line], work_b.at[line % 2], None)
+        store_right(right_zp + line, work_b.at[line % 2])
+
+    def couples(cell, blocks):
         low = lane_low((64, 128))
-        block = right[pl.ds(pl.multiple_of(cell * 64, 64), 64), :]
-        zero = jnp.zeros_like(block)
-        weight = jnp.concatenate([jnp.where(low, block, zero), jnp.where(low, zero, block)], axis=0)
-        stack = [ref[pl.ds(pl.multiple_of(at, 32), 32), :] for ref, at, _, _, _ in blocks]
+        zero = jnp.zeros((64, 128), BF16)
+        wide = jnp.zeros((128, 128), BF16)
+        columns = []
+        for k in range(2):
+            block = right[pl.ds(pl.multiple_of((cell + k) * 64, 64), 64), :]
+            corner = jnp.concatenate([jnp.where(low, block, zero), jnp.where(low, zero, block)], axis=0)
+            columns.append(jnp.concatenate([corner, wide] if k == 0 else [wide, corner], axis=0))
+        weight = jnp.concatenate(columns, axis=1)
+        stack = [
+            jnp.concatenate([ref[pl.ds(pl.multiple_of(at, 32), 32), :] for at in ats], axis=1)
+            for _, ref, ats, _ in blocks
+        ]
         stack = jnp.concatenate(stack, axis=0) if len(stack) > 1 else stack[0]
         both = jnp.dot(stack, weight, preferred_element_type=F32)
-        turned = pltpu.roll(both, 64, axis=1)
-        for number, (_, _, flip, key_f, key_b) in enumerate(blocks):
-            part = slice(number * 32, number * 32 + 32)
-            couple = jnp.concatenate([both[part], turned[part]], axis=0).astype(BF16)
-            lhs = left[pl.ds(pl.multiple_of(flip * 64, 64), 64), :]
-            term = jnp.dot(lhs, couple, preferred_element_type=F32)
-            if key_f is not None:
-                acc_f[key_f] += term
-            if key_b is not None:
-                acc_b[key_b] += term
+        for number, (f, _, _, cells) in enumerate(blocks):
+            for k in range(2):
+                part = both[number * 32 : number * 32 + 32, k * 128 : k * 128 + 128]
+                turned = pltpu.roll(part, 64, axis=1)
+                side = f % 2 * 64
+                for p in range(2):
+                    value = (part if p == f % 2 else turned)[:, side : side + 64]
+                    at = pl.multiple_of(cells[k] * 64 + p * 32, 32)
+                    couple[pl.ds(at, 32), f * 64 : f * 64 + 64] = value.astype(BF16)
+
+    def add(ref, at, low_side, value):
+        low = lane_low((64, 128))
+        zero = jnp.zeros((64, 128), F32)
+        ref[at] += jnp.where(low, value, zero) if low_side else jnp.where(low, zero, value)
+
+    def terms(cell, keys, tiles):
+        at = pl.multiple_of(cell * 64, 128)
+        first, last = tiles
+        out = jnp.dot(
+            left[pl.ds(at, 128), :],
+            couple[pl.ds(at, 128), first * 128 : last * 128],
+            preferred_element_type=F32,
+        )
+        for k in range(2):
+            for f, (key_f, key_b) in keys[k].items():
+                tile = f // 2 - first
+                term = out[k * 64 : k * 64 + 64, tile * 128 : tile * 128 + 128]
+                if key_f is not None:
+                    add(acc_f, key_f, f % 2 == 0, term)
+                if key_b is not None:
+                    add(acc_b, key_b, f % 2 == 0, term)
 
     def key(e, number):
         return agg[e] * SLOTS + slot[number, e]
+
+    cells_xm, cells_ym, cells_zm = left_xm * 8, left_ym * 8, left_zm * 8
 
     @pl.loop(0, LINES)
     def _(line):
         x, y = line // BY, line % BY
-        flip_x = jnp.where(x > 0, (line - BY) * 8, (left_xm + y) * 8)
-        flip_y = jnp.where(y > 0, (line - 1) * 8, (left_ym + x) * 8)
-        for z in range(BZ):
+        into_x = jnp.where(x > 0, (line - BY) * 8, cells_xm + y * 8)
+        into_y = jnp.where(y > 0, (line - 1) * 8, cells_ym + x * 8)
+        for z in range(0, BZ, 2):
             n = line * BZ + z
-            back_x = jnp.where(x > 0, n - BY * BZ, 0)
-            back_y = jnp.where(y > 0, n - BZ, 0)
-            key_x = jnp.where(x > 0, key(back_x, 2), KEYS)
-            key_y = jnp.where(y > 0, key(back_y, 4), KEYS)
-            products(
+            couples(
                 n,
                 [
-                    (ra_d, n * 32, n, key(n, 0), None),
-                    (ra_x, n * 32, flip_x + z, key_x, key(n, 1)),
-                    (ra_y, (line + x) * 256 + z * 32, flip_y + z, key_y, key(n, 3)),
+                    (0, ra_d, [(n + k) * 32 for k in range(2)], [n, n + 1]),
+                    (1, ra_x, [(n + k) * 32 for k in range(2)], [into_x + z, into_x + z + 1]),
                     (
+                        2,
+                        ra_y,
+                        [(line + x) * 256 + (z + k) * 32 for k in range(2)],
+                        [into_y + z, into_y + z + 1],
+                    ),
+                    (
+                        3,
                         ra_z,
-                        line * 288 + z * 32,
-                        left_zm * 8 + line if z == 0 else n - 1,
-                        None if z == 0 else key(n - 1, 6),
-                        key(n, 5),
+                        [line * 288 + (z + k) * 32 for k in range(2)],
+                        [cells_zm + line if z == 0 else n - 1, n],
                     ),
                 ],
             )
-        e = line * BZ + BZ - 1
-        products(right_zp * 8 + line, [(ra_z, line * 288 + BZ * 32, e, key(e, 6), None)])
 
     @pl.loop(0, BY)
     def _(y):
-        for z in range(BZ):
+        for z in range(0, BZ, 2):
             e = ((BX - 1) * BY + y) * BZ + z
             at = (BX * BY + y) * 256 + z * 32
-            products((right_xp + y) * 8 + z, [(ra_x, at, e, key(e, 2), None)])
+            couples((right_xp + y) * 8 + z, [(1, ra_x, [at, at + 32], [e, e + 1])])
 
     @pl.loop(0, BX)
     def _(x):
-        for z in range(BZ):
+        for z in range(0, BZ, 2):
             e = (x * BY + BY - 1) * BZ + z
             at = (x * (BY + 1) + BY) * 256 + z * 32
-            products((right_yp + x) * 8 + z, [(ra_y, at, e, key(e, 4), None)])
+            couples((right_yp + x) * 8 + z, [(2, ra_y, [at, at + 32], [e, e + 1])])
+
+    @pl.loop(0, LINES // 2)
+    def _(half):
+        line = half * 2
+        e = line * BZ + BZ - 1
+        at = line * 288 + BZ * 32
+        couples(right_zp * 8 + line, [(3, ra_z, [at, at + 288], [e, e + BZ])])
+
+    @pl.loop(0, LINES)
+    def _(line):
+        x, y = line // BY, line % BY
+        for z in range(0, BZ, 2):
+            keys = []
+            for k in range(2):
+                e = line * BZ + z + k
+                next_x = jnp.where(x < BX - 1, e + BY * BZ, 0)
+                next_y = jnp.where(y < BY - 1, e + BZ, 0)
+                keys.append(
+                    {
+                        0: (key(e, 0), None),
+                        1: (key(e, 2), jnp.where(x < BX - 1, key(next_x, 1), KEYS)),
+                        2: (key(e, 4), jnp.where(y < BY - 1, key(next_y, 3), KEYS)),
+                        3: (key(e, 6), key(e + 1, 5) if z + k < BZ - 1 else None),
+                    }
+                )
+            terms(line * BZ + z, keys, (0, 2))
+
+    @pl.loop(0, BY)
+    def _(y):
+        for z in range(0, BZ, 2):
+            n = y * BZ + z
+            terms(cells_xm + n, [{1: (None, key(n + k, 1))} for k in range(2)], (0, 1))
+
+    @pl.loop(0, BX)
+    def _(x):
+        for z in range(0, BZ, 2):
+            n = x * BY * BZ + z
+            keys = [{2: (None, key(n + k, 3))} for k in range(2)]
+            terms(cells_ym + x * BZ + z, keys, (1, 2))
+
+    @pl.loop(0, LINES // 2)
+    def _(half):
+        n = half * 2 * BZ
+        keys = [{3: (None, key(n + k * BZ, 5))} for k in range(2)]
+        terms(cells_zm + half * 2, keys, (1, 2))
 
     depth = send.shape[0]
 
@@ -183,14 +267,23 @@
 
     @pl.loop(0, AGG_DEV)
     def _(r):
-        low = lane_low((32, 128))
-        for s in range(SLOTS):
-            k = r * SLOTS + s
-            work_b[0:64, 0:64] = acc_f[k, :, 0:64] + acc_b[k].T[0:64, :]
-            even = work_b[pl.ds(0, 32, stride=2), :]
-            odd = work_b[pl.ds(1, 32, stride=2), :]
-            row = jnp.where(low, even, pltpu.roll(odd, 64, axis=1)).astype(BF16)
-            rows[pl.ds(pl.multiple_of(r * ROW + s * 32, 32), 32), :] = row
+        low, low_half = lane_low((64, 128)), lane_low((32, 128))
+
+        def folded(ref, s):
+            value = ref[r * SLOTS + s]
+            return value + pltpu.roll(value, 64, axis=1)
+
+        for s in range(0, SLOTS, 2):
+            first = folded(acc_b, s)
+            pair = jnp.where(low, first, folded(acc_b, s + 1)) if s + 1 < SLOTS else first
+            flipped = pair.T
+            for k in range(min(2, SLOTS - s)):
+                work = work_b.at[(s + k) // 4, pl.ds((s + k) % 4 * 64, 64)]
+                work[:, 0:64] = folded(acc_f, s + k)[:, 0:64] + flipped[k * 64 : k * 64 + 64]
+                even = work[pl.ds(0, 32, stride=2), :]
+                odd = work[pl.ds(1, 32, stride=2), :]
+                row = jnp.where(low_half, even, pltpu.roll(odd, 64, axis=1)).astype(BF16)
+                rows[pl.ds(pl.multiple_of(r * ROW + (s + k) * 32, 32), 32), :] = row
         c = owner[r]
         place = tally[c]
         tally[c] = place + 1
@@ -228,10 +321,11 @@
             pltpu.VMEM((BX * (BY + 1) * 256, 128), BF16),
             pltpu.VMEM((LINES * 288, 128), BF16),
             pltpu.VMEM((lines_right * 512, 128), BF16),
-            pltpu.VMEM((lines_right * 512, 64), BF16),
-            pltpu.VMEM((256, 128), F32),
-            pltpu.VMEM((512, 128), F32),
-            pltpu.VMEM((512, 128), F32),
+            pltpu.VMEM((lines_right * 512, 128), BF16),
+            pltpu.VMEM((lines_right * 512, 256), BF16),
+            pltpu.VMEM((4, 256, 128), F32),
+            pltpu.VMEM((2, 512, 128), F32),
+            pltpu.VMEM((2, 512, 128), F32),
             pltpu.VMEM((KEYS + 1, 64, 128), F32),
             pltpu.VMEM((KEYS + 1, 64, 128), F32),
             pltpu.VMEM((AGG_DEV * ROW, 128), BF16),

time: 230 us -> 190 us (0.83); the launches traced: 227 us -> 190 us
  Pallas kernels: 114 us -> 76.1 us
    pallas_call x1, Pallas kernels: 109 us -> 70.9 us  [coarse_rows(): pl.pallas_call(compute_kernel, out_shape=jax.ShapeDtypeStruct((depth, PAC...]
where the time goes in v2:
time: 190 us
  Pallas kernels  76.1 us (40%)
  blocking collectives  57 us (30%)
  starting transfers between devices  28.2 us (15%)
  local copies, waits for them, and re-layouts  23.2 us (12%)
  waiting for transfers between devices  3.24 us (2%)
    pallas_call x1, Pallas kernels, coarse_rows(): pl.pallas_call(compute_kernel, out_shape=jax.ShapeDtypeStruct((depth, PAC...  70.9 us
    all_to_all x1, blocking collectives, shards(): taken = lax.all_to_all(send, 'gz', 0, 0, tiled=True)  57 us
    ppermute x6, starting transfers between devices, to_next(): return lax.ppermute(block, axis, [(i, i + 1) for i in range(count - 1)])  24.3 us
    unnamed x18, local copies, waits for them, and re-layouts  5.61 us
    pallas_call x1, Pallas kernels, place_rows(): pl.pallas_call(place_kernel, out_shape=jax.ShapeDtypeStruct((count, SLOTS...  5.2 us
    reshape x1, local copies, waits for them, and re-layouts, shards(): return coarse.reshape(1, 1, 1, holding, SLOTS, block)  4.12 us
    ppermute x3, starting transfers between devices, to_previous(): return lax.ppermute(block, axis, [(i + 1, i) for i in range(count - 1)])  3.85 us
  transfers between devices with their start and end apart: 9, of which 3 were waited for; matrix products, arithmetic and copies ran while one was open for 5% of the time, Pallas kernels for 0%

profile of v2, /device:TPU:0, one launch (start us, length us, event | category | flops | bytes accessed | tf_op | source)
XLA Modules:
  0.0 189.7 jit_solution(7024508813173993950)
XLA Ops:
  0.0 2.7 %slice_reduce_fusion.2 = bf16[4,6,4096]{2,1,0:T(8,128)(2,1)S(1)} fusion(bf16[3,4,6,8,4096]{4,3,2,1,0:T(8,128)(2,1)} %param.7), kind=kLoop, calls=%fused_computation.4 | loop fusion | bytes 393216 | tf_op jit(solution)/shard_map/slice | solution.py:405
  2.8 0.7 reshape_squeeze.9
  3.5 5.7 %collective-permute-start.2 = (bf16[3,8,4096]{2,1,0:T(8,128)(2,1)}, bf16[3,8,4096]{2,1,0:T(8,128)(2,1)}, u32[]{:S(2)}, u32[]{:S(2)}) collective-permute-start(bf16[3,8,4096]{2,1,0:T(8,128)(2,1)} %reshape_squeeze.9), channel_id=1, source_target_pairs={{0,1},{1,2},{2,3},{3,4},{4,5},{5,6},{6,7},{7,8},{8,9},{9,10},{10,1... | collective-permute-start | bytes 589832 | tf_op jit(solution)/shard_map/ppermute | solution.py:383
  9.2 1.0 slice_bitcast_fusion.5
  10.2 3.2 %collective-permute-start.1 = (bf16[4,8,4096]{2,1,0:T(8,128)(2,1)S(1)}, bf16[4,8,4096]{2,1,0:T(8,128)(2,1)}, u32[]{:S(2)}, u32[]{:S(2)}) collective-permute-start(bf16[4,8,4096]{2,1,0:T(8,128)(2,1)S(1)} %slice_bitcast_fusion.5), channel_id=1, source_target_pairs={{0,32},{1,33},{2,34},{3,35},{4,36},{5,37},{6,38},{7,39},{8,40},{9,... | collective-permute-start | bytes 786440 | tf_op jit(solution)/shard_map/ppermute | solution.py:383
  13.4 1.0 slice_bitcast_fusion.2
  14.4 1.3 collective-permute-start
  15.7 3.7 %slice_reduce_fusion = (bf16[4,6,4096]{2,1,0:T(8,128)(2,1)S(1)}, bf16[4,6,4096]{2,1,0:T(8,128)(2,1)S(1)}) fusion(bf16[4,6,8,4096]{3,2,1,0:T(8,128)(2,1)} %param.8), kind=kLoop, calls=%fused_computation | loop fusion | bytes 786432 | tf_op jit(solution)/shard_map/slice | solution.py:411
  19.5 0.8 reshape_squeeze.10
  20.2 5.0 %collective-permute-start.7 = (bf16[3,8,4096]{2,1,0:T(8,128)(2,1)}, bf16[3,8,4096]{2,1,0:T(8,128)(2,1)}, u32[]{:S(2)}, u32[]{:S(2)}) collective-permute-start(bf16[3,8,4096]{2,1,0:T(8,128)(2,1)} %reshape_squeeze.10), channel_id=1, source_target_pairs={{0,1},{1,2},{2,3},{3,4},{4,5},{5,6},{6,7},{7,8},{8,9},{9,10},{10,1... | collective-permute-start | bytes 589832 | tf_op jit(solution)/shard_map/ppermute | solution.py:383
  25.2 0.8 reshape_squeeze.11
  25.9 1.3 collective-permute-start.8
  27.2 0.0 copy-done.2
  27.2 0.1 slice_bitcast_fusion
  27.3 0.0 collective-permute-done.2.rim_z
  27.3 1.3 collective-permute-start.4
  28.6 0.0 collective-permute-done.7.p_zm
  28.6 4.5 %collective-permute-start.3 = (bf16[6,8,4096]{2,1,0:T(8,128)(2,1)S(1)}, bf16[6,8,4096]{2,1,0:T(8,128)(2,1)}, u32[]{:S(2)}, u32[]{:S(2)}) collective-permute-start(bf16[6,8,4096]{2,1,0:T(8,128)(2,1)S(1)} %get-tuple-element.10), channel_id=1, source_target_pairs={{0,64},{1,65},{2,66},{3,67},{4,68},{5,69},{6,70},{7,71},{8,72},{9,... | collective-permute-start | bytes 1179656 | tf_op jit(solution)/shard_map/ppermute | solution.py:383
  33.2 0.8 slice_bitcast_fusion.3
  34.0 1.3 collective-permute-done.8.p_zp
  35.3 1.3 collective-permute-start.6
  36.6 0.0 collective-permute-done.1.rim_y
  36.6 0.0 copy-done.6
  36.6 4.6 %collective-permute-start.5 = (bf16[4,8,4096]{2,1,0:T(8,128)(2,1)}, bf16[4,8,4096]{2,1,0:T(8,128)(2,1)S(1)}, u32[]{:S(2)}, u32[]{:S(2)}) collective-permute-start(bf16[4,8,4096]{2,1,0:T(8,128)(2,1)} %get-tuple-element.8), channel_id=1, source_target_pairs={{0,32},{1,33},{2,34},{3,35},{4,36},{5,37},{6,38},{7,39},{8,40},{9,... | collective-permute-start | bytes 786440 | tf_op jit(solution)/shard_map/ppermute | solution.py:383
  41.2 0.0 copy-done.7
  41.2 0.7 reshape.43.agg
  41.9 0.9 copy.21
  42.8 0.7 reshape.44.slot
  43.5 0.3 collective-permute-done.6.p_yp
  43.8 1.6 collective-permute-done.5.p_ym
  45.4 0.0 collective-permute-done.rim_x
  45.4 0.0 collective-permute-done.4.p_xp
  45.4 0.0 collective-permute-done.3.p_xm
  45.4 0.0 copy-done.4
  45.4 0.7 copy-done.5
  46.1 0.1 copy-done.3
  46.2 70.9 %coarse_rows.1 = bf16[32,464,128]{2,1,0:T(8,128)(2,1)} custom-call(s32[192]{0:T(256)} %reshape.43.agg, s32[7,192]{1,0:T(8,128)} %reshape.44.slot, s32[24]{0:T(128)} %owner.1, bf16[24,8,4096]{2,1,0:T(8,128)(2,1)} %bitcast.27, bf16[3,24,8,4096]{3,2,1,0:T(8,128)(2,1)} %bitcast.26, bf16[24,8,4096]{2,1,0:T(8,128)(2,1)} %bitcast.25, ...), custom_call_target="tpu_custom_call" | custom-call | tf_op jit(solution)/shard_map/coarse_rows/pallas_call | solution.py:313
  117.1 57.0 %all_to_all.5.taken = bf16[32,464,128]{2,1,0:T(8,128)(2,1)S(1)} all-to-all(bf16[32,464,128]{2,1,0:T(8,128)(2,1)} %coarse_rows.1), channel_id=1, replica_groups=mesh['gx'=2,'gy'=2,'gz'=32] {'gz'}, dimensions={0} | all-to-all | bytes 7602176 | tf_op jit(solution)/shard_map/all_to_all | solution.py:416
  174.1 1.8 copy-done
  175.9 0.1 reduce-window.4
  176.0 0.5 slice.49
  176.5 0.1 reduce.3
  176.6 0.1 convert_reduce_fusion
  176.7 1.5 fusion
  178.2 0.1 select_reduce_fusion
  178.3 2.1 %copy-done.1 = bf16[32,464,128]{2,1,0:T(8,128)(2,1)S(1)} copy-done((bf16[32,464,128]{2,1,0:T(8,128)(2,1)S(1)}, bf16[32,464,128]{2,1,0:T(8,128)(2,1)}, u32[]{:S(2)}) %copy-start.1) | copy-done | bytes 3801112
  180.4 5.2 %place_rows.1 = bf16[64,7,4096]{2,1,0:T(8,128)(2,1)S(1)} custom-call(s32[64]{0:T(128)S(1)} %add_minimum_fusion.source, s32[1]{0:T(128)} %bitcast.10.total, bf16[32,464,128]{2,1,0:T(8,128)(2,1)S(1)} %copy-done.1), custom_call_target="tpu_custom_call" | custom-call | tf_op jit(solution)/shard_map/place_rows/pallas_call | solution.py:366
  185.6 4.1 %copy.26 = bf16[1,1,1,64,7,4096]{5,3,4,2,1,0:T(8,128)(2,1)} copy(bf16[1,1,1,64,7,4096]{5,4,3,2,1,0:T(8,128)(2,1)S(1)} %bitcast.24) | data formatting | bytes 7340032 | tf_op jit(solution)/shard_map/reshape | solution.py:426
  (11 shorter events, 0.0 us)
Async XLA Ops:
  0.0 27.2 %copy-start.2 = (bf16[4,6,8,4096]{3,2,1,0:T(8,128)(2,1)S(1)}, bf16[4,6,8,4096]{3,2,1,0:T(8,128)(2,1)}, u32[]{:S(2)}) copy-start(bf16[4,6,8,4096]{3,2,1,0:T(8,128)(2,1)} %param.8) | copy-start | bytes 4718596
  0.0 41.2 %copy-start.7 = (s32[4,6,8]{2,0,1:T(4,128)S(1)}, s32[4,6,8]{2,0,1:T(4,128)}, u32[]{:S(2)}) copy-start(s32[4,6,8]{2,0,1:T(4,128)} %param.9) | copy-start | bytes 2308
  3.5 23.8 %collective-permute-start.2 = (bf16[3,8,4096]{2,1,0:T(8,128)(2,1)}, bf16[3,8,4096]{2,1,0:T(8,128)(2,1)}, u32[]{:S(2)}, u32[]{:S(2)}) collective-permute-start(bf16[3,8,4096]{2,1,0:T(8,128)(2,1)} %reshape_squeeze.9), channel_id=1, source_target_pairs={{0,1},{1,2},{2,3},{3,4},{4,5},{5,6},{6,7},{7,8},{8,9},{9,10},{10,1... | collective-permute-start | bytes 589832 | tf_op jit(solution)/shard_map/ppermute | solution.py:383
  10.2 26.4 %collective-permute-start.1 = (bf16[4,8,4096]{2,1,0:T(8,128)(2,1)S(1)}, bf16[4,8,4096]{2,1,0:T(8,128)(2,1)}, u32[]{:S(2)}, u32[]{:S(2)}) collective-permute-start(bf16[4,8,4096]{2,1,0:T(8,128)(2,1)S(1)} %slice_bitcast_fusion.5), channel_id=1, source_target_pairs={{0,32},{1,33},{2,34},{3,35},{4,36},{5,37},{6,38},{7,39},{8,40},{9,... | collective-permute-start | bytes 786440 | tf_op jit(solution)/shard_map/ppermute | solution.py:383
  14.4 31.0 %collective-permute-start = (bf16[6,8,4096]{2,1,0:T(8,128)(2,1)S(1)}, bf16[6,8,4096]{2,1,0:T(8,128)(2,1)S(1)}, u32[]{:S(2)}, u32[]{:S(2)}) collective-permute-start(bf16[6,8,4096]{2,1,0:T(8,128)(2,1)S(1)} %slice_bitcast_fusion.2), channel_id=1, source_target_pairs={{0,64},{1,65},{2,66},{3,67},{4,68},{5,69},{6,70},{7,71},{8,72},{9,... | collective-permute-start | bytes 1179656 | tf_op jit(solution)/shard_map/ppermute | solution.py:383
  20.2 8.4 %collective-permute-start.7 = (bf16[3,8,4096]{2,1,0:T(8,128)(2,1)}, bf16[3,8,4096]{2,1,0:T(8,128)(2,1)}, u32[]{:S(2)}, u32[]{:S(2)}) collective-permute-start(bf16[3,8,4096]{2,1,0:T(8,128)(2,1)} %reshape_squeeze.10), channel_id=1, source_target_pairs={{0,1},{1,2},{2,3},{3,4},{4,5},{5,6},{6,7},{7,8},{8,9},{9,10},{10,1... | collective-permute-start | bytes 589832 | tf_op jit(solution)/shard_map/ppermute | solution.py:383
  25.9 9.4 %collective-permute-start.8 = (bf16[3,8,4096]{2,1,0:T(8,128)(2,1)}, bf16[3,8,4096]{2,1,0:T(8,128)(2,1)S(1)}, u32[]{:S(2)}, u32[]{:S(2)}) collective-permute-start(bf16[3,8,4096]{2,1,0:T(8,128)(2,1)} %reshape_squeeze.11), channel_id=1, source_target_pairs={{1,0},{2,1},{3,2},{4,3},{5,4},{6,5},{7,6},{8,7},{9,8},{10,9},{11,1... | collective-permute-start | bytes 589832 | tf_op jit(solution)/shard_map/ppermute | solution.py:388
  27.3 18.1 %collective-permute-start.4 = (bf16[6,8,4096]{2,1,0:T(8,128)(2,1)S(1)}, bf16[6,8,4096]{2,1,0:T(8,128)(2,1)}, u32[]{:S(2)}, u32[]{:S(2)}) collective-permute-start(bf16[6,8,4096]{2,1,0:T(8,128)(2,1)S(1)} %get-tuple-element.9), channel_id=1, source_target_pairs={{64,0},{65,1},{66,2},{67,3},{68,4},{69,5},{70,6},{71,7},{72,8},{73... | collective-permute-start | bytes 1179656 | tf_op jit(solution)/shard_map/ppermute | solution.py:388
  28.6 16.8 %collective-permute-start.3 = (bf16[6,8,4096]{2,1,0:T(8,128)(2,1)S(1)}, bf16[6,8,4096]{2,1,0:T(8,128)(2,1)}, u32[]{:S(2)}, u32[]{:S(2)}) collective-permute-start(bf16[6,8,4096]{2,1,0:T(8,128)(2,1)S(1)} %get-tuple-element.10), channel_id=1, source_target_pairs={{0,64},{1,65},{2,66},{3,67},{4,68},{5,69},{6,70},{7,71},{8,72},{9,... | collective-permute-start | bytes 1179656 | tf_op jit(solution)/shard_map/ppermute | solution.py:383
  35.3 1.3 copy-start.6
  35.3 8.5 %collective-permute-start.6 = (bf16[4,8,4096]{2,1,0:T(8,128)(2,1)}, bf16[4,8,4096]{2,1,0:T(8,128)(2,1)S(1)}, u32[]{:S(2)}, u32[]{:S(2)}) collective-permute-start(bf16[4,8,4096]{2,1,0:T(8,128)(2,1)} %get-tuple-element.7), channel_id=1, source_target_pairs={{32,0},{33,1},{34,2},{35,3},{36,4},{37,5},{38,6},{39,7},{40,8},{41... | collective-permute-start | bytes 786440 | tf_op jit(solution)/shard_map/ppermute | solution.py:388
  36.6 8.8 %collective-permute-start.5 = (bf16[4,8,4096]{2,1,0:T(8,128)(2,1)}, bf16[4,8,4096]{2,1,0:T(8,128)(2,1)S(1)}, u32[]{:S(2)}, u32[]{:S(2)}) collective-permute-start(bf16[4,8,4096]{2,1,0:T(8,128)(2,1)} %get-tuple-element.8), channel_id=1, source_target_pairs={{0,32},{1,33},{2,34},{3,35},{4,36},{5,37},{6,38},{7,39},{8,40},{9,... | collective-permute-start | bytes 786440 | tf_op jit(solution)/shard_map/ppermute | solution.py:383
  43.8 1.6 copy-start.4
  45.4 0.7 copy-start.5
  45.4 0.8 copy-start.3
  174.1 1.8 copy-start
  178.3 2.1 %copy-start.1 = (bf16[32,464,128]{2,1,0:T(8,128)(2,1)S(1)}, bf16[32,464,128]{2,1,0:T(8,128)(2,1)}, u32[]{:S(2)}) copy-start(bf16[32,464,128]{2,1,0:T(8,128)(2,1)} %copy-done) | copy-start | bytes 11403268

commit v3 on v2

--- a/solution.py
+++ b/solution.py
@@ -14,6 +14,7 @@
 ROW = SLOTS * NODES * NODES // 128
 PACK = PLACES * ROW + 16
 KEYS = AGG_DEV * SLOTS
+STEP, STEP_TWICE = 36, 68
 F32 = jnp.float32
 BF16 = jnp.bfloat16
 
@@ -25,7 +26,7 @@
 def spread(line, scratch):
     values = line.astype(F32)
     for tile in range(32):
-        scratch[pl.ds(tile, 8, stride=32), :] = values[:, tile * 128 : tile * 128 + 128]
+        scratch[pl.ds(tile, 8, stride=STEP), :] = values[:, tile * 128 : tile * 128 + 128]
 
 
 def spread_twice(line, natural, by_parity):
@@ -37,15 +38,15 @@
         even = jnp.where(low, here, swapped)
         odd = jnp.where(low, swapped, here)
         if natural is not None:
-            natural[pl.ds(2 * tile, 8, stride=64), :] = even
-            natural[pl.ds(2 * tile + 1, 8, stride=64), :] = odd
+            natural[pl.ds(2 * tile, 8, stride=STEP_TWICE), :] = even
+            natural[pl.ds(2 * tile + 1, 8, stride=STEP_TWICE), :] = odd
         if by_parity is not None:
-            by_parity[pl.ds(tile, 8, stride=64), :] = even
-            by_parity[pl.ds(32 + tile, 8, stride=64), :] = odd
+            by_parity[pl.ds(tile, 8, stride=STEP_TWICE), :] = even
+            by_parity[pl.ds(32 + tile, 8, stride=STEP_TWICE), :] = odd
 
 
 def compute_kernel(
-    agg, slot, owner,
+    keys, onward, owner,
     a_diag, a_face, prolong, rim_x, rim_y, rim_z,
     p_xm, p_xp, p_ym, p_yp, p_zm, p_zp,
     send,
@@ -55,20 +56,23 @@
     def store_spread(line, dest, base, bench):
         work = work_a.at[bench]
         spread(line, work)
-        dest[pl.ds(pl.multiple_of(base, 32), 256), :] = work[...].astype(BF16)
+        for z in range(8):
+            at = pl.multiple_of(base + z * 32, 32)
+            dest[pl.ds(at, 32), :] = work[z * STEP : z * STEP + 32, :].astype(BF16)
 
     right_xp, right_yp, right_zp = LINES, LINES + BY, LINES + BY + BX
     left_xm, left_ym, left_zm = LINES, LINES + BY, LINES + BY + BX
 
     def store_right(base, work):
-        right[pl.ds(pl.multiple_of(base * 512, 512), 512), :] = work[...].astype(BF16)
+        for z in range(8):
+            at = pl.multiple_of(base * 512 + z * 64, 64)
+            right[pl.ds(at, 64), :] = work[z * STEP_TWICE : z * STEP_TWICE + 64, :].astype(BF16)
 
     def store_left(base, work):
         low = lane_low((64, 128))
         zero = jnp.zeros((64, 128), F32)
         for pair in range(4):
-            first = work[pair * 128 : pair * 128 + 64, :]
-            second = work[pair * 128 + 64 : pair * 128 + 128, :]
+            first, second = (work[z * STEP_TWICE : z * STEP_TWICE + 64, :] for z in (2 * pair, 2 * pair + 1))
             block = jnp.concatenate([jnp.where(low, first, zero), jnp.where(low, zero, second)], axis=0)
             at = pl.multiple_of(base * 512 + pair * 128, 128)
             left[pl.ds(at, 128), :] = block.astype(BF16).T
@@ -114,7 +118,7 @@
         spread(rim_z[line], work)
         for k in range(8):
             at = (line * 8 + k) * 288
-            ra_z[at : at + 32, :] = work[k * 32 : k * 32 + 32, :].astype(BF16)
+            ra_z[at : at + 32, :] = work[k * STEP : k * STEP + 32, :].astype(BF16)
         spread_twice(p_zm[line], None, work_c.at[line % 2])
         store_left(left_zm + line, work_c.at[line % 2])
         spread_twice(p_zp[line], work_b.at[line % 2], None)
@@ -151,7 +155,7 @@
         zero = jnp.zeros((64, 128), F32)
         ref[at] += jnp.where(low, value, zero) if low_side else jnp.where(low, zero, value)
 
-    def terms(cell, keys, tiles):
+    def terms(cell, places, tiles):
         at = pl.multiple_of(cell * 64, 128)
         first, last = tiles
         out = jnp.dot(
@@ -160,16 +164,13 @@
             preferred_element_type=F32,
         )
         for k in range(2):
-            for f, (key_f, key_b) in keys[k].items():
+            for f, (key_f, key_b) in places[k].items():
                 tile = f // 2 - first
                 term = out[k * 64 : k * 64 + 64, tile * 128 : tile * 128 + 128]
                 if key_f is not None:
                     add(acc_f, key_f, f % 2 == 0, term)
                 if key_b is not None:
                     add(acc_b, key_b, f % 2 == 0, term)
-
-    def key(e, number):
-        return agg[e] * SLOTS + slot[number, e]
 
     cells_xm, cells_ym, cells_zm = left_xm * 8, left_ym * 8, left_zm * 8
 
@@ -223,41 +224,38 @@
 
     @pl.loop(0, LINES)
     def _(line):
-        x, y = line // BY, line % BY
-        for z in range(0, BZ, 2):
-            keys = []
+        for z in range(0, BZ, 2):
+            places = []
             for k in range(2):
                 e = line * BZ + z + k
-                next_x = jnp.where(x < BX - 1, e + BY * BZ, 0)
-                next_y = jnp.where(y < BY - 1, e + BZ, 0)
-                keys.append(
+                places.append(
                     {
-                        0: (key(e, 0), None),
-                        1: (key(e, 2), jnp.where(x < BX - 1, key(next_x, 1), KEYS)),
-                        2: (key(e, 4), jnp.where(y < BY - 1, key(next_y, 3), KEYS)),
-                        3: (key(e, 6), key(e + 1, 5) if z + k < BZ - 1 else None),
+                        0: (keys[0, e], None),
+                        1: (keys[2, e], onward[0, e]),
+                        2: (keys[4, e], onward[1, e]),
+                        3: (keys[6, e], onward[2, e] if z + k < BZ - 1 else None),
                     }
                 )
-            terms(line * BZ + z, keys, (0, 2))
+            terms(line * BZ + z, places, (0, 2))
 
     @pl.loop(0, BY)
     def _(y):
         for z in range(0, BZ, 2):
             n = y * BZ + z
-            terms(cells_xm + n, [{1: (None, key(n + k, 1))} for k in range(2)], (0, 1))
+            terms(cells_xm + n, [{1: (None, keys[1, n + k])} for k in range(2)], (0, 1))
 
     @pl.loop(0, BX)
     def _(x):
         for z in range(0, BZ, 2):
             n = x * BY * BZ + z
-            keys = [{2: (None, key(n + k, 3))} for k in range(2)]
-            terms(cells_ym + x * BZ + z, keys, (1, 2))
+            places = [{2: (None, keys[3, n + k])} for k in range(2)]
+            terms(cells_ym + x * BZ + z, places, (1, 2))
 
     @pl.loop(0, LINES // 2)
     def _(half):
         n = half * 2 * BZ
-        keys = [{3: (None, key(n + k * BZ, 5))} for k in range(2)]
-        terms(cells_zm + half * 2, keys, (1, 2))
+        places = [{3: (None, keys[5, n + k * BZ])} for k in range(2)]
+        terms(cells_zm + half * 2, places, (1, 2))
 
     depth = send.shape[0]
 
@@ -269,21 +267,21 @@
     def _(r):
         low, low_half = lane_low((64, 128)), lane_low((32, 128))
 
-        def folded(ref, s):
-            value = ref[r * SLOTS + s]
-            return value + pltpu.roll(value, 64, axis=1)
-
         for s in range(0, SLOTS, 2):
-            first = folded(acc_b, s)
-            pair = jnp.where(low, first, folded(acc_b, s + 1)) if s + 1 < SLOTS else first
+            first = acc_b[r * SLOTS + s]
+            second = acc_b[r * SLOTS + s + 1] if s + 1 < SLOTS else first
+            pair = jnp.where(low, first, second)
+            pair += pltpu.roll(jnp.where(low, second, first), 64, axis=1)
             flipped = pair.T
             for k in range(min(2, SLOTS - s)):
-                work = work_b.at[(s + k) // 4, pl.ds((s + k) % 4 * 64, 64)]
-                work[:, 0:64] = folded(acc_f, s + k)[:, 0:64] + flipped[k * 64 : k * 64 + 64]
-                even = work[pl.ds(0, 32, stride=2), :]
-                odd = work[pl.ds(1, 32, stride=2), :]
-                row = jnp.where(low_half, even, pltpu.roll(odd, 64, axis=1)).astype(BF16)
-                rows[pl.ds(pl.multiple_of(r * ROW + (s + k) * 32, 32), 32), :] = row
+                acc_f[r * SLOTS + s + k, :, 0:64] += flipped[k * 64 : k * 64 + 64]
+        for s in range(SLOTS):
+            total = acc_f.at[r * SLOTS + s]
+            even = total[pl.ds(0, 32, stride=2), :]
+            odd = total[pl.ds(1, 32, stride=2), :]
+            row = jnp.where(low_half, even, odd)
+            row += pltpu.roll(jnp.where(low_half, odd, even), 64, axis=1)
+            rows[pl.ds(pl.multiple_of(r * ROW + s * 32, 32), 32), :] = row.astype(BF16)
         c = owner[r]
         place = tally[c]
         tally[c] = place + 1
@@ -306,7 +304,7 @@
         pltpu.make_async_copy(rows.at[pl.ds(0, ROW)], send.at[0, pl.ds(0, ROW)], sems.at[r]).wait()
 
 
-def coarse_rows(agg, slot, owner, arrays, depth):
+def coarse_rows(keys, onward, owner, arrays, depth):
     smem = pl.BlockSpec(memory_space=pltpu.SMEM)
     vmem = pl.BlockSpec(memory_space=pltpu.VMEM)
     lines_right = LINES + BY + BX + LINES // 8
@@ -323,9 +321,9 @@
             pltpu.VMEM((lines_right * 512, 128), BF16),
             pltpu.VMEM((lines_right * 512, 128), BF16),
             pltpu.VMEM((lines_right * 512, 256), BF16),
-            pltpu.VMEM((4, 256, 128), F32),
-            pltpu.VMEM((2, 512, 128), F32),
-            pltpu.VMEM((2, 512, 128), F32),
+            pltpu.VMEM((4, 8 * STEP, 128), F32),
+            pltpu.VMEM((2, 8 * STEP_TWICE, 128), F32),
+            pltpu.VMEM((2, 8 * STEP_TWICE, 128), F32),
             pltpu.VMEM((KEYS + 1, 64, 128), F32),
             pltpu.VMEM((KEYS + 1, 64, 128), F32),
             pltpu.VMEM((AGG_DEV * ROW, 128), BF16),
@@ -336,7 +334,7 @@
         ],
         compiler_params=pltpu.CompilerParams(vmem_limit_bytes=63 << 20),
         name="coarse_rows",
-    )(agg, slot, owner, *arrays)
+    )(keys, onward, owner, *arrays)
 
 
 GROUP = 8
@@ -351,9 +349,10 @@
         def _():
             at = source[t]
             row = taken[at // PLACES, pl.ds(pl.multiple_of(at % PLACES * ROW, 32), ROW), :]
-            work[k, 0:ROW, :] = row.astype(F32)
+            for s in range(SLOTS):
+                work[k, s * STEP : s * STEP + 32, :] = row[s * 32 : s * 32 + 32].astype(F32)
             for tile in range(32):
-                piece = work[k, pl.ds(tile, SLOTS, stride=32), :]
+                piece = work[k, pl.ds(tile, SLOTS, stride=STEP), :]
                 out[k, :, tile * 128 : tile * 128 + 128] = piece.astype(BF16)
 
         @pl.when(t >= total[0])
@@ -410,9 +409,15 @@
         to_next(face_z(prolong[:, :, BZ - 1]), "gz"),
         to_previous(face_z(prolong[:, :, 0]), "gz"),
     ]
-    send = coarse_rows(
-        aggregate.reshape(-1), pair_slot.reshape(SLOTS, -1), row_owner, arrays, depth
+    keys = aggregate[None] * SLOTS + pair_slot
+    onward = jnp.stack(
+        [
+            jnp.pad(keys[1, 1:], ((0, 1), (0, 0), (0, 0)), constant_values=KEYS),
+            jnp.pad(keys[3, :, 1:], ((0, 0), (0, 1), (0, 0)), constant_values=KEYS),
+            jnp.pad(keys[5, :, :, 1:], ((0, 0), (0, 0), (0, 1)), constant_values=KEYS),
+        ]
     )
+    send = coarse_rows(keys.reshape(SLOTS, -1), onward.reshape(3, -1), row_owner, arrays, depth)
     taken = lax.all_to_all(send, "gz", 0, 0, tiled=True)
     count = taken[:, PLACES * ROW, 0].astype(jnp.int32)
     ends = jnp.cumsum(count)

time: 190 us -> 165 us (0.87)
  Pallas kernels: 76.1 us -> 49.9 us
    pallas_call x1, Pallas kernels: 70.9 us -> 46.7 us  [coarse_rows(): pl.pallas_call(compute_kernel, out_shape=jax.ShapeDtypeStruct((depth, PAC...]
    pallas_call x1, Pallas kernels: 5.2 us -> 3.19 us  [place_rows(): pl.pallas_call(place_kernel, out_shape=jax.ShapeDtypeStruct((count, SLOTS...]
    unnamed x18 -> x23, local copies, waits for them, and re-layouts: 5.61 us -> 4.85 us
  transfers between devices with their start and end apart: 9 -> 9, of which waited for: 3 -> 3; matrix products, arithmetic and copies ran while one was open for 5% -> 7% of each run, Pallas kernels for 0% -> 0%
where the time goes in v3:
time: 165 us; the launch traced here: 164 us
  blocking collectives  57 us (35%)
  Pallas kernels  49.9 us (30%)
  starting transfers between devices  27.4 us (17%)
  local copies, waits for them, and re-layouts  22.9 us (14%)
  waiting for transfers between devices  3.87 us (2%)
  other arithmetic  2.47 us (1%)
    all_to_all x1, blocking collectives, shards(): taken = lax.all_to_all(send, 'gz', 0, 0, tiled=True)  57 us
    pallas_call x1, Pallas kernels, coarse_rows(): pl.pallas_call(compute_kernel, out_shape=jax.ShapeDtypeStruct((depth, PAC...  46.7 us
    ppermute x6, starting transfers between devices, to_next(): return lax.ppermute(block, axis, [(i, i + 1) for i in range(count - 1)])  23.6 us
    unnamed x23, local copies, waits for them, and re-layouts  4.85 us
    reshape x1, local copies, waits for them, and re-layouts, shards(): return coarse.reshape(1, 1, 1, holding, SLOTS, block)  4.12 us
    ppermute x3, starting transfers between devices, to_previous(): return lax.ppermute(block, axis, [(i + 1, i) for i in range(count - 1)])  3.85 us
    slice x1, local copies, waits for them, and re-layouts, shards(): prolong[:, :, 0]  3.72 us
  transfers between devices with their start and end apart: 9, of which 3 were waited for; matrix products, arithmetic and copies ran while one was open for 7% of the time, Pallas kernels for 0%

profile of v3, /device:TPU:0, one launch (start us, length us, event | category | flops | bytes accessed | tf_op | source)
XLA Modules:
  0.0 163.9 jit_solution(15546712755815438598)
XLA Ops:
  0.0 2.8 %slice_reduce_fusion.2 = bf16[4,6,4096]{2,1,0:T(8,128)(2,1)S(1)} fusion(bf16[3,4,6,8,4096]{4,3,2,1,0:T(8,128)(2,1)} %param.7), kind=kLoop, calls=%fused_computation.4 | loop fusion | bytes 393216 | tf_op jit(solution)/shard_map/slice | solution.py:404
  2.8 0.1 reshape_squeeze.9
  2.8 5.1 %collective-permute-start.2 = (bf16[3,8,4096]{2,1,0:T(8,128)(2,1)S(1)}, bf16[3,8,4096]{2,1,0:T(8,128)(2,1)S(1)}, u32[]{:S(2)}, u32[]{:S(2)}) collective-permute-start(bf16[3,8,4096]{2,1,0:T(8,128)(2,1)S(1)} %reshape_squeeze.9), channel_id=1, source_target_pairs={{0,1},{1,2},{2,3},{3,4},{4,5},{5,6},{6,7},{7,8},{8,9},{9,10},{10,1... | collective-permute-start | bytes 589832 | tf_op jit(solution)/shard_map/ppermute | solution.py:382
  7.9 1.7 %slice_bitcast_fusion.5 = bf16[4,8,4096]{2,1,0:T(8,128)(2,1)} fusion(bf16[3,4,6,8,4096]{4,3,2,1,0:T(8,128)(2,1)} %param.7), kind=kLoop, calls=%fused_computation.8 | loop fusion | bytes 524288 | tf_op jit(solution)/shard_map/squeeze | solution.py:403
  9.6 3.2 %collective-permute-start.1 = (bf16[4,8,4096]{2,1,0:T(8,128)(2,1)}, bf16[4,8,4096]{2,1,0:T(8,128)(2,1)}, u32[]{:S(2)}, u32[]{:S(2)}) collective-permute-start(bf16[4,8,4096]{2,1,0:T(8,128)(2,1)} %slice_bitcast_fusion.5), channel_id=1, source_target_pairs={{0,32},{1,33},{2,34},{3,35},{4,36},{5,37},{6,38},{7,39},{8,40},{9,... | collective-permute-start | bytes 786440 | tf_op jit(solution)/shard_map/ppermute | solution.py:382
  12.8 1.0 slice_bitcast_fusion.2
  13.8 1.3 collective-permute-start
  15.1 3.7 %slice_reduce_fusion = (bf16[4,6,4096]{2,1,0:T(8,128)(2,1)S(1)}, bf16[4,6,4096]{2,1,0:T(8,128)(2,1)S(1)}) fusion(bf16[4,6,8,4096]{3,2,1,0:T(8,128)(2,1)} %param.8), kind=kLoop, calls=%fused_computation | loop fusion | bytes 786432 | tf_op jit(solution)/shard_map/slice | solution.py:410
  18.8 0.8 reshape_squeeze.10
  19.6 5.6 %collective-permute-start.7 = (bf16[3,8,4096]{2,1,0:T(8,128)(2,1)}, bf16[3,8,4096]{2,1,0:T(8,128)(2,1)}, u32[]{:S(2)}, u32[]{:S(2)}) collective-permute-start(bf16[3,8,4096]{2,1,0:T(8,128)(2,1)} %reshape_squeeze.10), channel_id=1, source_target_pairs={{0,1},{1,2},{2,3},{3,4},{4,5},{5,6},{6,7},{7,8},{8,9},{9,10},{10,1... | collective-permute-start | bytes 589832 | tf_op jit(solution)/shard_map/ppermute | solution.py:382
  25.2 0.8 reshape_squeeze.11
  26.0 1.3 collective-permute-start.8
  27.3 0.8 slice_bitcast_fusion.3
  28.1 0.8 slice_bitcast_fusion
  28.9 0.1 slice_bitcast_fusion.6
  29.0 0.0 collective-permute-done.2.rim_z
  29.0 1.3 collective-permute-start.4
  30.3 0.0 collective-permute-done.7.p_zm
  30.3 3.8 %collective-permute-start.3 = (bf16[6,8,4096]{2,1,0:T(8,128)(2,1)S(1)}, bf16[6,8,4096]{2,1,0:T(8,128)(2,1)}, u32[]{:S(2)}, u32[]{:S(2)}) collective-permute-start(bf16[6,8,4096]{2,1,0:T(8,128)(2,1)S(1)} %get-tuple-element.10), channel_id=1, source_target_pairs={{0,64},{1,65},{2,66},{3,67},{4,68},{5,69},{6,70},{7,71},{8,72},{9,... | collective-permute-start | bytes 1179656 | tf_op jit(solution)/shard_map/ppermute | solution.py:382
  34.1 0.1 stack.13
  34.3 0.1 stack.14
  34.3 1.1 collective-permute-done.8.p_zp
  35.4 1.3 collective-permute-start.6
  36.7 0.0 collective-permute-done.1.rim_y
  36.7 4.6 %collective-permute-start.5 = (bf16[4,8,4096]{2,1,0:T(8,128)(2,1)}, bf16[4,8,4096]{2,1,0:T(8,128)(2,1)S(1)}, u32[]{:S(2)}, u32[]{:S(2)}) collective-permute-start(bf16[4,8,4096]{2,1,0:T(8,128)(2,1)} %get-tuple-element.8), channel_id=1, source_target_pairs={{0,32},{1,33},{2,34},{3,35},{4,36},{5,37},{6,38},{7,39},{8,40},{9,... | collective-permute-start | bytes 786440 | tf_op jit(solution)/shard_map/ppermute | solution.py:382
  41.4 0.1 stack.12
  41.4 0.7 reshape.49.keys
  42.1 0.6 pad_add_fusion.onward
  42.7 1.2 collective-permute-done.6.p_yp
  43.9 1.6 collective-permute-done.5.p_ym
  45.5 0.0 collective-permute-done.rim_x
  45.5 0.0 collective-permute-done.4.p_xp
  45.5 0.0 collective-permute-done.3.p_xm
  45.5 0.7 copy-done.6
  46.2 0.1 copy-done.3
  46.3 0.1 copy-done.4
  46.5 46.7 %coarse_rows.1 = bf16[32,464,128]{2,1,0:T(8,128)(2,1)} custom-call(s32[7,192]{1,0:T(8,128)} %reshape.49.keys, s32[3,192]{1,0:T(4,128)} %pad_add_fusion.onward, s32[24]{0:T(128)} %owner.1, bf16[24,8,4096]{2,1,0:T(8,128)(2,1)} %bitcast.36, bf16[3,24,8,4096]{3,2,1,0:T(8,128)(2,1)} %bitcast.35, bf16[24,8,4096]{2,1,0:T(8,128)(2,1)} %bitcast.34, ...), custom_call_target="tpu_custom_call" | custom-call | tf_op jit(solution)/shard_map/coarse_rows/pallas_call | solution.py:311
  93.2 57.0 %all_to_all.5.taken = bf16[32,464,128]{2,1,0:T(8,128)(2,1)S(1)} all-to-all(bf16[32,464,128]{2,1,0:T(8,128)(2,1)} %coarse_rows.1), channel_id=1, replica_groups=mesh['gx'=2,'gy'=2,'gz'=32] {'gz'}, dimensions={0} | all-to-all | bytes 7602176 | tf_op jit(solution)/shard_map/all_to_all | solution.py:421
  150.2 1.8 %copy-done = bf16[32,464,128]{2,1,0:T(8,128)(2,1)} copy-done((bf16[32,464,128]{2,1,0:T(8,128)(2,1)}, bf16[32,464,128]{2,1,0:T(8,128)(2,1)S(1)}, u32[]{:S(2)}) %copy-start) | copy-done | bytes 3801112
  152.1 0.1 reduce-window.4
  152.1 0.5 slice.64
  152.6 0.1 reduce.3
  152.8 0.1 convert_reduce_fusion
  152.8 1.5 fusion
  154.3 0.1 select_reduce_fusion
  154.5 2.1 %copy-done.1 = bf16[32,464,128]{2,1,0:T(8,128)(2,1)S(1)} copy-done((bf16[32,464,128]{2,1,0:T(8,128)(2,1)S(1)}, bf16[32,464,128]{2,1,0:T(8,128)(2,1)}, u32[]{:S(2)}) %copy-start.1) | copy-done | bytes 3801112
  156.5 3.2 %place_rows.1 = bf16[64,7,4096]{2,1,0:T(8,128)(2,1)S(1)} custom-call(s32[64]{0:T(128)S(1)} %add_minimum_fusion.source, s32[1]{0:T(128)} %bitcast.13.total, bf16[32,464,128]{2,1,0:T(8,128)(2,1)S(1)} %copy-done.1), custom_call_target="tpu_custom_call" | custom-call | tf_op jit(solution)/shard_map/place_rows/pallas_call | solution.py:365
  159.7 4.1 %copy.33 = bf16[1,1,1,64,7,4096]{5,3,4,2,1,0:T(8,128)(2,1)} copy(bf16[1,1,1,64,7,4096]{5,4,3,2,1,0:T(8,128)(2,1)S(1)} %bitcast.33) | data formatting | bytes 7340032 | tf_op jit(solution)/shard_map/reshape | solution.py:431
  (28 shorter events, 0.1 us)
Async XLA Ops:
  0.0 27.2 %copy-start.2 = (bf16[4,6,8,4096]{3,2,1,0:T(8,128)(2,1)S(1)}, bf16[4,6,8,4096]{3,2,1,0:T(8,128)(2,1)}, u32[]{:S(2)}) copy-start(bf16[4,6,8,4096]{3,2,1,0:T(8,128)(2,1)} %param.8) | copy-start | bytes 4718596
  0.0 28.9 %copy-start.9 = (s32[4,6,8]{2,0,1:T(4,128)S(1)}, s32[4,6,8]{2,0,1:T(4,128)}, u32[]{:S(2)}) copy-start(s32[4,6,8]{2,0,1:T(4,128)} %param.9) | copy-start | bytes 2308
  0.0 28.9 %copy-start.8 = (s32[7,4,6,8]{3,1,2,0:T(4,128)S(1)}, s32[7,4,6,8]{3,1,2,0:T(4,128)}, u32[]{:S(2)}) copy-start(s32[7,4,6,8]{3,1,2,0:T(4,128)} %param.10) | copy-start | bytes 16132
  2.8 26.1 %collective-permute-start.2 = (bf16[3,8,4096]{2,1,0:T(8,128)(2,1)S(1)}, bf16[3,8,4096]{2,1,0:T(8,128)(2,1)S(1)}, u32[]{:S(2)}, u32[]{:S(2)}) collective-permute-start(bf16[3,8,4096]{2,1,0:T(8,128)(2,1)S(1)} %reshape_squeeze.9), channel_id=1, source_target_pairs={{0,1},{1,2},{2,3},{3,4},{4,5},{5,6},{6,7},{7,8},{8,9},{9,10},{10,1... | collective-permute-start | bytes 589832 | tf_op jit(solution)/shard_map/ppermute | solution.py:382
  9.6 27.2 %collective-permute-start.1 = (bf16[4,8,4096]{2,1,0:T(8,128)(2,1)}, bf16[4,8,4096]{2,1,0:T(8,128)(2,1)}, u32[]{:S(2)}, u32[]{:S(2)}) collective-permute-start(bf16[4,8,4096]{2,1,0:T(8,128)(2,1)} %slice_bitcast_fusion.5), channel_id=1, source_target_pairs={{0,32},{1,33},{2,34},{3,35},{4,36},{5,37},{6,38},{7,39},{8,40},{9,... | collective-permute-start | bytes 786440 | tf_op jit(solution)/shard_map/ppermute | solution.py:382
  13.8 31.7 %collective-permute-start = (bf16[6,8,4096]{2,1,0:T(8,128)(2,1)S(1)}, bf16[6,8,4096]{2,1,0:T(8,128)(2,1)S(1)}, u32[]{:S(2)}, u32[]{:S(2)}) collective-permute-start(bf16[6,8,4096]{2,1,0:T(8,128)(2,1)S(1)} %slice_bitcast_fusion.2), channel_id=1, source_target_pairs={{0,64},{1,65},{2,66},{3,67},{4,68},{5,69},{6,70},{7,71},{8,72},{9,... | collective-permute-start | bytes 1179656 | tf_op jit(solution)/shard_map/ppermute | solution.py:382
  19.6 10.7 %collective-permute-start.7 = (bf16[3,8,4096]{2,1,0:T(8,128)(2,1)}, bf16[3,8,4096]{2,1,0:T(8,128)(2,1)}, u32[]{:S(2)}, u32[]{:S(2)}) collective-permute-start(bf16[3,8,4096]{2,1,0:T(8,128)(2,1)} %reshape_squeeze.10), channel_id=1, source_target_pairs={{0,1},{1,2},{2,3},{3,4},{4,5},{5,6},{6,7},{7,8},{8,9},{9,10},{10,1... | collective-permute-start | bytes 589832 | tf_op jit(solution)/shard_map/ppermute | solution.py:382
  26.0 9.5 %collective-permute-start.8 = (bf16[3,8,4096]{2,1,0:T(8,128)(2,1)}, bf16[3,8,4096]{2,1,0:T(8,128)(2,1)}, u32[]{:S(2)}, u32[]{:S(2)}) collective-permute-start(bf16[3,8,4096]{2,1,0:T(8,128)(2,1)} %reshape_squeeze.11), channel_id=1, source_target_pairs={{1,0},{2,1},{3,2},{4,3},{5,4},{6,5},{7,6},{8,7},{9,8},{10,9},{11,1... | collective-permute-start | bytes 589832 | tf_op jit(solution)/shard_map/ppermute | solution.py:387
  29.0 17.2 %copy-start.7 = (bf16[3,8,4096]{2,1,0:T(8,128)(2,1)}, bf16[3,8,4096]{2,1,0:T(8,128)(2,1)S(1)}, u32[]{:S(2)}) copy-start(bf16[3,8,4096]{2,1,0:T(8,128)(2,1)S(1)} %collective-permute-done.2.rim_z) | copy-start | bytes 589828
  29.0 16.5 %collective-permute-start.4 = (bf16[6,8,4096]{2,1,0:T(8,128)(2,1)}, bf16[6,8,4096]{2,1,0:T(8,128)(2,1)S(1)}, u32[]{:S(2)}, u32[]{:S(2)}) collective-permute-start(bf16[6,8,4096]{2,1,0:T(8,128)(2,1)} %get-tuple-element.9), channel_id=1, source_target_pairs={{64,0},{65,1},{66,2},{67,3},{68,4},{69,5},{70,6},{71,7},{72,8},{73... | collective-permute-start | bytes 1179656 | tf_op jit(solution)/shard_map/ppermute | solution.py:387
  30.3 15.2 %collective-permute-start.3 = (bf16[6,8,4096]{2,1,0:T(8,128)(2,1)S(1)}, bf16[6,8,4096]{2,1,0:T(8,128)(2,1)}, u32[]{:S(2)}, u32[]{:S(2)}) collective-permute-start(bf16[6,8,4096]{2,1,0:T(8,128)(2,1)S(1)} %get-tuple-element.10), channel_id=1, source_target_pairs={{0,64},{1,65},{2,66},{3,67},{4,68},{5,69},{6,70},{7,71},{8,72},{9,... | collective-permute-start | bytes 1179656 | tf_op jit(solution)/shard_map/ppermute | solution.py:382
  35.4 8.5 %collective-permute-start.6 = (bf16[4,8,4096]{2,1,0:T(8,128)(2,1)}, bf16[4,8,4096]{2,1,0:T(8,128)(2,1)S(1)}, u32[]{:S(2)}, u32[]{:S(2)}) collective-permute-start(bf16[4,8,4096]{2,1,0:T(8,128)(2,1)} %get-tuple-element.7), channel_id=1, source_target_pairs={{32,0},{33,1},{34,2},{35,3},{36,4},{37,5},{38,6},{39,7},{40,8},{41... | collective-permute-start | bytes 786440 | tf_op jit(solution)/shard_map/ppermute | solution.py:387
  36.7 8.8 %collective-permute-start.5 = (bf16[4,8,4096]{2,1,0:T(8,128)(2,1)}, bf16[4,8,4096]{2,1,0:T(8,128)(2,1)S(1)}, u32[]{:S(2)}, u32[]{:S(2)}) collective-permute-start(bf16[4,8,4096]{2,1,0:T(8,128)(2,1)} %get-tuple-element.8), channel_id=1, source_target_pairs={{0,32},{1,33},{2,34},{3,35},{4,36},{5,37},{6,38},{7,39},{8,40},{9,... | collective-permute-start | bytes 786440 | tf_op jit(solution)/shard_map/ppermute | solution.py:382
  43.9 1.6 copy-start.5
  45.5 0.7 copy-start.6
  45.5 0.8 copy-start.3
  45.5 1.0 copy-start.4
  150.2 1.8 %copy-start = (bf16[32,464,128]{2,1,0:T(8,128)(2,1)}, bf16[32,464,128]{2,1,0:T(8,128)(2,1)S(1)}, u32[]{:S(2)}) copy-start(bf16[32,464,128]{2,1,0:T(8,128)(2,1)S(1)} %all_to_all.5.taken) | copy-start | bytes 11403268
  154.5 2.1 %copy-start.1 = (bf16[32,464,128]{2,1,0:T(8,128)(2,1)S(1)}, bf16[32,464,128]{2,1,0:T(8,128)(2,1)}, u32[]{:S(2)}) copy-start(bf16[32,464,128]{2,1,0:T(8,128)(2,1)} %copy-done) | copy-start | bytes 11403268

commit v4 on v3

--- a/solution.py
+++ b/solution.py
@@ -45,11 +45,129 @@
             by_parity[pl.ds(32 + tile, 8, stride=STEP_TWICE), :] = odd
 
 
+MESH = pl.DeviceIdType.MESH
+
+
+def halo_kernel(
+    prolong, a_face,
+    rim_x, rim_y, rim_z, p_xm, p_xp, p_ym, p_yp, p_zm, p_zp,
+    cells, faces, work, zero, zero_z, out_az, out_p_last, out_p_first, load_sems, send_sems, recv_sems, zero_sems,
+):
+    depth = lax.axis_size("gz")
+    gx, gy, gz = (lax.axis_index(axis) for axis in ("gx", "gy", "gz"))
+    next_z, previous_z = lax.rem(gz + 1, depth), lax.rem(gz + depth - 1, depth)
+    barrier = pltpu.get_barrier_semaphore()
+    for target in ({"gx": 1 - gx}, {"gy": 1 - gy}, {"gz": next_z}, {"gz": previous_z}):
+        pl.semaphore_signal(barrier, inc=1, device_id=target, device_id_type=MESH)
+    loads = [
+        pltpu.make_async_copy(prolong, cells, load_sems.at[0]),
+        pltpu.make_async_copy(a_face.at[2], faces, load_sems.at[1]),
+    ]
+    for load in loads:
+        load.start()
+    zero[...] = jnp.zeros_like(zero)
+    zero_z[...] = jnp.zeros_like(zero_z)
+    pl.semaphore_wait(barrier, 4)
+
+    def exchange(number, source, dest, target, sends, receives, blank):
+        copy = pltpu.make_async_remote_copy(
+            source, dest, send_sems.at[number], recv_sems.at[number], device_id=target, device_id_type=MESH
+        )
+        fill = pltpu.make_async_copy(blank, dest, zero_sems.at[number])
+
+        @pl.when(sends)
+        def _():
+            copy.start()
+
+        @pl.when(jnp.logical_not(receives))
+        def _():
+            fill.start()
+
+        def finish():
+            @pl.when(sends)
+            def _():
+                copy.wait_send()
+
+            @pl.when(receives)
+            def _():
+                copy.wait_recv()
+
+            @pl.when(jnp.logical_not(receives))
+            def _():
+                fill.wait()
+
+        return finish
+
+    ends = []
+    for number, axis, here, last, first, pairs in (
+        (0, "gx", gx, lambda ref: ref.at[BX - 1], lambda ref: ref.at[0], (p_xm, p_xp, rim_x)),
+        (3, "gy", gy, lambda ref: ref.at[:, BY - 1], lambda ref: ref.at[:, 0], (p_ym, p_yp, rim_y)),
+    ):
+        count = lax.axis_size(axis)
+        up, down = {axis: lax.rem(here + 1, count)}, {axis: lax.rem(here + count - 1, count)}
+        before, after = here > 0, here < count - 1
+        blank = zero.at[pl.ds(0, pairs[0].shape[0])]
+        ends += [
+            exchange(number, last(prolong), pairs[0], up, after, before, blank),
+            exchange(number + 1, first(prolong), pairs[1], down, before, after, blank),
+            exchange(number + 2, last(a_face.at[number // 3]), pairs[2], up, after, before, blank),
+        ]
+    for load in loads:
+        load.wait()
+
+    @pl.loop(0, LINES)
+    def _(line):
+        at = pl.ds(pl.multiple_of(line * 32, 32), 32)
+        x, y = line // BY, line % BY
+        spread(cells[x, y], work.at[0])
+        out_p_first[at, :] = work[0, 0:32, :].astype(BF16)
+        out_p_last[at, :] = work[0, 7 * STEP : 7 * STEP + 32, :].astype(BF16)
+        spread(faces[x, y], work.at[1])
+        out_az[at, :] = work[1, 7 * STEP : 7 * STEP + 32, :].astype(BF16)
+
+    before, after = gz > 0, gz < depth - 1
+    ends += [
+        exchange(6, out_p_last, p_zm, {"gz": next_z}, after, before, zero_z),
+        exchange(7, out_p_first, p_zp, {"gz": previous_z}, before, after, zero_z),
+        exchange(8, out_az, rim_z, {"gz": next_z}, after, before, zero_z),
+    ]
+    for finish in ends:
+        finish()
+
+
+def halo(prolong, a_face):
+    any_space = pl.BlockSpec(memory_space=pl.ANY)
+    x_face, y_face, z_face = (BY, BZ, NODES * NODES), (BX, BZ, NODES * NODES), (LINES * 32, 128)
+    shapes = (x_face, y_face, z_face, x_face, x_face, y_face, y_face, z_face, z_face)
+    return pl.pallas_call(
+        halo_kernel,
+        out_shape=[jax.ShapeDtypeStruct(shape, BF16) for shape in shapes],
+        in_specs=[any_space] * 2,
+        out_specs=[any_space] * len(shapes),
+        scratch_shapes=[
+            pltpu.VMEM(prolong.shape, BF16),
+            pltpu.VMEM(prolong.shape, BF16),
+            pltpu.VMEM((2, 8 * STEP, 128), F32),
+            pltpu.VMEM(x_face, BF16),
+            pltpu.VMEM(z_face, BF16),
+            pltpu.VMEM(z_face, BF16),
+            pltpu.VMEM(z_face, BF16),
+            pltpu.VMEM(z_face, BF16),
+            pltpu.SemaphoreType.DMA((2,)),
+            pltpu.SemaphoreType.DMA((9,)),
+            pltpu.SemaphoreType.DMA((9,)),
+            pltpu.SemaphoreType.DMA((9,)),
+        ],
+        compiler_params=pltpu.CompilerParams(collective_id=0, has_side_effects=True, vmem_limit_bytes=63 << 20),
+        name="halo",
+    )(prolong, a_face)
+
+
 def compute_kernel(
-    keys, onward, owner,
+    aggregate, slot, owner,
     a_diag, a_face, prolong, rim_x, rim_y, rim_z,
     p_xm, p_xp, p_ym, p_yp, p_zm, p_zp,
-    send,
+    send, keys, key_work, key_sem,
     ra_d, ra_x, ra_y, ra_z, right, left, couple, work_a, work_b, work_c,
     acc_f, acc_b, rows, counts, tally, sems, count_sem,
 ):
@@ -77,6 +195,9 @@
             at = pl.multiple_of(base * 512 + pair * 128, 128)
             left[pl.ds(at, 128), :] = block.astype(BF16).T
 
+    key_work[...] = aggregate[...][None] * SLOTS + slot[...]
+    told_keys = pltpu.make_async_copy(key_work, keys, key_sem)
+    told_keys.start()
     acc_f[...] = jnp.zeros_like(acc_f)
     acc_b[...] = jnp.zeros_like(acc_b)
 
@@ -113,16 +234,30 @@
             spread_twice(p_yp[line], work_b.at[k], None)
             store_right(right_yp + line, work_b.at[k])
 
-    for line in range(LINES // 8):
-        work = work_a.at[line]
-        spread(rim_z[line], work)
-        for k in range(8):
-            at = (line * 8 + k) * 288
-            ra_z[at : at + 32, :] = work[k * STEP : k * STEP + 32, :].astype(BF16)
-        spread_twice(p_zm[line], None, work_c.at[line % 2])
-        store_left(left_zm + line, work_c.at[line % 2])
-        spread_twice(p_zp[line], work_b.at[line % 2], None)
-        store_right(right_zp + line, work_b.at[line % 2])
+    @pl.loop(0, LINES // 2)
+    def _(half):
+        low = lane_low((32, 128))
+        blocks = []
+        for k in range(2):
+            line = half * 2 + k
+            at = pl.ds(pl.multiple_of(line * 32, 32), 32)
+            ra_z[pl.ds(pl.multiple_of(line * 288, 32), 32), :] = rim_z[at, :]
+            here = p_zp[at, :].astype(F32)
+            turned = pltpu.roll(here, 64, axis=1)
+            work = work_b.at[k]
+            work[pl.ds(0, 32, stride=2), :] = jnp.where(low, here, turned)
+            work[pl.ds(1, 32, stride=2), :] = jnp.where(low, turned, here)
+            at_right = pl.multiple_of((right_zp * 8 + line) * 64, 64)
+            right[pl.ds(at_right, 64), :] = work[0:64, :].astype(BF16)
+            here = p_zm[at, :].astype(F32)
+            turned = pltpu.roll(here, 64, axis=1)
+            zero = jnp.zeros_like(here)
+            if k == 0:
+                blocks += [jnp.where(low, here, zero), jnp.where(low, turned, zero)]
+            else:
+                blocks += [jnp.where(low, zero, turned), jnp.where(low, zero, here)]
+        block = jnp.concatenate(blocks, axis=0).astype(BF16)
+        left[pl.ds(pl.multiple_of((left_zm * 8 + half * 2) * 64, 128), 128), :] = block.T
 
     def couples(cell, blocks):
         low = lane_low((64, 128))
@@ -173,6 +308,7 @@
                     add(acc_b, key_b, f % 2 == 0, term)
 
     cells_xm, cells_ym, cells_zm = left_xm * 8, left_ym * 8, left_zm * 8
+    told_keys.wait()
 
     @pl.loop(0, LINES)
     def _(line):
@@ -224,16 +360,19 @@
 
     @pl.loop(0, LINES)
     def _(line):
+        x, y = line // BY, line % BY
+        next_x, next_y = jnp.minimum(x + 1, BX - 1), jnp.minimum(y + 1, BY - 1)
         for z in range(0, BZ, 2):
             places = []
-            for k in range(2):
-                e = line * BZ + z + k
+            for k in range(z, z + 2):
+                onward_x = jnp.where(x < BX - 1, keys[1, y, next_x, k], KEYS)
+                onward_y = jnp.where(y < BY - 1, keys[3, next_y, x, k], KEYS)
                 places.append(
                     {
-                        0: (keys[0, e], None),
-                        1: (keys[2, e], onward[0, e]),
-                        2: (keys[4, e], onward[1, e]),
-                        3: (keys[6, e], onward[2, e] if z + k < BZ - 1 else None),
+                        0: (keys[0, y, x, k], None),
+                        1: (keys[2, y, x, k], onward_x),
+                        2: (keys[4, y, x, k], onward_y),
+                        3: (keys[6, y, x, k], keys[5, y, x, k + 1] if k < BZ - 1 else None),
                     }
                 )
             terms(line * BZ + z, places, (0, 2))
@@ -242,19 +381,18 @@
     def _(y):
         for z in range(0, BZ, 2):
             n = y * BZ + z
-            terms(cells_xm + n, [{1: (None, keys[1, n + k])} for k in range(2)], (0, 1))
+            terms(cells_xm + n, [{1: (None, keys[1, y, 0, z + k])} for k in range(2)], (0, 1))
 
     @pl.loop(0, BX)
     def _(x):
         for z in range(0, BZ, 2):
-            n = x * BY * BZ + z
-            places = [{2: (None, keys[3, n + k])} for k in range(2)]
+            places = [{2: (None, keys[3, 0, x, z + k])} for k in range(2)]
             terms(cells_ym + x * BZ + z, places, (1, 2))
 
     @pl.loop(0, LINES // 2)
     def _(half):
-        n = half * 2 * BZ
-        places = [{3: (None, keys[5, n + k * BZ])} for k in range(2)]
+        line = half * 2
+        places = [{3: (None, keys[5, line % BY + k, line // BY, 0])} for k in range(2)]
         terms(cells_zm + half * 2, places, (1, 2))
 
     depth = send.shape[0]
@@ -304,16 +442,19 @@
         pltpu.make_async_copy(rows.at[pl.ds(0, ROW)], send.at[0, pl.ds(0, ROW)], sems.at[r]).wait()
 
 
-def coarse_rows(keys, onward, owner, arrays, depth):
+def coarse_rows(aggregate, slot, owner, arrays, depth):
     smem = pl.BlockSpec(memory_space=pltpu.SMEM)
     vmem = pl.BlockSpec(memory_space=pltpu.VMEM)
     lines_right = LINES + BY + BX + LINES // 8
     return pl.pallas_call(
         compute_kernel,
         out_shape=jax.ShapeDtypeStruct((depth, PACK, 128), BF16),
-        in_specs=[smem] * 3 + [vmem] * len(arrays),
+        in_specs=[vmem, vmem, smem] + [vmem] * len(arrays),
         out_specs=pl.BlockSpec(memory_space=pl.ANY),
         scratch_shapes=[
+            pltpu.SMEM((SLOTS, BY, BX, BZ), jnp.int32),
+            pltpu.VMEM((SLOTS, BY, BX, BZ), jnp.int32),
+            pltpu.SemaphoreType.DMA,
             pltpu.VMEM((LINES * 256, 128), BF16),
             pltpu.VMEM(((LINES + BY) * 256, 128), BF16),
             pltpu.VMEM((BX * (BY + 1) * 256, 128), BF16),
@@ -334,57 +475,94 @@
         ],
         compiler_params=pltpu.CompilerParams(vmem_limit_bytes=63 << 20),
         name="coarse_rows",
-    )(keys, onward, owner, *arrays)
-
-
-GROUP = 8
-
-
-def place_kernel(source, total, taken, out, work):
-    step = pl.program_id(0)
-    for k in range(GROUP):
-        t = step * GROUP + k
-
-        @pl.when(t < total[0])
+    )(aggregate, slot, owner, *arrays)
+
+
+GROUP, ROW_STEP = 8, ROW + 4
+
+
+def place_kernel(taken, out, told, counts, tally, source, held, work, shaped, sems, row_sems, out_sems):
+    depth, count = taken.shape[0], out.shape[1]
+    load = pltpu.make_async_copy(taken.at[:, pl.ds(PLACES * ROW, 16)], told, sems.at[0])
+    load.start()
+
+    @pl.loop(0, count + PLACES)
+    def _(t):
+        source[t] = 0
+
+    load.wait()
+    for c in range(depth):
+        counts[c : c + 1, :] = told[c, 0:1, :].astype(F32).astype(jnp.int32)
+    move = pltpu.make_async_copy(counts, tally, sems.at[1])
+    move.start()
+    move.wait()
+
+    def order(c, total):
+        for k in range(PLACES):
+            source[total + k] = c * PLACES + k
+        return total + tally[c, 0]
+
+    total = lax.fori_loop(0, depth, order, 0)
+
+    def row_copy(t):
+        at = source[t]
+        place = pl.multiple_of(lax.rem(at, PLACES) * ROW, 32)
+        return pltpu.make_async_copy(taken.at[at // PLACES, pl.ds(place, ROW)], held.at[t], row_sems.at[t])
+
+    @pl.loop(0, count)
+    def _(t):
+        @pl.when(t >= total)
         def _():
-            at = source[t]
-            row = taken[at // PLACES, pl.ds(pl.multiple_of(at % PLACES * ROW, 32), ROW), :]
-            for s in range(SLOTS):
-                work[k, s * STEP : s * STEP + 32, :] = row[s * 32 : s * 32 + 32].astype(F32)
+            source[t] = 0
+
+        row_copy(t).start()
+
+    def out_copy(group):
+        rows = pl.ds(pl.multiple_of(group * GROUP, GROUP), GROUP)
+        return pltpu.make_async_copy(shaped.at[group], out.at[:, rows, :], out_sems.at[group])
+
+    @pl.loop(0, count // GROUP)
+    def _(group):
+        for k in range(GROUP):
+            t = group * GROUP + k
+            row_copy(t).wait()
+            row = held[t].astype(F32)
+            work[k * ROW_STEP : k * ROW_STEP + ROW, :] = jnp.where(t < total, row, jnp.zeros_like(row))
+        for s in range(SLOTS):
             for tile in range(32):
-                piece = work[k, pl.ds(tile, SLOTS, stride=STEP), :]
-                out[k, :, tile * 128 : tile * 128 + 128] = piece.astype(BF16)
-
-        @pl.when(t >= total[0])
-        def _():
-            out[k] = jnp.zeros((SLOTS, NODES * NODES), BF16)
-
-
-def place_rows(source, total, taken):
-    count = source.shape[0]
+                piece = work[pl.ds(s * 32 + tile, GROUP, stride=ROW_STEP), :]
+                shaped[group, s, :, tile * 128 : tile * 128 + 128] = piece.astype(BF16)
+        out_copy(group).start()
+
+    @pl.loop(0, count // GROUP)
+    def _(group):
+        out_copy(group).wait()
+
+
+def place_rows(taken):
+    depth = taken.shape[0]
+    count = depth * PLACES
+    any_space = pl.BlockSpec(memory_space=pl.ANY)
     return pl.pallas_call(
         place_kernel,
-        out_shape=jax.ShapeDtypeStruct((count, SLOTS, NODES * NODES), BF16),
-        grid_spec=pltpu.PrefetchScalarGridSpec(
-            num_scalar_prefetch=2,
-            grid=(count // GROUP,),
-            in_specs=[pl.BlockSpec(memory_space=pltpu.VMEM)],
-            out_specs=pl.BlockSpec((GROUP, SLOTS, NODES * NODES), lambda i, s, n: (i, 0, 0)),
-            scratch_shapes=[pltpu.VMEM((GROUP, 256, 128), F32)],
-        ),
-        compiler_params=pltpu.CompilerParams(vmem_limit_bytes=40 << 20),
+        out_shape=jax.ShapeDtypeStruct((SLOTS, count, NODES * NODES), BF16),
+        in_specs=[any_space],
+        out_specs=any_space,
+        scratch_shapes=[
+            pltpu.VMEM((depth, 16, 128), BF16),
+            pltpu.VMEM((depth, 128), jnp.int32),
+            pltpu.SMEM((depth, 128), jnp.int32),
+            pltpu.SMEM((count + PLACES,), jnp.int32),
+            pltpu.VMEM((count, ROW, 128), BF16),
+            pltpu.VMEM((GROUP * ROW_STEP, 128), F32),
+            pltpu.VMEM((count // GROUP, SLOTS, GROUP, NODES * NODES), BF16),
+            pltpu.SemaphoreType.DMA((2,)),
+            pltpu.SemaphoreType.DMA((count,)),
+            pltpu.SemaphoreType.DMA((count // GROUP,)),
+        ],
+        compiler_params=pltpu.CompilerParams(vmem_limit_bytes=63 << 20),
         name="place_rows",
-    )(source, total, taken)
-
-
-def to_next(block, axis):
-    count = lax.axis_size(axis)
-    return lax.ppermute(block, axis, [(i, i + 1) for i in range(count - 1)])
-
-
-def to_previous(block, axis):
-    count = lax.axis_size(axis)
-    return lax.ppermute(block, axis, [(i + 1, i) for i in range(count - 1)])
+    )(taken)
 
 
 def shards(a_diag, a_face, prolong, aggregate, pair_slot, row_owner):
@@ -392,42 +570,17 @@
     depth = lax.axis_size("gz")
     holding = PLACES * depth
 
-    def face_z(cells):
-        return cells.reshape(LINES // 8, 8, block)
-
     arrays = [
         a_diag.reshape(LINES, BZ, block),
         a_face.reshape(3, LINES, BZ, block),
         prolong.reshape(LINES, BZ, block),
-        to_next(a_face[0, BX - 1], "gx"),
-        to_next(a_face[1, :, BY - 1], "gy"),
-        to_next(face_z(a_face[2, :, :, BZ - 1]), "gz"),
-        to_next(prolong[BX - 1], "gx"),
-        to_previous(prolong[0], "gx"),
-        to_next(prolong[:, BY - 1], "gy"),
-        to_previous(prolong[:, 0], "gy"),
-        to_next(face_z(prolong[:, :, BZ - 1]), "gz"),
-        to_previous(face_z(prolong[:, :, 0]), "gz"),
+        *halo(prolong, a_face),
     ]
-    keys = aggregate[None] * SLOTS + pair_slot
-    onward = jnp.stack(
-        [
-            jnp.pad(keys[1, 1:], ((0, 1), (0, 0), (0, 0)), constant_values=KEYS),
-            jnp.pad(keys[3, :, 1:], ((0, 0), (0, 1), (0, 0)), constant_values=KEYS),
-            jnp.pad(keys[5, :, :, 1:], ((0, 0), (0, 0), (0, 1)), constant_values=KEYS),
-        ]
+    send = coarse_rows(
+        aggregate.transpose(1, 0, 2), pair_slot.transpose(0, 2, 1, 3), row_owner, arrays, depth
     )
-    send = coarse_rows(keys.reshape(SLOTS, -1), onward.reshape(3, -1), row_owner, arrays, depth)
     taken = lax.all_to_all(send, "gz", 0, 0, tiled=True)
-    count = taken[:, PLACES * ROW, 0].astype(jnp.int32)
-    ends = jnp.cumsum(count)
-    spot = jnp.arange(holding, dtype=jnp.int32)
-    origin = jnp.sum((ends[None, :] <= spot[:, None]).astype(jnp.int32), axis=1)
-    starts = jnp.sum(
-        jnp.where(jnp.arange(depth)[None, :] < origin[:, None], count[None, :], 0), axis=1
-    )
-    source = jnp.minimum(origin * PLACES + (spot - starts), holding - 1)
-    coarse = place_rows(source, ends[-1:], taken)
+    coarse = place_rows(taken).transpose(1, 0, 2)
     return coarse.reshape(1, 1, 1, holding, SLOTS, block)
 
 

time: 165 us -> 144 us (0.87)
  Pallas kernels: 49.9 us -> 85.8 us
  starting transfers between devices: 27.4 us -> 0 us
  local copies, waits for them, and re-layouts: 22.9 us -> 0 us
  waiting for transfers between devices: 3.87 us -> 0 us
  other arithmetic: 2.47 us -> 0 us
    pallas_call x1 -> x2, Pallas kernels: 3.19 us -> 37.7 us  [the longest x1 29.1 us: halo(): pl.pallas_call(halo_kernel, out_shape=[jax.ShapeDtypeStruct(shape, BF16)...]
    ppermute x9 -> x0, starting transfers between devices: 27.4 us -> none  [the longest x6 23.6 us: to_next(): return lax.ppermute(block, axis, [(i, i + 1) for i in range(count - 1)])]
    slice x3 -> x0, local copies, waits for them, and re-layouts: 6.99 us -> none  [the longest x1 3.72 us: shards(): prolong[:, :, 0]]
    unnamed x23 -> x0, local copies, waits for them, and re-layouts: 4.85 us -> none
    reshape x2 -> x0, local copies, waits for them, and re-layouts: 4.82 us -> none  [the longest x1 4.12 us: shards(): return coarse.reshape(1, 1, 1, holding, SLOTS, block)]
    squeeze x7 -> x0, local copies, waits for them, and re-layouts: 4.39 us -> none  [the longest x1 1.67 us: shards(): a_face[1, :, BY - 1]]
    ppermute x9 -> x0, waiting for transfers between devices: 3.87 us -> none  [the longest x3 2.27 us: to_previous(): return lax.ppermute(block, axis, [(i + 1, i) for i in range(count - 1)])]
    another operation x6 -> x0, local copies, waits for them, and re-layouts: 1.84 us -> none  [the longest x3 1.59 us: face_z(): return cells.reshape(LINES // 8, 8, block)]
  transfers between devices with their start and end apart: 9 -> 0, of which waited for: 3 -> 0; matrix products, arithmetic and copies ran while one was open for 7% -> 0% of each run, Pallas kernels for 0% -> 0%
where the time goes in v4:
time: 144 us
  Pallas kernels  85.8 us (60%)
  blocking collectives  58.2 us (40%)
    all_to_all x1, blocking collectives, shards(): taken = lax.all_to_all(send, 'gz', 0, 0, tiled=True)  58.2 us
    pallas_call x1, Pallas kernels, coarse_rows(): pl.pallas_call(compute_kernel, out_shape=jax.ShapeDtypeStruct((depth, PAC...  48.1 us
    pallas_call x1, Pallas kernels, halo(): pl.pallas_call(halo_kernel, out_shape=[jax.ShapeDtypeStruct(shape, BF16)...  29.1 us
    pallas_call x1, Pallas kernels, place_rows(): pl.pallas_call(place_kernel, out_shape=jax.ShapeDtypeStruct((SLOTS, count...  8.6 us

profile of v4, /device:TPU:0, one launch (start us, length us, event | category | flops | bytes accessed | tf_op | source)
XLA Modules:
  0.0 144.1 jit_solution(15602111416524213961)
XLA Ops:
  0.0 29.1 %halo.1 = (bf16[6,8,4096]{2,1,0:T(8,128)(2,1)}, bf16[4,8,4096]{2,1,0:T(8,128)(2,1)}, bf16[768,128]{1,0:T(8,128)(2,1)}, bf16[6,8,4096]{2,1,0:T(8,128)(2,1)}, bf16...) custom-call(bf16[4,6,8,4096]{3,2,1,0:T(8,128)(2,1)} %prolong.1, ...), custom_call_target="tpu_custom_call" | custom-call | tf_op jit(solution)/shard_map/halo/pallas_call | solution.py:142
  29.1 48.1 %coarse_rows.1 = bf16[32,464,128]{2,1,0:T(8,128)(2,1)} custom-call(s32[6,4,8]{2,1,0:T(4,128)} %bitcast.12, s32[7,6,4,8]{3,2,1,0:T(4,128)} %bitcast.11, s32[24]{0:T(128)} %owner.1, bf16[24,8,4096]{2,1,0:T(8,128)(2,1)} %bitcast.10, bf16[3,24,8,4096]{3,2,1,0:T(8,128)(2,1)} %bitcast.8, bf16[24,8,4096]{2,1,0:T(8,128)(2,1)} %bitcast.9, ...), custom_call_target="tpu_custom_call" | custom-call | tf_op jit(solution)/shard_map/coarse_rows/pallas_call | solution.py:449
  77.2 58.2 %all_to_all.5.taken = bf16[32,464,128]{2,1,0:T(8,128)(2,1)} all-to-all(bf16[32,464,128]{2,1,0:T(8,128)(2,1)} %coarse_rows.1), channel_id=1, replica_groups=mesh['gx'=2,'gy'=2,'gz'=32] {'gz'}, dimensions={0} | all-to-all | bytes 7602176 | tf_op jit(solution)/shard_map/all_to_all | solution.py:582
  135.5 8.6 %place_rows.1 = bf16[7,64,4096]{2,1,0:T(8,128)(2,1)} custom-call(bf16[32,464,128]{2,1,0:T(8,128)(2,1)} %all_to_all.5.taken), custom_call_target="tpu_custom_call" | custom-call | tf_op jit(solution)/shard_map/place_rows/pallas_call | solution.py:546

commit v5 on v4

--- a/solution.py
+++ b/solution.py
@@ -48,10 +48,66 @@
 MESH = pl.DeviceIdType.MESH
 
 
-def halo_kernel(
-    prolong, a_face,
+def couples(right, cell, stride, couple, blocks):
+    low = lane_low((64, 128))
+    zero = jnp.zeros((64, 128), BF16)
+    wide = jnp.zeros((128, 128), BF16)
+    columns = []
+    for k in range(2):
+        block = right[pl.ds(pl.multiple_of((cell + k * stride) * 64, 64), 64), :]
+        corner = jnp.concatenate([jnp.where(low, block, zero), jnp.where(low, zero, block)], axis=0)
+        columns.append(jnp.concatenate([corner, wide] if k == 0 else [wide, corner], axis=0))
+    weight = jnp.concatenate(columns, axis=1)
+    stack = [
+        jnp.concatenate([ref[pl.ds(pl.multiple_of(at, 32), 32), :] for at in ats], axis=1)
+        for _, ref, ats, _ in blocks
+    ]
+    stack = jnp.concatenate(stack, axis=0) if len(stack) > 1 else stack[0]
+    both = jnp.dot(stack, weight, preferred_element_type=F32)
+    for number, (f, _, _, cells) in enumerate(blocks):
+        for k in range(2):
+            part = both[number * 32 : number * 32 + 32, k * 128 : k * 128 + 128]
+            turned = pltpu.roll(part, 64, axis=1)
+            side = f % 2 * 64
+            for p in range(2):
+                value = (part if p == f % 2 else turned)[:, side : side + 64]
+                at = pl.multiple_of(cells[k] * 64 + p * 32, 32)
+                couple[pl.ds(at, 32), f * 64 : f * 64 + 64] = value.astype(BF16)
+
+
+def store_spread(line, dest, base, work):
+    spread(line, work)
+    for z in range(8):
+        at = pl.multiple_of(base + z * 32, 32)
+        dest[pl.ds(at, 32), :] = work[z * STEP : z * STEP + 32, :].astype(BF16)
+
+
+def store_right(right, base, work):
+    for z in range(8):
+        at = pl.multiple_of(base * 512 + z * 64, 64)
+        right[pl.ds(at, 64), :] = work[z * STEP_TWICE : z * STEP_TWICE + 64, :].astype(BF16)
+
+
+def store_left(left, base, work):
+    low = lane_low((64, 128))
+    zero = jnp.zeros((64, 128), F32)
+    for pair in range(4):
+        first, second = (work[z * STEP_TWICE : z * STEP_TWICE + 64, :] for z in (2 * pair, 2 * pair + 1))
+        block = jnp.concatenate([jnp.where(low, first, zero), jnp.where(low, zero, second)], axis=0)
+        at = pl.multiple_of(base * 512 + pair * 128, 128)
+        left[pl.ds(at, 128), :] = block.astype(BF16).T
+
+
+CELLS = LINES * BZ
+
+
+def inner_kernel(
+    prolong, a_face, a_diag,
     rim_x, rim_y, rim_z, p_xm, p_xp, p_ym, p_yp, p_zm, p_zp,
-    cells, faces, work, zero, zero_z, out_az, out_p_last, out_p_first, load_sems, send_sems, recv_sems, zero_sems,
+    couple_out, left_out, right_x, right_y, right_z, face_x, face_y, face_z,
+    in_p, in_d, in_f, zero, zero_z, out_az, out_p_last, out_p_first,
+    ra_d, ra_x, ra_y, ra_z, right, first_z, left, couple, work_a, work_b, work_c,
+    load_sems, send_sems, recv_sems, zero_sems, out_sems,
 ):
     depth = lax.axis_size("gz")
     gx, gy, gz = (lax.axis_index(axis) for axis in ("gx", "gy", "gz"))
@@ -60,8 +116,10 @@
     for target in ({"gx": 1 - gx}, {"gy": 1 - gy}, {"gz": next_z}, {"gz": previous_z}):
         pl.semaphore_signal(barrier, inc=1, device_id=target, device_id_type=MESH)
     loads = [
-        pltpu.make_async_copy(prolong, cells, load_sems.at[0]),
-        pltpu.make_async_copy(a_face.at[2], faces, load_sems.at[1]),
+        pltpu.make_async_copy(prolong, in_p, load_sems.at[0]),
+        pltpu.make_async_copy(a_face.at[2], in_f.at[2], load_sems.at[1]),
+        pltpu.make_async_copy(a_diag, in_d, load_sems.at[2]),
+        pltpu.make_async_copy(a_face.at[pl.ds(0, 2)], in_f.at[pl.ds(0, 2)], load_sems.at[3]),
     ]
     for load in loads:
         load.start()
@@ -100,8 +158,8 @@
 
     ends = []
     for number, axis, here, last, first, pairs in (
+        (3, "gy", gy, lambda ref: ref.at[:, BY - 1], lambda ref: ref.at[:, 0], (p_ym, p_yp, rim_y)),
         (0, "gx", gx, lambda ref: ref.at[BX - 1], lambda ref: ref.at[0], (p_xm, p_xp, rim_x)),
-        (3, "gy", gy, lambda ref: ref.at[:, BY - 1], lambda ref: ref.at[:, 0], (p_ym, p_yp, rim_y)),
     ):
         count = lax.axis_size(axis)
         up, down = {axis: lax.rem(here + 1, count)}, {axis: lax.rem(here + count - 1, count)}
@@ -112,18 +170,28 @@
             exchange(number + 1, first(prolong), pairs[1], down, before, after, blank),
             exchange(number + 2, last(a_face.at[number // 3]), pairs[2], up, after, before, blank),
         ]
-    for load in loads:
-        load.wait()
-
-    @pl.loop(0, LINES)
-    def _(line):
-        at = pl.ds(pl.multiple_of(line * 32, 32), 32)
-        x, y = line // BY, line % BY
-        spread(cells[x, y], work.at[0])
-        out_p_first[at, :] = work[0, 0:32, :].astype(BF16)
-        out_p_last[at, :] = work[0, 7 * STEP : 7 * STEP + 32, :].astype(BF16)
-        spread(faces[x, y], work.at[1])
-        out_az[at, :] = work[1, 7 * STEP : 7 * STEP + 32, :].astype(BF16)
+
+    loads[0].wait()
+    loads[1].wait()
+
+    @pl.loop(0, LINES // 2)
+    def _(half):
+        low = lane_low((32, 128))
+        for k in range(2):
+            line = half * 2 + k
+            x, y = line // BY, line % BY
+            at = pl.ds(pl.multiple_of(line * 32, 32), 32)
+            natural, by_parity, work = work_b.at[k], work_c.at[k], work_a.at[k]
+            spread_twice(in_p[x, y], natural, by_parity)
+            for z, dest in ((0, out_p_first), (BZ - 1, out_p_last)):
+                even, odd = (by_parity[z * STEP_TWICE + p * 32 : z * STEP_TWICE + p * 32 + 32, :] for p in range(2))
+                dest[at, :] = jnp.where(low, even, odd).astype(BF16)
+            store_spread(in_f[2, x, y], ra_z, line * 288 + 32, work)
+            out_az[at, :] = work[(BZ - 1) * STEP : (BZ - 1) * STEP + 32, :].astype(BF16)
+            ra_z[pl.ds(pl.multiple_of(line * 288, 32), 32), :] = jnp.zeros((32, 128), BF16)
+            store_right(right, line, natural)
+            first_z[pl.ds(pl.multiple_of(line * 64, 64), 64), :] = natural[0:64, :].astype(BF16)
+            store_left(left, line, by_parity)
 
     before, after = gz > 0, gz < depth - 1
     ends += [
@@ -131,69 +199,123 @@
         exchange(7, out_p_first, p_zp, {"gz": previous_z}, before, after, zero_z),
         exchange(8, out_az, rim_z, {"gz": next_z}, after, before, zero_z),
     ]
+    loads[2].wait()
+    loads[3].wait()
+
+    @pl.loop(0, LINES)
+    def _(line):
+        x, y = line // BY, line % BY
+        store_spread(in_d[x, y], ra_d, line * 256, work_a.at[0])
+        store_spread(in_f[0, x, y], ra_x, line * 256, work_a.at[1])
+        store_spread(in_f[1, x, y], ra_y, line * 256, work_a.at[2])
+
+    moves = []
+
+    def put(source, dest):
+        copy = pltpu.make_async_copy(source, dest, out_sems.at[len(moves)])
+        copy.start()
+        moves.append(copy)
+
+    put(left, left_out)
+    put(right.at[pl.ds(0, BY * 512)], right_x)
+    put(first_z, right_z)
+    put(ra_x.at[pl.ds((LINES - BY) * 256, BY * 256)], face_x)
+    put(out_az, face_z)
+    for x in range(BX):
+        put(right.at[pl.ds(x * BY * 512, 512)], right_y.at[pl.ds(x * 512, 512)])
+        put(ra_y.at[pl.ds((x * BY + BY - 1) * 256, 256)], face_y.at[pl.ds(x * 256, 256)])
+
+    for x in range(BX):
+
+        @pl.loop(0, BY)
+        def _(y):
+            line = x * BY + y
+            from_y = jnp.where(y > 0, line - 1, line)
+            into_y = jnp.where(y > 0, (line - 1) * BZ, CELLS)
+            for z in range(0, BZ, 2):
+                n = line * BZ + z
+                both = range(2)
+                blocks = [
+                    (0, ra_d, [(n + k) * 32 for k in both], [n, n + 1]),
+                    (2, ra_y, [from_y * 256 + (z + k) * 32 for k in both], [into_y + z, into_y + z + 1]),
+                    (3, ra_z, [line * 288 + (z + k) * 32 for k in both], [CELLS if z == 0 else n - 1, n]),
+                ]
+                if x > 0:
+                    e = n - BY * BZ
+                    blocks.append((1, ra_x, [(e + k) * 32 for k in both], [e, e + 1]))
+                couples(right, n, 1, couple, blocks)
+
+        if x > 0:
+            rows = pl.ds((x - 1) * BY * BZ * 64, BY * BZ * 64)
+            put(couple.at[rows], couple_out.at[rows])
+    rows = pl.ds((BX - 1) * BY * BZ * 64, BY * BZ * 64)
+    put(couple.at[rows], couple_out.at[rows])
     for finish in ends:
         finish()
-
-
-def halo(prolong, a_face):
+    for copy in moves:
+        copy.wait()
+
+
+def inner(prolong, a_face, a_diag):
     any_space = pl.BlockSpec(memory_space=pl.ANY)
     x_face, y_face, z_face = (BY, BZ, NODES * NODES), (BX, BZ, NODES * NODES), (LINES * 32, 128)
-    shapes = (x_face, y_face, z_face, x_face, x_face, y_face, y_face, z_face, z_face)
+    shapes = (
+        x_face, y_face, z_face, x_face, x_face, y_face, y_face, z_face, z_face,
+        (CELLS * 64, 256), (CELLS * 64, 128),
+        (BY * 512, 128), (BX * 512, 128), (LINES * 64, 128),
+        (BY * 256, 128), (BX * 256, 128), z_face,
+    )
     return pl.pallas_call(
-        halo_kernel,
+        inner_kernel,
         out_shape=[jax.ShapeDtypeStruct(shape, BF16) for shape in shapes],
-        in_specs=[any_space] * 2,
+        in_specs=[any_space] * 3,
         out_specs=[any_space] * len(shapes),
         scratch_shapes=[
             pltpu.VMEM(prolong.shape, BF16),
-            pltpu.VMEM(prolong.shape, BF16),
-            pltpu.VMEM((2, 8 * STEP, 128), F32),
+            pltpu.VMEM(a_diag.shape, BF16),
+            pltpu.VMEM(a_face.shape, BF16),
             pltpu.VMEM(x_face, BF16),
             pltpu.VMEM(z_face, BF16),
             pltpu.VMEM(z_face, BF16),
             pltpu.VMEM(z_face, BF16),
             pltpu.VMEM(z_face, BF16),
-            pltpu.SemaphoreType.DMA((2,)),
+            pltpu.VMEM((LINES * 256, 128), BF16),
+            pltpu.VMEM((LINES * 256, 128), BF16),
+            pltpu.VMEM((LINES * 256, 128), BF16),
+            pltpu.VMEM((LINES * 288, 128), BF16),
+            pltpu.VMEM((CELLS * 64, 128), BF16),
+            pltpu.VMEM((LINES * 64, 128), BF16),
+            pltpu.VMEM((CELLS * 64, 128), BF16),
+            pltpu.VMEM(((CELLS + BZ) * 64, 256), BF16),
+            pltpu.VMEM((3, 8 * STEP, 128), F32),
+            pltpu.VMEM((2, 8 * STEP_TWICE, 128), F32),
+            pltpu.VMEM((2, 8 * STEP_TWICE, 128), F32),
+            pltpu.SemaphoreType.DMA((4,)),
             pltpu.SemaphoreType.DMA((9,)),
             pltpu.SemaphoreType.DMA((9,)),
             pltpu.SemaphoreType.DMA((9,)),
+            pltpu.SemaphoreType.DMA((5 + 3 * BX,)),
         ],
         compiler_params=pltpu.CompilerParams(collective_id=0, has_side_effects=True, vmem_limit_bytes=63 << 20),
-        name="halo",
-    )(prolong, a_face)
+        name="inner",
+    )(prolong, a_face, a_diag)
 
 
 def compute_kernel(
     aggregate, slot, owner,
-    a_diag, a_face, prolong, rim_x, rim_y, rim_z,
-    p_xm, p_xp, p_ym, p_yp, p_zm, p_zp,
-    send, keys, key_work, key_sem,
-    ra_d, ra_x, ra_y, ra_z, right, left, couple, work_a, work_b, work_c,
+    rim_x, rim_y, rim_z, p_xm, p_xp, p_ym, p_yp, p_zm, p_zp,
+    couple_in, left_in, right_x, right_y, right_z, face_x, face_y, face_z,
+    send, keys, key_work, key_sem, in_sems, edge, right, left, couple, work_a, work_b, work_c,
     acc_f, acc_b, rows, counts, tally, sems, count_sem,
 ):
-    def store_spread(line, dest, base, bench):
-        work = work_a.at[bench]
-        spread(line, work)
-        for z in range(8):
-            at = pl.multiple_of(base + z * 32, 32)
-            dest[pl.ds(at, 32), :] = work[z * STEP : z * STEP + 32, :].astype(BF16)
-
-    right_xp, right_yp, right_zp = LINES, LINES + BY, LINES + BY + BX
-    left_xm, left_ym, left_zm = LINES, LINES + BY, LINES + BY + BX
-
-    def store_right(base, work):
-        for z in range(8):
-            at = pl.multiple_of(base * 512 + z * 64, 64)
-            right[pl.ds(at, 64), :] = work[z * STEP_TWICE : z * STEP_TWICE + 64, :].astype(BF16)
-
-    def store_left(base, work):
-        low = lane_low((64, 128))
-        zero = jnp.zeros((64, 128), F32)
-        for pair in range(4):
-            first, second = (work[z * STEP_TWICE : z * STEP_TWICE + 64, :] for z in (2 * pair, 2 * pair + 1))
-            block = jnp.concatenate([jnp.where(low, first, zero), jnp.where(low, zero, second)], axis=0)
-            at = pl.multiple_of(base * 512 + pair * 128, 128)
-            left[pl.ds(at, 128), :] = block.astype(BF16).T
+    plane = BY * BZ * 64
+    brought = []
+    for x in range(BX):
+        at = pl.ds(x * plane, plane)
+        for k, (source, dest) in enumerate(((couple_in, couple), (left_in, left))):
+            copy = pltpu.make_async_copy(source.at[at], dest.at[at], in_sems.at[x, k])
+            copy.start()
+            brought.append(copy)
 
     key_work[...] = aggregate[...][None] * SLOTS + slot[...]
     told_keys = pltpu.make_async_copy(key_work, keys, key_sem)
@@ -201,38 +323,24 @@
     acc_f[...] = jnp.zeros_like(acc_f)
     acc_b[...] = jnp.zeros_like(acc_b)
 
-    @pl.loop(0, LINES // 2)
-    def _(half):
-        for k in range(2):
-            line = half * 2 + k
-            natural, by_parity = work_b.at[k], work_c.at[k]
-            spread_twice(prolong[line], natural, by_parity)
-            store_right(line, natural)
-            store_left(line, by_parity)
-            store_spread(a_diag[line], ra_d, line * 256, 0)
-            store_spread(a_face[0, line], ra_x, (line + BY) * 256, 1)
-            store_spread(a_face[1, line], ra_y, (line + line // BY + 1) * 256, 2)
-            store_spread(a_face[2, line], ra_z, line * 288 + 32, 3)
-
-    @pl.loop(0, BY // 2)
-    def _(half):
-        for k in range(2):
-            line = half * 2 + k
-            store_spread(rim_x[line], ra_x, line * 256, k)
-            spread_twice(p_xm[line], None, work_c.at[k])
-            store_left(left_xm + line, work_c.at[k])
-            spread_twice(p_xp[line], work_b.at[k], None)
-            store_right(right_xp + line, work_b.at[k])
-
-    @pl.loop(0, BX // 2)
-    def _(half):
-        for k in range(2):
-            line = half * 2 + k
-            store_spread(rim_y[line], ra_y, line * (BY + 1) * 256, k)
-            spread_twice(p_ym[line], None, work_c.at[k])
-            store_left(left_ym + line, work_c.at[k])
-            spread_twice(p_yp[line], work_b.at[k], None)
-            store_right(right_yp + line, work_b.at[k])
+    right_xp, right_yp, right_zp = 0, BY, BY + BX
+    left_xm, left_ym, left_zm = LINES, LINES + BY, LINES + BY + BX
+    cells_xm, cells_ym, cells_zm = left_xm * 8, left_ym * 8, left_zm * 8
+
+    for count, rim, before, after, near, base in (
+        (BY, rim_x, p_xm, p_xp, left_xm, right_xp),
+        (BX, rim_y, p_ym, p_yp, left_ym, right_yp),
+    ):
+
+        @pl.loop(0, count // 2)
+        def _(half):
+            for k in range(2):
+                line = half * 2 + k
+                store_spread(rim[line], edge, (base + line) * 256, work_a.at[k])
+                spread_twice(before[line], None, work_c.at[k])
+                store_left(left, near + line, work_c.at[k])
+                spread_twice(after[line], work_b.at[k], None)
+                store_right(right, base + line, work_b.at[k])
 
     @pl.loop(0, LINES // 2)
     def _(half):
@@ -241,7 +349,6 @@
         for k in range(2):
             line = half * 2 + k
             at = pl.ds(pl.multiple_of(line * 32, 32), 32)
-            ra_z[pl.ds(pl.multiple_of(line * 288, 32), 32), :] = rim_z[at, :]
             here = p_zp[at, :].astype(F32)
             turned = pltpu.roll(here, 64, axis=1)
             work = work_b.at[k]
@@ -259,31 +366,43 @@
         block = jnp.concatenate(blocks, axis=0).astype(BF16)
         left[pl.ds(pl.multiple_of((left_zm * 8 + half * 2) * 64, 128), 128), :] = block.T
 
-    def couples(cell, blocks):
-        low = lane_low((64, 128))
-        zero = jnp.zeros((64, 128), BF16)
-        wide = jnp.zeros((128, 128), BF16)
-        columns = []
-        for k in range(2):
-            block = right[pl.ds(pl.multiple_of((cell + k) * 64, 64), 64), :]
-            corner = jnp.concatenate([jnp.where(low, block, zero), jnp.where(low, zero, block)], axis=0)
-            columns.append(jnp.concatenate([corner, wide] if k == 0 else [wide, corner], axis=0))
-        weight = jnp.concatenate(columns, axis=1)
-        stack = [
-            jnp.concatenate([ref[pl.ds(pl.multiple_of(at, 32), 32), :] for at in ats], axis=1)
-            for _, ref, ats, _ in blocks
-        ]
-        stack = jnp.concatenate(stack, axis=0) if len(stack) > 1 else stack[0]
-        both = jnp.dot(stack, weight, preferred_element_type=F32)
-        for number, (f, _, _, cells) in enumerate(blocks):
-            for k in range(2):
-                part = both[number * 32 : number * 32 + 32, k * 128 : k * 128 + 128]
-                turned = pltpu.roll(part, 64, axis=1)
-                side = f % 2 * 64
-                for p in range(2):
-                    value = (part if p == f % 2 else turned)[:, side : side + 64]
-                    at = pl.multiple_of(cells[k] * 64 + p * 32, 32)
-                    couple[pl.ds(at, 32), f * 64 : f * 64 + 64] = value.astype(BF16)
+    for count, f, base, beyond, weights in ((BY, 1, right_xp, cells_xm, right_x), (BX, 2, right_yp, cells_ym, right_y)):
+
+        @pl.loop(0, count)
+        def _(line):
+            for z in range(0, BZ, 2):
+                at = (base + line) * 256 + z * 32
+                e = beyond + line * BZ + z
+                couples(weights, line * BZ + z, 1, couple, [(f, edge, [at, at + 32], [e, e + 1])])
+
+    @pl.loop(0, LINES // 2)
+    def _(half):
+        line = half * 2
+        e = cells_zm + line
+        couples(right_z, line, 1, couple, [(3, rim_z, [line * 32, line * 32 + 32], [e, e + 1])])
+
+    for copy in brought:
+        copy.wait()
+
+    @pl.loop(0, BY)
+    def _(y):
+        for z in range(0, BZ, 2):
+            e = ((BX - 1) * BY + y) * BZ + z
+            at = y * 256 + z * 32
+            couples(right, (right_xp + y) * 8 + z, 1, couple, [(1, face_x, [at, at + 32], [e, e + 1])])
+
+    @pl.loop(0, BX)
+    def _(x):
+        for z in range(0, BZ, 2):
+            e = (x * BY + BY - 1) * BZ + z
+            at = x * 256 + z * 32
+            couples(right, (right_yp + x) * 8 + z, 1, couple, [(2, face_y, [at, at + 32], [e, e + 1])])
+
+    @pl.loop(0, LINES // 2)
+    def _(half):
+        line = half * 2
+        e = line * BZ + BZ - 1
+        couples(right, right_zp * 8 + line, 1, couple, [(3, face_z, [line * 32, line * 32 + 32], [e, e + BZ])])
 
     def add(ref, at, low_side, value):
         low = lane_low((64, 128))
@@ -307,56 +426,7 @@
                 if key_b is not None:
                     add(acc_b, key_b, f % 2 == 0, term)
 
-    cells_xm, cells_ym, cells_zm = left_xm * 8, left_ym * 8, left_zm * 8
     told_keys.wait()
-
-    @pl.loop(0, LINES)
-    def _(line):
-        x, y = line // BY, line % BY
-        into_x = jnp.where(x > 0, (line - BY) * 8, cells_xm + y * 8)
-        into_y = jnp.where(y > 0, (line - 1) * 8, cells_ym + x * 8)
-        for z in range(0, BZ, 2):
-            n = line * BZ + z
-            couples(
-                n,
-                [
-                    (0, ra_d, [(n + k) * 32 for k in range(2)], [n, n + 1]),
-                    (1, ra_x, [(n + k) * 32 for k in range(2)], [into_x + z, into_x + z + 1]),
-                    (
-                        2,
-                        ra_y,
-                        [(line + x) * 256 + (z + k) * 32 for k in range(2)],
-                        [into_y + z, into_y + z + 1],
-                    ),
-                    (
-                        3,
-                        ra_z,
-                        [line * 288 + (z + k) * 32 for k in range(2)],
-                        [cells_zm + line if z == 0 else n - 1, n],
-                    ),
-                ],
-            )
-
-    @pl.loop(0, BY)
-    def _(y):
-        for z in range(0, BZ, 2):
-            e = ((BX - 1) * BY + y) * BZ + z
-            at = (BX * BY + y) * 256 + z * 32
-            couples((right_xp + y) * 8 + z, [(1, ra_x, [at, at + 32], [e, e + 1])])
-
-    @pl.loop(0, BX)
-    def _(x):
-        for z in range(0, BZ, 2):
-            e = (x * BY + BY - 1) * BZ + z
-            at = (x * (BY + 1) + BY) * 256 + z * 32
-            couples((right_yp + x) * 8 + z, [(2, ra_y, [at, at + 32], [e, e + 1])])
-
-    @pl.loop(0, LINES // 2)
-    def _(half):
-        line = half * 2
-        e = line * BZ + BZ - 1
-        at = line * 288 + BZ * 32
-        couples(right_zp * 8 + line, [(3, ra_z, [at, at + 288], [e, e + BZ])])
 
     @pl.loop(0, LINES)
     def _(line):
@@ -445,24 +515,23 @@
 def coarse_rows(aggregate, slot, owner, arrays, depth):
     smem = pl.BlockSpec(memory_space=pltpu.SMEM)
     vmem = pl.BlockSpec(memory_space=pltpu.VMEM)
-    lines_right = LINES + BY + BX + LINES // 8
+    any_space = pl.BlockSpec(memory_space=pl.ANY)
+    beyond = BY + BX + LINES // 8
     return pl.pallas_call(
         compute_kernel,
         out_shape=jax.ShapeDtypeStruct((depth, PACK, 128), BF16),
-        in_specs=[vmem, vmem, smem] + [vmem] * len(arrays),
-        out_specs=pl.BlockSpec(memory_space=pl.ANY),
+        in_specs=[vmem, vmem, smem] + [vmem] * 9 + [any_space] * 2 + [vmem] * 6,
+        out_specs=any_space,
         scratch_shapes=[
             pltpu.SMEM((SLOTS, BY, BX, BZ), jnp.int32),
             pltpu.VMEM((SLOTS, BY, BX, BZ), jnp.int32),
             pltpu.SemaphoreType.DMA,
-            pltpu.VMEM((LINES * 256, 128), BF16),
-            pltpu.VMEM(((LINES + BY) * 256, 128), BF16),
-            pltpu.VMEM((BX * (BY + 1) * 256, 128), BF16),
-            pltpu.VMEM((LINES * 288, 128), BF16),
-            pltpu.VMEM((lines_right * 512, 128), BF16),
-            pltpu.VMEM((lines_right * 512, 128), BF16),
-            pltpu.VMEM((lines_right * 512, 256), BF16),
-            pltpu.VMEM((4, 8 * STEP, 128), F32),
+            pltpu.SemaphoreType.DMA((BX, 2)),
+            pltpu.VMEM(((BY + BX) * 256, 128), BF16),
+            pltpu.VMEM((beyond * 512, 128), BF16),
+            pltpu.VMEM(((LINES + beyond) * 512, 128), BF16),
+            pltpu.VMEM(((LINES + beyond) * 512, 256), BF16),
+            pltpu.VMEM((2, 8 * STEP, 128), F32),
             pltpu.VMEM((2, 8 * STEP_TWICE, 128), F32),
             pltpu.VMEM((2, 8 * STEP_TWICE, 128), F32),
             pltpu.VMEM((KEYS + 1, 64, 128), F32),
@@ -570,12 +639,7 @@
     depth = lax.axis_size("gz")
     holding = PLACES * depth
 
-    arrays = [
-        a_diag.reshape(LINES, BZ, block),
-        a_face.reshape(3, LINES, BZ, block),
-        prolong.reshape(LINES, BZ, block),
-        *halo(prolong, a_face),
-    ]
+    arrays = inner(prolong, a_face, a_diag)
     send = coarse_rows(
         aggregate.transpose(1, 0, 2), pair_slot.transpose(0, 2, 1, 3), row_owner, arrays, depth
     )

time: 144 us -> 136 us (0.944)
  Pallas kernels: 85.8 us -> 77 us
    pallas_call x1, Pallas kernels: 48.1 us -> 39.2 us  [coarse_rows(): pl.pallas_call(compute_kernel, out_shape=jax.ShapeDtypeStruct((depth, PAC...]
where the time goes in v5:
time: 136 us; the launch traced here: 135 us
  Pallas kernels  77 us (57%)
  blocking collectives  58.2 us (43%)
    all_to_all x1, blocking collectives, shards(): taken = lax.all_to_all(send, 'gz', 0, 0, tiled=True)  58.2 us
    pallas_call x1, Pallas kernels, coarse_rows(): pl.pallas_call(compute_kernel, out_shape=jax.ShapeDtypeStruct((depth, PAC...  39.2 us
    pallas_call x1, Pallas kernels, inner(): pl.pallas_call(inner_kernel, out_shape=[jax.ShapeDtypeStruct(shape, BF16)...  29.3 us
    pallas_call x1, Pallas kernels, place_rows(): pl.pallas_call(place_kernel, out_shape=jax.ShapeDtypeStruct((SLOTS, count...  8.48 us

profile of v5, /device:TPU:0, one launch (start us, length us, event | category | flops | bytes accessed | tf_op | source)
XLA Modules:
  0.0 135.3 jit_solution(6771030989323332997)
XLA Ops:
  0.0 29.3 %inner.1 = (bf16[6,8,4096]{2,1,0:T(8,128)(2,1)}, bf16[4,8,4096]{2,1,0:T(8,128)(2,1)}, bf16[768,128]{1,0:T(8,128)(2,1)}, bf16[6,8,4096]{2,1,0:T(8,128)(2,1)}, bf1...) custom-call(bf16[4,6,8,4096]{3,2,1,0:T(8,128)(2,1)} %prolong.1, ...), custom_call_target="tpu_custom_call" | custom-call | tf_op jit(solution)/shard_map/inner/pallas_call | solution.py:268
  29.3 39.2 %coarse_rows.1 = bf16[32,464,128]{2,1,0:T(8,128)(2,1)} custom-call(s32[6,4,8]{2,1,0:T(4,128)} %bitcast.6, s32[7,6,4,8]{3,2,1,0:T(4,128)} %bitcast.5, s32[24]{0:T(128)} %owner.1, bf16[6,8,4096]{2,1,0:T(8,128)(2,1)} %get-tuple-element.22.rim_x, bf16[4,8,4096]{2,1,0:T(8,128)(2,1)} %get-tuple-element.23.rim_y, bf16[768,128]{1,0:T(8,128)(2,1)} %get-tuple-element.24.rim_z, ...), custom_call_target="tpu_custom_call" | custom-call | tf_op jit(solution)/shard_map/coarse_rows/pallas_call | solution.py:520
  68.6 58.2 %all_to_all.5.taken = bf16[32,464,128]{2,1,0:T(8,128)(2,1)} all-to-all(bf16[32,464,128]{2,1,0:T(8,128)(2,1)} %coarse_rows.1), channel_id=1, replica_groups=mesh['gx'=2,'gy'=2,'gz'=32] {'gz'}, dimensions={0} | all-to-all | bytes 7602176 | tf_op jit(solution)/shard_map/all_to_all | solution.py:646
  126.8 8.5 %place_rows.1 = bf16[7,64,4096]{2,1,0:T(8,128)(2,1)} custom-call(bf16[32,464,128]{2,1,0:T(8,128)(2,1)} %all_to_all.5.taken), custom_call_target="tpu_custom_call" | custom-call | tf_op jit(solution)/shard_map/place_rows/pallas_call | solution.py:615

commit v6 on v5

--- a/solution.py
+++ b/solution.py
@@ -12,7 +12,7 @@
 LINES = BX * BY
 PLACES = 2
 ROW = SLOTS * NODES * NODES // 128
-PACK = PLACES * ROW + 16
+PACK = PLACES * ROW
 KEYS = AGG_DEV * SLOTS
 STEP, STEP_TWICE = 36, 68
 F32 = jnp.float32
@@ -103,9 +103,9 @@
 
 def inner_kernel(
     prolong, a_face, a_diag,
-    rim_x, rim_y, rim_z, p_xm, p_xp, p_ym, p_yp, p_zm, p_zp,
+    m_x, m_y, m_z, p_xp, p_yp, p_zp,
     couple_out, left_out, right_x, right_y, right_z, face_x, face_y, face_z,
-    in_p, in_d, in_f, zero, zero_z, out_az, out_p_last, out_p_first,
+    in_p, in_d, in_f, zero, zero_m, out_mx, out_my, out_mz, out_az, out_p_first,
     ra_d, ra_x, ra_y, ra_z, right, first_z, left, couple, work_a, work_b, work_c,
     load_sems, send_sems, recv_sems, zero_sems, out_sems,
 ):
@@ -115,16 +115,20 @@
     barrier = pltpu.get_barrier_semaphore()
     for target in ({"gx": 1 - gx}, {"gy": 1 - gy}, {"gz": next_z}, {"gz": previous_z}):
         pl.semaphore_signal(barrier, inc=1, device_id=target, device_id_type=MESH)
-    loads = [
-        pltpu.make_async_copy(prolong, in_p, load_sems.at[0]),
-        pltpu.make_async_copy(a_face.at[2], in_f.at[2], load_sems.at[1]),
-        pltpu.make_async_copy(a_diag, in_d, load_sems.at[2]),
-        pltpu.make_async_copy(a_face.at[pl.ds(0, 2)], in_f.at[pl.ds(0, 2)], load_sems.at[3]),
-    ]
+    last_x, inner_x = pl.ds(BX - 1, 1), pl.ds(0, BX - 1)
+    load_parts = (
+        (prolong, in_p),
+        (a_face.at[0, last_x], in_f.at[0, last_x]),
+        (a_face.at[1], in_f.at[1]),
+        (a_face.at[2], in_f.at[2]),
+        (a_diag, in_d),
+        (a_face.at[0, inner_x], in_f.at[0, inner_x]),
+    )
+    loads = [pltpu.make_async_copy(*part, load_sems.at[k]) for k, part in enumerate(load_parts)]
     for load in loads:
         load.start()
     zero[...] = jnp.zeros_like(zero)
-    zero_z[...] = jnp.zeros_like(zero_z)
+    zero_m[...] = jnp.zeros_like(zero_m)
     pl.semaphore_wait(barrier, 4)
 
     def exchange(number, source, dest, target, sends, receives, blank):
@@ -156,23 +160,25 @@
 
         return finish
 
-    ends = []
-    for number, axis, here, last, first, pairs in (
-        (3, "gy", gy, lambda ref: ref.at[:, BY - 1], lambda ref: ref.at[:, 0], (p_ym, p_yp, rim_y)),
-        (0, "gx", gx, lambda ref: ref.at[BX - 1], lambda ref: ref.at[0], (p_xm, p_xp, rim_x)),
-    ):
-        count = lax.axis_size(axis)
-        up, down = {axis: lax.rem(here + 1, count)}, {axis: lax.rem(here + count - 1, count)}
-        before, after = here > 0, here < count - 1
-        blank = zero.at[pl.ds(0, pairs[0].shape[0])]
-        ends += [
-            exchange(number, last(prolong), pairs[0], up, after, before, blank),
-            exchange(number + 1, first(prolong), pairs[1], down, before, after, blank),
-            exchange(number + 2, last(a_face.at[number // 3]), pairs[2], up, after, before, blank),
-        ]
-
+    def to_line(axis, step):
+        here, count = lax.axis_index(axis), lax.axis_size(axis)
+        return {axis: lax.rem(here + (step + count), count)}
+
+    def has_line(axis, step):
+        here, count = lax.axis_index(axis), lax.axis_size(axis)
+        return here > 0 if step < 0 else here < count - 1
+
+    def pass_up(number, axis, source, dest, blank):
+        return exchange(number, source, dest, to_line(axis, 1), has_line(axis, 1), has_line(axis, -1), blank)
+
+    def pass_down(number, axis, source, dest, blank):
+        return exchange(number, source, dest, to_line(axis, -1), has_line(axis, -1), has_line(axis, 1), blank)
+
+    ends = [
+        pass_down(0, "gy", prolong.at[:, 0], p_yp, zero.at[pl.ds(0, BX)]),
+        pass_down(1, "gx", prolong.at[0], p_xp, zero),
+    ]
     loads[0].wait()
-    loads[1].wait()
 
     @pl.loop(0, LINES // 2)
     def _(half):
@@ -181,33 +187,82 @@
             line = half * 2 + k
             x, y = line // BY, line % BY
             at = pl.ds(pl.multiple_of(line * 32, 32), 32)
-            natural, by_parity, work = work_b.at[k], work_c.at[k], work_a.at[k]
+            natural, by_parity = work_b.at[k], work_c.at[k]
             spread_twice(in_p[x, y], natural, by_parity)
-            for z, dest in ((0, out_p_first), (BZ - 1, out_p_last)):
-                even, odd = (by_parity[z * STEP_TWICE + p * 32 : z * STEP_TWICE + p * 32 + 32, :] for p in range(2))
-                dest[at, :] = jnp.where(low, even, odd).astype(BF16)
-            store_spread(in_f[2, x, y], ra_z, line * 288 + 32, work)
-            out_az[at, :] = work[(BZ - 1) * STEP : (BZ - 1) * STEP + 32, :].astype(BF16)
+            even, odd = by_parity[0:32, :], by_parity[32:64, :]
+            out_p_first[at, :] = jnp.where(low, even, odd).astype(BF16)
             ra_z[pl.ds(pl.multiple_of(line * 288, 32), 32), :] = jnp.zeros((32, 128), BF16)
             store_right(right, line, natural)
             first_z[pl.ds(pl.multiple_of(line * 64, 64), 64), :] = natural[0:64, :].astype(BF16)
             store_left(left, line, by_parity)
 
-    before, after = gz > 0, gz < depth - 1
-    ends += [
-        exchange(6, out_p_last, p_zm, {"gz": next_z}, after, before, zero_z),
-        exchange(7, out_p_first, p_zp, {"gz": previous_z}, before, after, zero_z),
-        exchange(8, out_az, rim_z, {"gz": next_z}, after, before, zero_z),
-    ]
+    ends.append(pass_down(2, "gz", out_p_first, p_zp, zero_m.at[pl.ds(0, LINES * 32)]))
+    loads[1].wait()
     loads[2].wait()
     loads[3].wait()
 
-    @pl.loop(0, LINES)
-    def _(line):
-        x, y = line // BY, line % BY
-        store_spread(in_d[x, y], ra_d, line * 256, work_a.at[0])
-        store_spread(in_f[0, x, y], ra_x, line * 256, work_a.at[1])
-        store_spread(in_f[1, x, y], ra_y, line * 256, work_a.at[2])
+    def outgoing(work, pair, line):
+        blocks = []
+        for z in (2 * pair, 2 * pair + 1):
+            block = work[z * STEP : z * STEP + 32, :]
+            blocks += [block, pltpu.roll(block, 64, axis=1)]
+        block = jnp.concatenate(blocks, axis=0).astype(BF16)
+        at = pl.multiple_of(line * 512 + pair * 128, 128)
+        return jnp.dot(left[pl.ds(at, 128), :], block, preferred_element_type=F32)
+
+    def side_by_side(first, second):
+        return jnp.where(lane_low((64, 128)), first, pltpu.roll(second, 64, axis=1)).astype(BF16)
+
+    for f, count, out, line_of in (
+        (0, BY, out_mx, lambda k: (BX - 1) * BY + k),
+        (1, BX, out_my, lambda k: k * BY + BY - 1),
+    ):
+
+        @pl.loop(0, count // 2)
+        def _(half):
+            for k in range(2):
+                row = half * 2 + k
+                line = line_of(row)
+                work = work_a.at[k]
+                store_spread(in_f[f, line // BY, line % BY], (ra_x, ra_y)[f], line * 256, work)
+                for pair in range(4):
+                    both = outgoing(work, pair, line)
+                    at = pl.multiple_of(row * 256 + pair * 64, 64)
+                    out[pl.ds(at, 64), :] = side_by_side(both[0:64], both[64:128])
+
+    @pl.loop(0, LINES // 2)
+    def _(half):
+        last = []
+        for k in range(2):
+            line = half * 2 + k
+            work = work_a.at[k]
+            store_spread(in_f[2, line // BY, line % BY], ra_z, line * 288 + 32, work)
+            at = pl.ds(pl.multiple_of(line * 32, 32), 32)
+            out_az[at, :] = work[(BZ - 1) * STEP : (BZ - 1) * STEP + 32, :].astype(BF16)
+            last.append(outgoing(work, BZ // 2 - 1, line)[64:128])
+        out_mz[pl.ds(pl.multiple_of(half * 64, 64), 64), :] = side_by_side(*last)
+
+    for number, axis, source, dest in ((3, "gy", out_my, m_y), (4, "gz", out_mz, m_z), (5, "gx", out_mx, m_x)):
+        ends.append(pass_up(number, axis, source, dest, zero_m.at[pl.ds(0, source.shape[0])]))
+    loads[4].wait()
+    loads[5].wait()
+
+    @pl.loop(0, LINES // 2)
+    def _(half):
+        for k in range(2):
+            line = half * 2 + k
+            store_spread(in_d[line // BY, line % BY], ra_d, line * 256, work_a.at[k])
+
+    @pl.loop(0, (LINES - BY) // 2)
+    def _(half):
+        for k in range(2):
+            line = half * 2 + k
+            store_spread(in_f[0, line // BY, line % BY], ra_x, line * 256, work_a.at[k])
+
+    @pl.loop(0, BX)
+    def _(x):
+        for y in range(BY - 1):
+            store_spread(in_f[1, x, y], ra_y, (x * BY + y) * 256, work_a.at[y % 3])
 
     moves = []
 
@@ -260,7 +315,7 @@
     any_space = pl.BlockSpec(memory_space=pl.ANY)
     x_face, y_face, z_face = (BY, BZ, NODES * NODES), (BX, BZ, NODES * NODES), (LINES * 32, 128)
     shapes = (
-        x_face, y_face, z_face, x_face, x_face, y_face, y_face, z_face, z_face,
+        (BY * 256, 128), (BX * 256, 128), (LINES * 32, 128), x_face, y_face, z_face,
         (CELLS * 64, 256), (CELLS * 64, 128),
         (BY * 512, 128), (BX * 512, 128), (LINES * 64, 128),
         (BY * 256, 128), (BX * 256, 128), z_face,
@@ -275,8 +330,10 @@
             pltpu.VMEM(a_diag.shape, BF16),
             pltpu.VMEM(a_face.shape, BF16),
             pltpu.VMEM(x_face, BF16),
-            pltpu.VMEM(z_face, BF16),
-            pltpu.VMEM(z_face, BF16),
+            pltpu.VMEM((BY * 256, 128), BF16),
+            pltpu.VMEM((BY * 256, 128), BF16),
+            pltpu.VMEM((BX * 256, 128), BF16),
+            pltpu.VMEM((LINES * 32, 128), BF16),
             pltpu.VMEM(z_face, BF16),
             pltpu.VMEM(z_face, BF16),
             pltpu.VMEM((LINES * 256, 128), BF16),
@@ -290,10 +347,10 @@
             pltpu.VMEM((3, 8 * STEP, 128), F32),
             pltpu.VMEM((2, 8 * STEP_TWICE, 128), F32),
             pltpu.VMEM((2, 8 * STEP_TWICE, 128), F32),
-            pltpu.SemaphoreType.DMA((4,)),
-            pltpu.SemaphoreType.DMA((9,)),
-            pltpu.SemaphoreType.DMA((9,)),
-            pltpu.SemaphoreType.DMA((9,)),
+            pltpu.SemaphoreType.DMA((6,)),
+            pltpu.SemaphoreType.DMA((6,)),
+            pltpu.SemaphoreType.DMA((6,)),
+            pltpu.SemaphoreType.DMA((6,)),
             pltpu.SemaphoreType.DMA((5 + 3 * BX,)),
         ],
         compiler_params=pltpu.CompilerParams(collective_id=0, has_side_effects=True, vmem_limit_bytes=63 << 20),
@@ -303,10 +360,10 @@
 
 def compute_kernel(
     aggregate, slot, owner,
-    rim_x, rim_y, rim_z, p_xm, p_xp, p_ym, p_yp, p_zm, p_zp,
+    m_x, m_y, m_z, p_xp, p_yp, p_zp,
     couple_in, left_in, right_x, right_y, right_z, face_x, face_y, face_z,
-    send, keys, key_work, key_sem, in_sems, edge, right, left, couple, work_a, work_b, work_c,
-    acc_f, acc_b, rows, counts, tally, sems, count_sem,
+    send, keys, key_work, key_sem, in_sems, right, left, couple, work_b,
+    acc_f, acc_b, rows, absent, tally, sems, absent_sems,
 ):
     plane = BY * BZ * 64
     brought = []
@@ -317,6 +374,13 @@
             copy.start()
             brought.append(copy)
 
+    absent[...] = jnp.full(absent.shape, jnp.nan, BF16)
+    marks = []
+    for k in range(PLACES):
+        mark = pltpu.make_async_copy(absent, send.at[:, pl.ds(k * ROW, 16)], absent_sems.at[k])
+        mark.start()
+        marks.append(mark)
+
     key_work[...] = aggregate[...][None] * SLOTS + slot[...]
     told_keys = pltpu.make_async_copy(key_work, keys, key_sem)
     told_keys.start()
@@ -324,62 +388,60 @@
     acc_b[...] = jnp.zeros_like(acc_b)
 
     right_xp, right_yp, right_zp = 0, BY, BY + BX
-    left_xm, left_ym, left_zm = LINES, LINES + BY, LINES + BY + BX
-    cells_xm, cells_ym, cells_zm = left_xm * 8, left_ym * 8, left_zm * 8
-
-    for count, rim, before, after, near, base in (
-        (BY, rim_x, p_xm, p_xp, left_xm, right_xp),
-        (BX, rim_y, p_ym, p_yp, left_ym, right_yp),
-    ):
+
+    for count, after, base in ((BY, p_xp, right_xp), (BX, p_yp, right_yp)):
 
         @pl.loop(0, count // 2)
         def _(half):
             for k in range(2):
                 line = half * 2 + k
-                store_spread(rim[line], edge, (base + line) * 256, work_a.at[k])
-                spread_twice(before[line], None, work_c.at[k])
-                store_left(left, near + line, work_c.at[k])
                 spread_twice(after[line], work_b.at[k], None)
                 store_right(right, base + line, work_b.at[k])
 
     @pl.loop(0, LINES // 2)
     def _(half):
         low = lane_low((32, 128))
-        blocks = []
         for k in range(2):
             line = half * 2 + k
-            at = pl.ds(pl.multiple_of(line * 32, 32), 32)
-            here = p_zp[at, :].astype(F32)
+            here = p_zp[pl.ds(pl.multiple_of(line * 32, 32), 32), :].astype(F32)
             turned = pltpu.roll(here, 64, axis=1)
             work = work_b.at[k]
             work[pl.ds(0, 32, stride=2), :] = jnp.where(low, here, turned)
             work[pl.ds(1, 32, stride=2), :] = jnp.where(low, turned, here)
-            at_right = pl.multiple_of((right_zp * 8 + line) * 64, 64)
-            right[pl.ds(at_right, 64), :] = work[0:64, :].astype(BF16)
-            here = p_zm[at, :].astype(F32)
-            turned = pltpu.roll(here, 64, axis=1)
-            zero = jnp.zeros_like(here)
-            if k == 0:
-                blocks += [jnp.where(low, here, zero), jnp.where(low, turned, zero)]
-            else:
-                blocks += [jnp.where(low, zero, turned), jnp.where(low, zero, here)]
-        block = jnp.concatenate(blocks, axis=0).astype(BF16)
-        left[pl.ds(pl.multiple_of((left_zm * 8 + half * 2) * 64, 128), 128), :] = block.T
-
-    for count, f, base, beyond, weights in ((BY, 1, right_xp, cells_xm, right_x), (BX, 2, right_yp, cells_ym, right_y)):
-
-        @pl.loop(0, count)
-        def _(line):
-            for z in range(0, BZ, 2):
-                at = (base + line) * 256 + z * 32
-                e = beyond + line * BZ + z
-                couples(weights, line * BZ + z, 1, couple, [(f, edge, [at, at + 32], [e, e + 1])])
+            at = pl.multiple_of((right_zp * 8 + line) * 64, 64)
+            right[pl.ds(at, 64), :] = work[0:64, :].astype(BF16)
+
+    told_keys.wait()
+
+    def add(ref, at, low_side, value):
+        low = lane_low((64, 128))
+        zero = jnp.zeros((64, 128), F32)
+        ref[at] += jnp.where(low, value, zero) if low_side else jnp.where(low, zero, value)
+
+    def rim_terms(weights, cell, m, at, places):
+        low = lane_low((64, 128))
+        zero = jnp.zeros((64, 128), BF16)
+        first, second = (weights[pl.ds(pl.multiple_of((cell + k) * 64, 64), 64), :] for k in range(2))
+        weight = jnp.concatenate([jnp.where(low, first, zero), jnp.where(low, zero, second)], axis=0)
+        out = jnp.dot(m[pl.ds(pl.multiple_of(at, 64), 64), :], weight, preferred_element_type=F32)
+        for k in range(2):
+            add(acc_b, places[k], k == 0, out)
+
+    @pl.loop(0, BY)
+    def _(y):
+        for z in range(0, BZ, 2):
+            rim_terms(right_x, y * BZ + z, m_x, y * 256 + z * 32, [keys[1, y, 0, z + k] for k in range(2)])
+
+    @pl.loop(0, BX)
+    def _(x):
+        for z in range(0, BZ, 2):
+            rim_terms(right_y, x * BZ + z, m_y, x * 256 + z * 32, [keys[3, 0, x, z + k] for k in range(2)])
 
     @pl.loop(0, LINES // 2)
     def _(half):
         line = half * 2
-        e = cells_zm + line
-        couples(right_z, line, 1, couple, [(3, rim_z, [line * 32, line * 32 + 32], [e, e + 1])])
+        places = [keys[5, line % BY + k, line // BY, 0] for k in range(2)]
+        rim_terms(right_z, line, m_z, half * 64, places)
 
     for copy in brought:
         copy.wait()
@@ -404,29 +466,18 @@
         e = line * BZ + BZ - 1
         couples(right, right_zp * 8 + line, 1, couple, [(3, face_z, [line * 32, line * 32 + 32], [e, e + BZ])])
 
-    def add(ref, at, low_side, value):
-        low = lane_low((64, 128))
-        zero = jnp.zeros((64, 128), F32)
-        ref[at] += jnp.where(low, value, zero) if low_side else jnp.where(low, zero, value)
-
-    def terms(cell, places, tiles):
+    def terms(cell, places):
         at = pl.multiple_of(cell * 64, 128)
-        first, last = tiles
-        out = jnp.dot(
-            left[pl.ds(at, 128), :],
-            couple[pl.ds(at, 128), first * 128 : last * 128],
-            preferred_element_type=F32,
-        )
+        out = jnp.dot(left[pl.ds(at, 128), :], couple[pl.ds(at, 128), :], preferred_element_type=F32)
         for k in range(2):
             for f, (key_f, key_b) in places[k].items():
-                tile = f // 2 - first
+                tile = f // 2
                 term = out[k * 64 : k * 64 + 64, tile * 128 : tile * 128 + 128]
                 if key_f is not None:
                     add(acc_f, key_f, f % 2 == 0, term)
                 if key_b is not None:
                     add(acc_b, key_b, f % 2 == 0, term)
 
-    told_keys.wait()
 
     @pl.loop(0, LINES)
     def _(line):
@@ -445,27 +496,11 @@
                         3: (keys[6, y, x, k], keys[5, y, x, k + 1] if k < BZ - 1 else None),
                     }
                 )
-            terms(line * BZ + z, places, (0, 2))
-
-    @pl.loop(0, BY)
-    def _(y):
-        for z in range(0, BZ, 2):
-            n = y * BZ + z
-            terms(cells_xm + n, [{1: (None, keys[1, y, 0, z + k])} for k in range(2)], (0, 1))
-
-    @pl.loop(0, BX)
-    def _(x):
-        for z in range(0, BZ, 2):
-            places = [{2: (None, keys[3, 0, x, z + k])} for k in range(2)]
-            terms(cells_ym + x * BZ + z, places, (1, 2))
-
-    @pl.loop(0, LINES // 2)
-    def _(half):
-        line = half * 2
-        places = [{3: (None, keys[5, line % BY + k, line // BY, 0])} for k in range(2)]
-        terms(cells_zm + half * 2, places, (1, 2))
+            terms(line * BZ + z, places)
 
     depth = send.shape[0]
+    for copy in marks:
+        copy.wait()
 
     @pl.loop(0, depth)
     def _(c):
@@ -499,14 +534,6 @@
             sems.at[r],
         ).start()
 
-    @pl.loop(0, depth)
-    def _(c):
-        counts[c] = jnp.full((16, 128), tally[c], jnp.int32).astype(F32).astype(BF16)
-
-    told = pltpu.make_async_copy(counts, send.at[:, pl.ds(PLACES * ROW, 16)], count_sem)
-    told.start()
-    told.wait()
-
     @pl.loop(0, AGG_DEV)
     def _(r):
         pltpu.make_async_copy(rows.at[pl.ds(0, ROW)], send.at[0, pl.ds(0, ROW)], sems.at[r]).wait()
@@ -520,19 +547,16 @@
     return pl.pallas_call(
         compute_kernel,
         out_shape=jax.ShapeDtypeStruct((depth, PACK, 128), BF16),
-        in_specs=[vmem, vmem, smem] + [vmem] * 9 + [any_space] * 2 + [vmem] * 6,
+        in_specs=[vmem, vmem, smem] + [vmem] * 6 + [any_space] * 2 + [vmem] * 6,
         out_specs=any_space,
         scratch_shapes=[
             pltpu.SMEM((SLOTS, BY, BX, BZ), jnp.int32),
             pltpu.VMEM((SLOTS, BY, BX, BZ), jnp.int32),
             pltpu.SemaphoreType.DMA,
             pltpu.SemaphoreType.DMA((BX, 2)),
-            pltpu.VMEM(((BY + BX) * 256, 128), BF16),
             pltpu.VMEM((beyond * 512, 128), BF16),
-            pltpu.VMEM(((LINES + beyond) * 512, 128), BF16),
-            pltpu.VMEM(((LINES + beyond) * 512, 256), BF16),
-            pltpu.VMEM((2, 8 * STEP, 128), F32),
-            pltpu.VMEM((2, 8 * STEP_TWICE, 128), F32),
+            pltpu.VMEM((CELLS * 64, 128), BF16),
+            pltpu.VMEM((CELLS * 64, 256), BF16),
             pltpu.VMEM((2, 8 * STEP_TWICE, 128), F32),
             pltpu.VMEM((KEYS + 1, 64, 128), F32),
             pltpu.VMEM((KEYS + 1, 64, 128), F32),
@@ -540,7 +564,7 @@
             pltpu.VMEM((depth, 16, 128), BF16),
             pltpu.SMEM((depth,), jnp.int32),
             pltpu.SemaphoreType.DMA((AGG_DEV,)),
-            pltpu.SemaphoreType.DMA,
+            pltpu.SemaphoreType.DMA((PLACES,)),
         ],
         compiler_params=pltpu.CompilerParams(vmem_limit_bytes=63 << 20),
         name="coarse_rows",
@@ -552,17 +576,22 @@
 
 def place_kernel(taken, out, told, counts, tally, source, held, work, shaped, sems, row_sems, out_sems):
     depth, count = taken.shape[0], out.shape[1]
-    load = pltpu.make_async_copy(taken.at[:, pl.ds(PLACES * ROW, 16)], told, sems.at[0])
-    load.start()
+    loads = [
+        pltpu.make_async_copy(taken.at[:, pl.ds(k * ROW, 16)], told.at[k], sems.at[k]) for k in range(PLACES)
+    ]
+    for load in loads:
+        load.start()
 
     @pl.loop(0, count + PLACES)
     def _(t):
         source[t] = 0
 
-    load.wait()
+    for load in loads:
+        load.wait()
     for c in range(depth):
-        counts[c : c + 1, :] = told[c, 0:1, :].astype(F32).astype(jnp.int32)
-    move = pltpu.make_async_copy(counts, tally, sems.at[1])
+        here = [told[k, c, 0:1, :].astype(F32) for k in range(PLACES)]
+        counts[c : c + 1, :] = sum((value == value).astype(jnp.int32) for value in here)
+    move = pltpu.make_async_copy(counts, tally, sems.at[PLACES])
     move.start()
     move.wait()
 
@@ -618,14 +647,14 @@
         in_specs=[any_space],
         out_specs=any_space,
         scratch_shapes=[
-            pltpu.VMEM((depth, 16, 128), BF16),
+            pltpu.VMEM((PLACES, depth, 16, 128), BF16),
             pltpu.VMEM((depth, 128), jnp.int32),
             pltpu.SMEM((depth, 128), jnp.int32),
             pltpu.SMEM((count + PLACES,), jnp.int32),
             pltpu.VMEM((count, ROW, 128), BF16),
             pltpu.VMEM((GROUP * ROW_STEP, 128), F32),
             pltpu.VMEM((count // GROUP, SLOTS, GROUP, NODES * NODES), BF16),
-            pltpu.SemaphoreType.DMA((2,)),
+            pltpu.SemaphoreType.DMA((PLACES + 1,)),
             pltpu.SemaphoreType.DMA((count,)),
             pltpu.SemaphoreType.DMA((count // GROUP,)),
         ],

time: 136 us -> 122 us (0.90)
  Pallas kernels: 77 us -> 69.7 us
  blocking collectives: 58.2 us -> 52.2 us
    pallas_call x1, Pallas kernels: 39.2 us -> 31.4 us  [coarse_rows(): pl.pallas_call(compute_kernel, out_shape=jax.ShapeDtypeStruct((depth, PAC...]
    all_to_all x1, blocking collectives: 58.2 us -> 52.2 us  [shards(): taken = lax.all_to_all(send, 'gz', 0, 0, tiled=True)]
where the time goes in v6:
time: 122 us
  Pallas kernels  69.7 us (57%)
  blocking collectives  52.2 us (43%)
    all_to_all x1, blocking collectives, shards(): taken = lax.all_to_all(send, 'gz', 0, 0, tiled=True)  52.2 us
    pallas_call x1, Pallas kernels, coarse_rows(): pl.pallas_call(compute_kernel, out_shape=jax.ShapeDtypeStruct((depth, PAC...  31.4 us
    pallas_call x1, Pallas kernels, inner(): pl.pallas_call(inner_kernel, out_shape=[jax.ShapeDtypeStruct(shape, BF16)...  29.6 us
    pallas_call x1, Pallas kernels, place_rows(): pl.pallas_call(place_kernel, out_shape=jax.ShapeDtypeStruct((SLOTS, count...  8.73 us

profile of v6, /device:TPU:0, one launch (start us, length us, event | category | flops | bytes accessed | tf_op | source)
XLA Modules:
  0.0 122.0 jit_solution(13251182003475183444)
XLA Ops:
  0.0 29.6 %inner.1 = (bf16[1536,128]{1,0:T(8,128)(2,1)}, bf16[1024,128]{1,0:T(8,128)(2,1)}, bf16[768,128]{1,0:T(8,128)(2,1)}, bf16[6,8,4096]{2,1,0:T(8,128)(2,1)}, bf16[4,...) custom-call(bf16[4,6,8,4096]{3,2,1,0:T(8,128)(2,1)} %prolong.1, ...), custom_call_target="tpu_custom_call" | custom-call | tf_op jit(solution)/shard_map/inner/pallas_call | solution.py:323
  29.6 31.4 %coarse_rows.1 = bf16[32,448,128]{2,1,0:T(8,128)(2,1)} custom-call(s32[6,4,8]{2,1,0:T(4,128)} %bitcast.6, s32[7,6,4,8]{3,2,1,0:T(4,128)} %bitcast.5, s32[24]{0:T(128)} %owner.1, bf16[1536,128]{1,0:T(8,128)(2,1)} %get-tuple-element.19.m_x, bf16[1024,128]{1,0:T(8,128)(2,1)} %get-tuple-element.20.m_y, bf16[768,128]{1,0:T(8,128)(2,1)} %get-tuple-element.21.m_z, ...), custom_call_target="tpu_custom_call" | custom-call | tf_op jit(solution)/shard_map/coarse_rows/pallas_call | solution.py:547
  61.0 52.2 %all_to_all.5.taken = bf16[32,448,128]{2,1,0:T(8,128)(2,1)} all-to-all(bf16[32,448,128]{2,1,0:T(8,128)(2,1)} %coarse_rows.1), channel_id=1, replica_groups=mesh['gx'=2,'gy'=2,'gz'=32] {'gz'}, dimensions={0} | all-to-all | bytes 7340032 | tf_op jit(solution)/shard_map/all_to_all | solution.py:675
  113.2 8.7 %place_rows.1 = bf16[7,64,4096]{2,1,0:T(8,128)(2,1)} custom-call(bf16[32,448,128]{2,1,0:T(8,128)(2,1)} %all_to_all.5.taken), custom_call_target="tpu_custom_call" | custom-call | tf_op jit(solution)/shard_map/place_rows/pallas_call | solution.py:644

commit v7 on v6

--- a/solution.py
+++ b/solution.py
@@ -282,23 +282,24 @@
 
     for x in range(BX):
 
-        @pl.loop(0, BY)
-        def _(y):
-            line = x * BY + y
-            from_y = jnp.where(y > 0, line - 1, line)
-            into_y = jnp.where(y > 0, (line - 1) * BZ, CELLS)
-            for z in range(0, BZ, 2):
-                n = line * BZ + z
-                both = range(2)
-                blocks = [
-                    (0, ra_d, [(n + k) * 32 for k in both], [n, n + 1]),
-                    (2, ra_y, [from_y * 256 + (z + k) * 32 for k in both], [into_y + z, into_y + z + 1]),
-                    (3, ra_z, [line * 288 + (z + k) * 32 for k in both], [CELLS if z == 0 else n - 1, n]),
-                ]
-                if x > 0:
-                    e = n - BY * BZ
-                    blocks.append((1, ra_x, [(e + k) * 32 for k in both], [e, e + 1]))
-                couples(right, n, 1, couple, blocks)
+        @pl.loop(0, BY // 2)
+        def _(half):
+            for y in (half * 2, half * 2 + 1):
+                line = x * BY + y
+                from_y = jnp.where(y > 0, line - 1, line)
+                into_y = jnp.where(y > 0, (line - 1) * BZ, CELLS)
+                for z in range(0, BZ, 2):
+                    n = line * BZ + z
+                    both = range(2)
+                    blocks = [
+                        (0, ra_d, [(n + k) * 32 for k in both], [n, n + 1]),
+                        (2, ra_y, [from_y * 256 + (z + k) * 32 for k in both], [into_y + z, into_y + z + 1]),
+                        (3, ra_z, [line * 288 + (z + k) * 32 for k in both], [CELLS if z == 0 else n - 1, n]),
+                    ]
+                    if x > 0:
+                        e = n - BY * BZ
+                        blocks.append((1, ra_x, [(e + k) * 32 for k in both], [e, e + 1]))
+                    couples(right, n, 1, couple, blocks)
 
         if x > 0:
             rows = pl.ds((x - 1) * BY * BZ * 64, BY * BZ * 64)
@@ -359,12 +360,19 @@
 
 
 def compute_kernel(
-    aggregate, slot, owner,
-    m_x, m_y, m_z, p_xp, p_yp, p_zp,
-    couple_in, left_in, right_x, right_y, right_z, face_x, face_y, face_z,
-    send, keys, key_work, key_sem, in_sems, right, left, couple, work_b,
-    acc_f, acc_b, rows, absent, tally, sems, absent_sems,
+    aggregate, slot, owner, *refs
 ):
+    arrays, refs = refs[:14], refs[14:]
+    small, couple_in, left_in = arrays[:6] + arrays[8:], arrays[6], arrays[7]
+    send, held, refs = refs[0], refs[1:13], refs[13:]
+    m_x, m_y, m_z, p_xp, p_yp, p_zp, right_x, right_y, right_z, face_x, face_y, face_z = held
+    (
+    small_sems, keys, key_work, key_sem, in_sems, right, left, couple, work_b,
+    f_low, f_high, b_low, b_high, rows, absent, tally, sems, absent_sems,
+    ) = refs
+    fetched = [pltpu.make_async_copy(*pair, small_sems.at[k]) for k, pair in enumerate(zip(small, held))]
+    for copy in fetched:
+        copy.start()
     plane = BY * BZ * 64
     brought = []
     for x in range(BX):
@@ -384,8 +392,11 @@
     key_work[...] = aggregate[...][None] * SLOTS + slot[...]
     told_keys = pltpu.make_async_copy(key_work, keys, key_sem)
     told_keys.start()
-    acc_f[...] = jnp.zeros_like(acc_f)
-    acc_b[...] = jnp.zeros_like(acc_b)
+    for ref in (f_low, f_high, b_low, b_high):
+        ref[...] = jnp.zeros_like(ref)
+
+    for copy in fetched:
+        copy.wait()
 
     right_xp, right_yp, right_zp = 0, BY, BY + BX
 
@@ -413,19 +424,14 @@
 
     told_keys.wait()
 
-    def add(ref, at, low_side, value):
-        low = lane_low((64, 128))
-        zero = jnp.zeros((64, 128), F32)
-        ref[at] += jnp.where(low, value, zero) if low_side else jnp.where(low, zero, value)
-
     def rim_terms(weights, cell, m, at, places):
         low = lane_low((64, 128))
         zero = jnp.zeros((64, 128), BF16)
         first, second = (weights[pl.ds(pl.multiple_of((cell + k) * 64, 64), 64), :] for k in range(2))
         weight = jnp.concatenate([jnp.where(low, first, zero), jnp.where(low, zero, second)], axis=0)
         out = jnp.dot(m[pl.ds(pl.multiple_of(at, 64), 64), :], weight, preferred_element_type=F32)
-        for k in range(2):
-            add(acc_b, places[k], k == 0, out)
+        b_low[places[0]] += out
+        b_high[places[1]] += out
 
     @pl.loop(0, BY)
     def _(y):
@@ -474,9 +480,9 @@
                 tile = f // 2
                 term = out[k * 64 : k * 64 + 64, tile * 128 : tile * 128 + 128]
                 if key_f is not None:
-                    add(acc_f, key_f, f % 2 == 0, term)
+                    (f_low, f_high)[f % 2][key_f] += term
                 if key_b is not None:
-                    add(acc_b, key_b, f % 2 == 0, term)
+                    (b_low, b_high)[f % 2][key_b] += term
 
 
     @pl.loop(0, LINES)
@@ -506,25 +512,30 @@
     def _(c):
         tally[c] = 0
 
-    @pl.loop(0, AGG_DEV)
-    def _(r):
-        low, low_half = lane_low((64, 128)), lane_low((32, 128))
-
-        for s in range(0, SLOTS, 2):
-            first = acc_b[r * SLOTS + s]
-            second = acc_b[r * SLOTS + s + 1] if s + 1 < SLOTS else first
-            pair = jnp.where(low, first, second)
-            pair += pltpu.roll(jnp.where(low, second, first), 64, axis=1)
-            flipped = pair.T
-            for k in range(min(2, SLOTS - s)):
-                acc_f[r * SLOTS + s + k, :, 0:64] += flipped[k * 64 : k * 64 + 64]
+    def fold(r):
+        low = lane_low((64, 128))
+        for s in range(0, SLOTS, 4):
+            blocks = []
+            for k in (s, s + 2):
+                at = [r * SLOTS + min(k + side, SLOTS - 1) for side in range(2)]
+                pair = jnp.where(low, b_low[at[0]], b_high[at[1]])
+                pair += pltpu.roll(jnp.where(low, b_low[at[1]], b_high[at[0]]), 64, axis=1)
+                blocks.append(pair)
+            flipped = jnp.concatenate(blocks, axis=0).T
+            for k in range(s, min(s + 4, SLOTS)):
+                ref = f_low if k < s + 2 else f_high
+                ref[r * SLOTS + k] += flipped[k % 2 * 64 : k % 2 * 64 + 64]
+
+    def lay_out(r):
+        low_half = lane_low((32, 128))
         for s in range(SLOTS):
-            total = acc_f.at[r * SLOTS + s]
-            even = total[pl.ds(0, 32, stride=2), :]
-            odd = total[pl.ds(1, 32, stride=2), :]
-            row = jnp.where(low_half, even, odd)
-            row += pltpu.roll(jnp.where(low_half, odd, even), 64, axis=1)
+            parts = f_low.at[r * SLOTS + s], f_high.at[r * SLOTS + s]
+            even, odd = ([ref[pl.ds(p, 32, stride=2), :] for ref in parts] for p in range(2))
+            row = jnp.where(low_half, even[0], odd[1])
+            row += pltpu.roll(jnp.where(low_half, odd[0], even[1]), 64, axis=1)
             rows[pl.ds(pl.multiple_of(r * ROW + s * 32, 32), 32), :] = row.astype(BF16)
+
+    def hand_out(r):
         c = owner[r]
         place = tally[c]
         tally[c] = place + 1
@@ -534,6 +545,13 @@
             sems.at[r],
         ).start()
 
+    @pl.loop(0, AGG_DEV // 2)
+    def _(half):
+        pair = (half * 2, half * 2 + 1)
+        for step in (fold, lay_out, hand_out):
+            for r in pair:
+                step(r)
+
     @pl.loop(0, AGG_DEV)
     def _(r):
         pltpu.make_async_copy(rows.at[pl.ds(0, ROW)], send.at[0, pl.ds(0, ROW)], sems.at[r]).wait()
@@ -547,9 +565,11 @@
     return pl.pallas_call(
         compute_kernel,
         out_shape=jax.ShapeDtypeStruct((depth, PACK, 128), BF16),
-        in_specs=[vmem, vmem, smem] + [vmem] * 6 + [any_space] * 2 + [vmem] * 6,
+        in_specs=[vmem, vmem, smem] + [any_space] * len(arrays),
         out_specs=any_space,
-        scratch_shapes=[
+        scratch_shapes=[pltpu.VMEM(array.shape, BF16) for array in arrays[:6] + arrays[8:]]
+        + [
+            pltpu.SemaphoreType.DMA((12,)),
             pltpu.SMEM((SLOTS, BY, BX, BZ), jnp.int32),
             pltpu.VMEM((SLOTS, BY, BX, BZ), jnp.int32),
             pltpu.SemaphoreType.DMA,
@@ -558,6 +578,8 @@
             pltpu.VMEM((CELLS * 64, 128), BF16),
             pltpu.VMEM((CELLS * 64, 256), BF16),
             pltpu.VMEM((2, 8 * STEP_TWICE, 128), F32),
+            pltpu.VMEM((KEYS + 1, 64, 128), F32),
+            pltpu.VMEM((KEYS + 1, 64, 128), F32),
             pltpu.VMEM((KEYS + 1, 64, 128), F32),
             pltpu.VMEM((KEYS + 1, 64, 128), F32),
             pltpu.VMEM((AGG_DEV * ROW, 128), BF16),
@@ -571,7 +593,7 @@
     )(aggregate, slot, owner, *arrays)
 
 
-GROUP, ROW_STEP = 8, ROW + 4
+GROUP, ROW_STEP, ROW_PARTS = 8, ROW + 4, 4
 
 
 def place_kernel(taken, out, told, counts, tally, source, held, work, shaped, sems, row_sems, out_sems):
@@ -581,6 +603,13 @@
     ]
     for load in loads:
         load.start()
+    part = depth // ROW_PARTS
+    brought = []
+    for k in range(ROW_PARTS):
+        at = pl.ds(k * part, part)
+        copy = pltpu.make_async_copy(taken.at[at], held.at[at], row_sems.at[k])
+        copy.start()
+        brought.append(copy)
 
     @pl.loop(0, count + PLACES)
     def _(t):
@@ -602,18 +631,8 @@
 
     total = lax.fori_loop(0, depth, order, 0)
 
-    def row_copy(t):
-        at = source[t]
-        place = pl.multiple_of(lax.rem(at, PLACES) * ROW, 32)
-        return pltpu.make_async_copy(taken.at[at // PLACES, pl.ds(place, ROW)], held.at[t], row_sems.at[t])
-
-    @pl.loop(0, count)
-    def _(t):
-        @pl.when(t >= total)
-        def _():
-            source[t] = 0
-
-        row_copy(t).start()
+    for copy in brought:
+        copy.wait()
 
     def out_copy(group):
         rows = pl.ds(pl.multiple_of(group * GROUP, GROUP), GROUP)
@@ -623,8 +642,9 @@
     def _(group):
         for k in range(GROUP):
             t = group * GROUP + k
-            row_copy(t).wait()
-            row = held[t].astype(F32)
+            at = jnp.where(t < total, source[t], 0)
+            place = pl.multiple_of(lax.rem(at, PLACES) * ROW, 32)
+            row = held[at // PLACES, pl.ds(place, ROW), :].astype(F32)
             work[k * ROW_STEP : k * ROW_STEP + ROW, :] = jnp.where(t < total, row, jnp.zeros_like(row))
         for s in range(SLOTS):
             for tile in range(32):
@@ -651,11 +671,11 @@
             pltpu.VMEM((depth, 128), jnp.int32),
             pltpu.SMEM((depth, 128), jnp.int32),
             pltpu.SMEM((count + PLACES,), jnp.int32),
-            pltpu.VMEM((count, ROW, 128), BF16),
+            pltpu.VMEM((depth, PACK, 128), BF16),
             pltpu.VMEM((GROUP * ROW_STEP, 128), F32),
             pltpu.VMEM((count // GROUP, SLOTS, GROUP, NODES * NODES), BF16),
             pltpu.SemaphoreType.DMA((PLACES + 1,)),
-            pltpu.SemaphoreType.DMA((count,)),
+            pltpu.SemaphoreType.DMA((ROW_PARTS,)),
             pltpu.SemaphoreType.DMA((count // GROUP,)),
         ],
         compiler_params=pltpu.CompilerParams(vmem_limit_bytes=63 << 20),

time: 122 us -> 116 us (0.951)
  Pallas kernels: 69.7 us -> 62.8 us
    pallas_call x1, Pallas kernels: 8.73 us -> 4.94 us  [place_rows(): pl.pallas_call(place_kernel, out_shape=jax.ShapeDtypeStruct((SLOTS, count...]
    pallas_call x1, Pallas kernels: 31.4 us -> 29.4 us  [coarse_rows(): pl.pallas_call(compute_kernel, out_shape=jax.ShapeDtypeStruct((depth, PAC...]
    pallas_call x1, Pallas kernels: 29.6 us -> 28.4 us  [inner(): pl.pallas_call(inner_kernel, out_shape=[jax.ShapeDtypeStruct(shape, BF16)...]
where the time goes in v7:
time: 116 us; the launch traced here: 115 us
  Pallas kernels  62.8 us (54%)
  blocking collectives  52.7 us (45%)
    all_to_all x1, blocking collectives, shards(): taken = lax.all_to_all(send, 'gz', 0, 0, tiled=True)  52.7 us
    pallas_call x1, Pallas kernels, coarse_rows(): pl.pallas_call(compute_kernel, out_shape=jax.ShapeDtypeStruct((depth, PAC...  29.4 us
    pallas_call x1, Pallas kernels, inner(): pl.pallas_call(inner_kernel, out_shape=[jax.ShapeDtypeStruct(shape, BF16)...  28.4 us
    pallas_call x1, Pallas kernels, place_rows(): pl.pallas_call(place_kernel, out_shape=jax.ShapeDtypeStruct((SLOTS, count...  4.94 us

profile of v7, /device:TPU:0, one launch (start us, length us, event | category | flops | bytes accessed | tf_op | source)
XLA Modules:
  0.0 115.4 jit_solution(4523283376932330905)
XLA Ops:
  0.0 28.4 %inner.1 = (bf16[1536,128]{1,0:T(8,128)(2,1)}, bf16[1024,128]{1,0:T(8,128)(2,1)}, bf16[768,128]{1,0:T(8,128)(2,1)}, bf16[6,8,4096]{2,1,0:T(8,128)(2,1)}, bf16[4,...) custom-call(bf16[4,6,8,4096]{3,2,1,0:T(8,128)(2,1)} %prolong.1, ...), custom_call_target="tpu_custom_call" | custom-call | tf_op jit(solution)/shard_map/inner/pallas_call | solution.py:324
  28.4 29.4 %coarse_rows.1 = bf16[32,448,128]{2,1,0:T(8,128)(2,1)} custom-call(s32[6,4,8]{2,1,0:T(4,128)} %bitcast.6, s32[7,6,4,8]{3,2,1,0:T(4,128)} %bitcast.5, s32[24]{0:T(128)} %owner.1, bf16[1536,128]{1,0:T(8,128)(2,1)} %get-tuple-element.19.refs_0_, bf16[1024,128]{1,0:T(8,128)(2,1)} %get-tuple-element.20.refs_1_, bf16[768,128]{1,0:T(8,128)(2,1)} %get-tuple-element.21.refs_2_, ...), custom_call_target="tpu_custom_call" | custom-call | tf_op jit(solution)/shard_map/coarse_rows/pallas_call | solution.py:565
  57.8 52.7 %all_to_all.5.taken = bf16[32,448,128]{2,1,0:T(8,128)(2,1)} all-to-all(bf16[32,448,128]{2,1,0:T(8,128)(2,1)} %coarse_rows.1), channel_id=1, replica_groups=mesh['gx'=2,'gy'=2,'gz'=32] {'gz'}, dimensions={0} | all-to-all | bytes 7340032 | tf_op jit(solution)/shard_map/all_to_all | solution.py:695
  110.5 4.9 %place_rows.1 = bf16[7,64,4096]{2,1,0:T(8,128)(2,1)} custom-call(bf16[32,448,128]{2,1,0:T(8,128)(2,1)} %all_to_all.5.taken), custom_call_target="tpu_custom_call" | custom-call | tf_op jit(solution)/shard_map/place_rows/pallas_call | solution.py:664

commit v8 on v7

--- a/solution.py
+++ b/solution.py
@@ -19,6 +19,16 @@
 BF16 = jnp.bfloat16
 
 
+def sweep(count, by):
+    def run(body):
+        @pl.loop(0, count // by)
+        def _(turn):
+            for k in range(by):
+                body(turn * by + k, k)
+
+    return run
+
+
 def lane_low(shape):
     return lax.broadcasted_iota(jnp.int32, shape, 1) < 64
 
@@ -29,20 +39,14 @@
         scratch[pl.ds(tile, 8, stride=STEP), :] = values[:, tile * 128 : tile * 128 + 128]
 
 
-def spread_twice(line, natural, by_parity):
+def spread_twice(line, natural):
     values = line.astype(F32)
     low = lane_low((8, 128))
     for tile in range(32):
         here = values[:, tile * 128 : tile * 128 + 128]
         swapped = pltpu.roll(here, 64, axis=1)
-        even = jnp.where(low, here, swapped)
-        odd = jnp.where(low, swapped, here)
-        if natural is not None:
-            natural[pl.ds(2 * tile, 8, stride=STEP_TWICE), :] = even
-            natural[pl.ds(2 * tile + 1, 8, stride=STEP_TWICE), :] = odd
-        if by_parity is not None:
-            by_parity[pl.ds(tile, 8, stride=STEP_TWICE), :] = even
-            by_parity[pl.ds(32 + tile, 8, stride=STEP_TWICE), :] = odd
+        natural[pl.ds(2 * tile, 8, stride=STEP_TWICE), :] = jnp.where(low, here, swapped)
+        natural[pl.ds(2 * tile + 1, 8, stride=STEP_TWICE), :] = jnp.where(low, swapped, here)
 
 
 MESH = pl.DeviceIdType.MESH
@@ -91,8 +95,12 @@
 def store_left(left, base, work):
     low = lane_low((64, 128))
     zero = jnp.zeros((64, 128), F32)
+
+    def by_parity(z):
+        return jnp.concatenate([work[pl.ds(z * STEP_TWICE + p, 32, stride=2), :] for p in range(2)], axis=0)
+
     for pair in range(4):
-        first, second = (work[z * STEP_TWICE : z * STEP_TWICE + 64, :] for z in (2 * pair, 2 * pair + 1))
+        first, second = by_parity(2 * pair), by_parity(2 * pair + 1)
         block = jnp.concatenate([jnp.where(low, first, zero), jnp.where(low, zero, second)], axis=0)
         at = pl.multiple_of(base * 512 + pair * 128, 128)
         left[pl.ds(at, 128), :] = block.astype(BF16).T
@@ -106,7 +114,7 @@
     m_x, m_y, m_z, p_xp, p_yp, p_zp,
     couple_out, left_out, right_x, right_y, right_z, face_x, face_y, face_z,
     in_p, in_d, in_f, zero, zero_m, out_mx, out_my, out_mz, out_az, out_p_first,
-    ra_d, ra_x, ra_y, ra_z, right, first_z, left, couple, work_a, work_b, work_c,
+    ra_d, ra_x, ra_y, ra_z, right, first_z, left, couple, work_a, work_b,
     load_sems, send_sems, recv_sems, zero_sems, out_sems,
 ):
     depth = lax.axis_size("gz")
@@ -180,21 +188,20 @@
     ]
     loads[0].wait()
 
-    @pl.loop(0, LINES // 2)
-    def _(half):
+    @pl.loop(0, BX)
+    def _(x):
         low = lane_low((32, 128))
-        for k in range(2):
-            line = half * 2 + k
-            x, y = line // BY, line % BY
+        for y in range(BY):
+            line = x * BY + y
             at = pl.ds(pl.multiple_of(line * 32, 32), 32)
-            natural, by_parity = work_b.at[k], work_c.at[k]
-            spread_twice(in_p[x, y], natural, by_parity)
-            even, odd = by_parity[0:32, :], by_parity[32:64, :]
+            natural = work_b.at[y]
+            spread_twice(in_p[x, y], natural)
+            even, odd = (natural[pl.ds(p, 32, stride=2), :] for p in range(2))
             out_p_first[at, :] = jnp.where(low, even, odd).astype(BF16)
             ra_z[pl.ds(pl.multiple_of(line * 288, 32), 32), :] = jnp.zeros((32, 128), BF16)
             store_right(right, line, natural)
             first_z[pl.ds(pl.multiple_of(line * 64, 64), 64), :] = natural[0:64, :].astype(BF16)
-            store_left(left, line, by_parity)
+            store_left(left, line, natural)
 
     ends.append(pass_down(2, "gz", out_p_first, p_zp, zero_m.at[pl.ds(0, LINES * 32)]))
     loads[1].wait()
@@ -230,39 +237,36 @@
                     at = pl.multiple_of(row * 256 + pair * 64, 64)
                     out[pl.ds(at, 64), :] = side_by_side(both[0:64], both[64:128])
 
-    @pl.loop(0, LINES // 2)
-    def _(half):
-        last = []
-        for k in range(2):
-            line = half * 2 + k
-            work = work_a.at[k]
-            store_spread(in_f[2, line // BY, line % BY], ra_z, line * 288 + 32, work)
-            at = pl.ds(pl.multiple_of(line * 32, 32), 32)
-            out_az[at, :] = work[(BZ - 1) * STEP : (BZ - 1) * STEP + 32, :].astype(BF16)
-            last.append(outgoing(work, BZ // 2 - 1, line)[64:128])
-        out_mz[pl.ds(pl.multiple_of(half * 64, 64), 64), :] = side_by_side(*last)
+    @pl.loop(0, BX)
+    def _(x):
+        for y in range(0, BY, 2):
+            last = []
+            for k in range(2):
+                line = x * BY + y + k
+                work = work_a.at[y + k]
+                store_spread(in_f[2, x, y + k], ra_z, line * 288 + 32, work)
+                at = pl.ds(pl.multiple_of(line * 32, 32), 32)
+                out_az[at, :] = work[(BZ - 1) * STEP : (BZ - 1) * STEP + 32, :].astype(BF16)
+                last.append(outgoing(work, BZ // 2 - 1, line)[64:128])
+            at = pl.multiple_of((x * BY + y) * 32, 64)
+            out_mz[pl.ds(at, 64), :] = side_by_side(*last)
 
     for number, axis, source, dest in ((3, "gy", out_my, m_y), (4, "gz", out_mz, m_z), (5, "gx", out_mx, m_x)):
         ends.append(pass_up(number, axis, source, dest, zero_m.at[pl.ds(0, source.shape[0])]))
     loads[4].wait()
     loads[5].wait()
 
-    @pl.loop(0, LINES // 2)
-    def _(half):
-        for k in range(2):
-            line = half * 2 + k
-            store_spread(in_d[line // BY, line % BY], ra_d, line * 256, work_a.at[k])
-
-    @pl.loop(0, (LINES - BY) // 2)
-    def _(half):
-        for k in range(2):
-            line = half * 2 + k
-            store_spread(in_f[0, line // BY, line % BY], ra_x, line * 256, work_a.at[k])
-
     @pl.loop(0, BX)
     def _(x):
+        for y in range(BY):
+            store_spread(in_d[x, y], ra_d, (x * BY + y) * 256, work_a.at[y])
         for y in range(BY - 1):
-            store_spread(in_f[1, x, y], ra_y, (x * BY + y) * 256, work_a.at[y % 3])
+            store_spread(in_f[1, x, y], ra_y, (x * BY + y) * 256, work_a.at[y])
+
+    @pl.loop(0, BX - 1)
+    def _(x):
+        for y in range(BY):
+            store_spread(in_f[0, x, y], ra_x, (x * BY + y) * 256, work_a.at[y])
 
     moves = []
 
@@ -345,9 +349,8 @@
             pltpu.VMEM((LINES * 64, 128), BF16),
             pltpu.VMEM((CELLS * 64, 128), BF16),
             pltpu.VMEM(((CELLS + BZ) * 64, 256), BF16),
-            pltpu.VMEM((3, 8 * STEP, 128), F32),
-            pltpu.VMEM((2, 8 * STEP_TWICE, 128), F32),
-            pltpu.VMEM((2, 8 * STEP_TWICE, 128), F32),
+            pltpu.VMEM((BY, 8 * STEP, 128), F32),
+            pltpu.VMEM((BY, 8 * STEP_TWICE, 128), F32),
             pltpu.SemaphoreType.DMA((6,)),
             pltpu.SemaphoreType.DMA((6,)),
             pltpu.SemaphoreType.DMA((6,)),
@@ -402,25 +405,21 @@
 
     for count, after, base in ((BY, p_xp, right_xp), (BX, p_yp, right_yp)):
 
-        @pl.loop(0, count // 2)
-        def _(half):
-            for k in range(2):
-                line = half * 2 + k
-                spread_twice(after[line], work_b.at[k], None)
-                store_right(right, base + line, work_b.at[k])
-
-    @pl.loop(0, LINES // 2)
-    def _(half):
+        @sweep(count, 2)
+        def _(line, k):
+            spread_twice(after[line], work_b.at[k])
+            store_right(right, base + line, work_b.at[k])
+
+    @sweep(LINES, 8)
+    def _(line, k):
         low = lane_low((32, 128))
-        for k in range(2):
-            line = half * 2 + k
-            here = p_zp[pl.ds(pl.multiple_of(line * 32, 32), 32), :].astype(F32)
-            turned = pltpu.roll(here, 64, axis=1)
-            work = work_b.at[k]
-            work[pl.ds(0, 32, stride=2), :] = jnp.where(low, here, turned)
-            work[pl.ds(1, 32, stride=2), :] = jnp.where(low, turned, here)
-            at = pl.multiple_of((right_zp * 8 + line) * 64, 64)
-            right[pl.ds(at, 64), :] = work[0:64, :].astype(BF16)
+        here = p_zp[pl.ds(pl.multiple_of(line * 32, 32), 32), :].astype(F32)
+        turned = pltpu.roll(here, 64, axis=1)
+        work = work_b.at[k % 2, pl.ds(k // 2 * 64, 64)]
+        work[pl.ds(0, 32, stride=2), :] = jnp.where(low, here, turned)
+        work[pl.ds(1, 32, stride=2), :] = jnp.where(low, turned, here)
+        at = pl.multiple_of((right_zp * 8 + line) * 64, 64)
+        right[pl.ds(at, 64), :] = work[...].astype(BF16)
 
     told_keys.wait()
 
@@ -433,18 +432,18 @@
         b_low[places[0]] += out
         b_high[places[1]] += out
 
-    @pl.loop(0, BY)
-    def _(y):
+    @sweep(BY, 2)
+    def _(y, _turn):
         for z in range(0, BZ, 2):
             rim_terms(right_x, y * BZ + z, m_x, y * 256 + z * 32, [keys[1, y, 0, z + k] for k in range(2)])
 
-    @pl.loop(0, BX)
-    def _(x):
+    @sweep(BX, 2)
+    def _(x, _turn):
         for z in range(0, BZ, 2):
             rim_terms(right_y, x * BZ + z, m_y, x * 256 + z * 32, [keys[3, 0, x, z + k] for k in range(2)])
 
-    @pl.loop(0, LINES // 2)
-    def _(half):
+    @sweep(LINES // 2, 4)
+    def _(half, _turn):
         line = half * 2
         places = [keys[5, line % BY + k, line // BY, 0] for k in range(2)]
         rim_terms(right_z, line, m_z, half * 64, places)
@@ -452,22 +451,22 @@
     for copy in brought:
         copy.wait()
 
-    @pl.loop(0, BY)
-    def _(y):
+    @sweep(BY, 3)
+    def _(y, _turn):
         for z in range(0, BZ, 2):
             e = ((BX - 1) * BY + y) * BZ + z
             at = y * 256 + z * 32
             couples(right, (right_xp + y) * 8 + z, 1, couple, [(1, face_x, [at, at + 32], [e, e + 1])])
 
-    @pl.loop(0, BX)
-    def _(x):
+    @sweep(BX, 2)
+    def _(x, _turn):
         for z in range(0, BZ, 2):
             e = (x * BY + BY - 1) * BZ + z
             at = x * 256 + z * 32
             couples(right, (right_yp + x) * 8 + z, 1, couple, [(2, face_y, [at, at + 32], [e, e + 1])])
 
-    @pl.loop(0, LINES // 2)
-    def _(half):
+    @sweep(LINES // 2, 6)
+    def _(half, _turn):
         line = half * 2
         e = line * BZ + BZ - 1
         couples(right, right_zp * 8 + line, 1, couple, [(3, face_z, [line * 32, line * 32 + 32], [e, e + BZ])])
@@ -485,8 +484,8 @@
                     (b_low, b_high)[f % 2][key_b] += term
 
 
-    @pl.loop(0, LINES)
-    def _(line):
+    @sweep(LINES, 2)
+    def _(line, _turn):
         x, y = line // BY, line % BY
         next_x, next_y = jnp.minimum(x + 1, BX - 1), jnp.minimum(y + 1, BY - 1)
         for z in range(0, BZ, 2):

time: 116 us -> 107 us (0.922)
  Pallas kernels: 62.8 us -> 52.8 us
    pallas_call x1, Pallas kernels: 29.4 us -> 22 us  [coarse_rows(): pl.pallas_call(compute_kernel, out_shape=jax.ShapeDtypeStruct((depth, PAC...]
    pallas_call x1, Pallas kernels: 28.4 us -> 25.8 us  [inner(): pl.pallas_call(inner_kernel, out_shape=[jax.ShapeDtypeStruct(shape, BF16)...]
where the time goes in v8:
time: 107 us
  blocking collectives  53.8 us (50%)
  Pallas kernels  52.8 us (49%)
    all_to_all x1, blocking collectives, shards(): taken = lax.all_to_all(send, 'gz', 0, 0, tiled=True)  53.8 us
    pallas_call x1, Pallas kernels, inner(): pl.pallas_call(inner_kernel, out_shape=[jax.ShapeDtypeStruct(shape, BF16)...  25.8 us
    pallas_call x1, Pallas kernels, coarse_rows(): pl.pallas_call(compute_kernel, out_shape=jax.ShapeDtypeStruct((depth, PAC...  22 us
    pallas_call x1, Pallas kernels, place_rows(): pl.pallas_call(place_kernel, out_shape=jax.ShapeDtypeStruct((SLOTS, count...  4.94 us

profile of v8, /device:TPU:0, one launch (start us, length us, event | category | flops | bytes accessed | tf_op | source)
XLA Modules:
  0.0 106.6 jit_solution(24636714413433885)
XLA Ops:
  0.0 25.8 %inner.1 = (bf16[1536,128]{1,0:T(8,128)(2,1)}, bf16[1024,128]{1,0:T(8,128)(2,1)}, bf16[768,128]{1,0:T(8,128)(2,1)}, bf16[6,8,4096]{2,1,0:T(8,128)(2,1)}, bf16[4,...) custom-call(bf16[4,6,8,4096]{3,2,1,0:T(8,128)(2,1)} %prolong.1, ...), custom_call_target="tpu_custom_call" | custom-call | tf_op jit(solution)/shard_map/inner/pallas_call | solution.py:328
  25.8 22.0 %coarse_rows.1 = bf16[32,448,128]{2,1,0:T(8,128)(2,1)} custom-call(s32[6,4,8]{2,1,0:T(4,128)} %bitcast.6, s32[7,6,4,8]{3,2,1,0:T(4,128)} %bitcast.5, s32[24]{0:T(128)} %owner.1, bf16[1536,128]{1,0:T(8,128)(2,1)} %get-tuple-element.19.refs_0_, bf16[1024,128]{1,0:T(8,128)(2,1)} %get-tuple-element.20.refs_1_, bf16[768,128]{1,0:T(8,128)(2,1)} %get-tuple-element.21.refs_2_, ...), custom_call_target="tpu_custom_call" | custom-call | tf_op jit(solution)/shard_map/coarse_rows/pallas_call | solution.py:564
  47.9 53.8 %all_to_all.5.taken = bf16[32,448,128]{2,1,0:T(8,128)(2,1)} all-to-all(bf16[32,448,128]{2,1,0:T(8,128)(2,1)} %coarse_rows.1), channel_id=1, replica_groups=mesh['gx'=2,'gy'=2,'gz'=32] {'gz'}, dimensions={0} | all-to-all | bytes 7340032 | tf_op jit(solution)/shard_map/all_to_all | solution.py:694
  101.7 4.9 %place_rows.1 = bf16[7,64,4096]{2,1,0:T(8,128)(2,1)} custom-call(bf16[32,448,128]{2,1,0:T(8,128)(2,1)} %all_to_all.5.taken), custom_call_target="tpu_custom_call" | custom-call | tf_op jit(solution)/shard_map/place_rows/pallas_call | solution.py:663

commit v9 on v8

--- a/solution.py
+++ b/solution.py
@@ -225,17 +225,13 @@
         (1, BX, out_my, lambda k: k * BY + BY - 1),
     ):
 
-        @pl.loop(0, count // 2)
-        def _(half):
-            for k in range(2):
-                row = half * 2 + k
-                line = line_of(row)
-                work = work_a.at[k]
-                store_spread(in_f[f, line // BY, line % BY], (ra_x, ra_y)[f], line * 256, work)
-                for pair in range(4):
-                    both = outgoing(work, pair, line)
-                    at = pl.multiple_of(row * 256 + pair * 64, 64)
-                    out[pl.ds(at, 64), :] = side_by_side(both[0:64], both[64:128])
+        for row in range(count):
+            line = line_of(row)
+            work = work_a.at[row]
+            store_spread(in_f[f, line // BY, line % BY], (ra_x, ra_y)[f], line * 256, work)
+            for pair in range(4):
+                both = outgoing(work, pair, line)
+                out[row * 256 + pair * 64 : row * 256 + pair * 64 + 64, :] = side_by_side(both[0:64], both[64:128])
 
     @pl.loop(0, BX)
     def _(x):
@@ -286,9 +282,10 @@
 
     for x in range(BX):
 
-        @pl.loop(0, BY // 2)
+        @pl.loop(0, 2)
         def _(half):
-            for y in (half * 2, half * 2 + 1):
+            for k in range(BY // 2):
+                y = half * (BY // 2) + k
                 line = x * BY + y
                 from_y = jnp.where(y > 0, line - 1, line)
                 into_y = jnp.where(y > 0, (line - 1) * BZ, CELLS)
@@ -405,17 +402,17 @@
 
     for count, after, base in ((BY, p_xp, right_xp), (BX, p_yp, right_yp)):
 
-        @sweep(count, 2)
-        def _(line, k):
+        for line in range(count):
+            k = line
             spread_twice(after[line], work_b.at[k])
             store_right(right, base + line, work_b.at[k])
 
-    @sweep(LINES, 8)
+    @sweep(LINES, 12)
     def _(line, k):
         low = lane_low((32, 128))
         here = p_zp[pl.ds(pl.multiple_of(line * 32, 32), 32), :].astype(F32)
         turned = pltpu.roll(here, 64, axis=1)
-        work = work_b.at[k % 2, pl.ds(k // 2 * 64, 64)]
+        work = work_b.at[k % BY, pl.ds(k // BY * 64, 64)]
         work[pl.ds(0, 32, stride=2), :] = jnp.where(low, here, turned)
         work[pl.ds(1, 32, stride=2), :] = jnp.where(low, turned, here)
         at = pl.multiple_of((right_zp * 8 + line) * 64, 64)
@@ -432,17 +429,17 @@
         b_low[places[0]] += out
         b_high[places[1]] += out
 
-    @sweep(BY, 2)
+    @sweep(BY, 6)
     def _(y, _turn):
         for z in range(0, BZ, 2):
             rim_terms(right_x, y * BZ + z, m_x, y * 256 + z * 32, [keys[1, y, 0, z + k] for k in range(2)])
 
-    @sweep(BX, 2)
+    @sweep(BX, 4)
     def _(x, _turn):
         for z in range(0, BZ, 2):
             rim_terms(right_y, x * BZ + z, m_y, x * 256 + z * 32, [keys[3, 0, x, z + k] for k in range(2)])
 
-    @sweep(LINES // 2, 4)
+    @sweep(LINES // 2, 12)
     def _(half, _turn):
         line = half * 2
         places = [keys[5, line % BY + k, line // BY, 0] for k in range(2)]
@@ -451,21 +448,21 @@
     for copy in brought:
         copy.wait()
 
-    @sweep(BY, 3)
+    @sweep(BY, 6)
     def _(y, _turn):
         for z in range(0, BZ, 2):
             e = ((BX - 1) * BY + y) * BZ + z
             at = y * 256 + z * 32
             couples(right, (right_xp + y) * 8 + z, 1, couple, [(1, face_x, [at, at + 32], [e, e + 1])])
 
-    @sweep(BX, 2)
+    @sweep(BX, 4)
     def _(x, _turn):
         for z in range(0, BZ, 2):
             e = (x * BY + BY - 1) * BZ + z
             at = x * 256 + z * 32
             couples(right, (right_yp + x) * 8 + z, 1, couple, [(2, face_y, [at, at + 32], [e, e + 1])])
 
-    @sweep(LINES // 2, 6)
+    @sweep(LINES // 2, 12)
     def _(half, _turn):
         line = half * 2
         e = line * BZ + BZ - 1
@@ -484,7 +481,7 @@
                     (b_low, b_high)[f % 2][key_b] += term
 
 
-    @sweep(LINES, 2)
+    @sweep(LINES, 4)
     def _(line, _turn):
         x, y = line // BY, line % BY
         next_x, next_y = jnp.minimum(x + 1, BX - 1), jnp.minimum(y + 1, BY - 1)
@@ -507,8 +504,7 @@
     for copy in marks:
         copy.wait()
 
-    @pl.loop(0, depth)
-    def _(c):
+    for c in range(depth):
         tally[c] = 0
 
     def fold(r):
@@ -544,15 +540,13 @@
             sems.at[r],
         ).start()
 
-    @pl.loop(0, AGG_DEV // 2)
-    def _(half):
-        pair = (half * 2, half * 2 + 1)
+    @pl.loop(0, AGG_DEV // 4)
+    def _(turn):
         for step in (fold, lay_out, hand_out):
-            for r in pair:
-                step(r)
-
-    @pl.loop(0, AGG_DEV)
-    def _(r):
+            for k in range(4):
+                step(turn * 4 + k)
+
+    for r in range(AGG_DEV):
         pltpu.make_async_copy(rows.at[pl.ds(0, ROW)], send.at[0, pl.ds(0, ROW)], sems.at[r]).wait()
 
 
@@ -576,7 +570,7 @@
             pltpu.VMEM((beyond * 512, 128), BF16),
             pltpu.VMEM((CELLS * 64, 128), BF16),
             pltpu.VMEM((CELLS * 64, 256), BF16),
-            pltpu.VMEM((2, 8 * STEP_TWICE, 128), F32),
+            pltpu.VMEM((BY, 8 * STEP_TWICE, 128), F32),
             pltpu.VMEM((KEYS + 1, 64, 128), F32),
             pltpu.VMEM((KEYS + 1, 64, 128), F32),
             pltpu.VMEM((KEYS + 1, 64, 128), F32),
@@ -595,7 +589,7 @@
 GROUP, ROW_STEP, ROW_PARTS = 8, ROW + 4, 4
 
 
-def place_kernel(taken, out, told, counts, tally, source, held, work, shaped, sems, row_sems, out_sems):
+def place_kernel(taken, out, told, counts, tally, source, held, works, shaped, sems, row_sems, out_sems):
     depth, count = taken.shape[0], out.shape[1]
     loads = [
         pltpu.make_async_copy(taken.at[:, pl.ds(k * ROW, 16)], told.at[k], sems.at[k]) for k in range(PLACES)
@@ -610,10 +604,6 @@
         copy.start()
         brought.append(copy)
 
-    @pl.loop(0, count + PLACES)
-    def _(t):
-        source[t] = 0
-
     for load in loads:
         load.wait()
     for c in range(depth):
@@ -623,12 +613,11 @@
     move.start()
     move.wait()
 
-    def order(c, total):
+    total = 0
+    for c in range(depth):
         for k in range(PLACES):
             source[total + k] = c * PLACES + k
-        return total + tally[c, 0]
-
-    total = lax.fori_loop(0, depth, order, 0)
+        total += tally[c, 0]
 
     for copy in brought:
         copy.wait()
@@ -637,8 +626,9 @@
         rows = pl.ds(pl.multiple_of(group * GROUP, GROUP), GROUP)
         return pltpu.make_async_copy(shaped.at[group], out.at[:, rows, :], out_sems.at[group])
 
-    @pl.loop(0, count // GROUP)
-    def _(group):
+    @sweep(count // GROUP, 2)
+    def _(group, side):
+        work = works.at[side]
         for k in range(GROUP):
             t = group * GROUP + k
             at = jnp.where(t < total, source[t], 0)
@@ -651,8 +641,7 @@
                 shaped[group, s, :, tile * 128 : tile * 128 + 128] = piece.astype(BF16)
         out_copy(group).start()
 
-    @pl.loop(0, count // GROUP)
-    def _(group):
+    for group in range(count // GROUP):
         out_copy(group).wait()
 
 
@@ -671,7 +660,7 @@
             pltpu.SMEM((depth, 128), jnp.int32),
             pltpu.SMEM((count + PLACES,), jnp.int32),
             pltpu.VMEM((depth, PACK, 128), BF16),
-            pltpu.VMEM((GROUP * ROW_STEP, 128), F32),
+            pltpu.VMEM((2, GROUP * ROW_STEP, 128), F32),
             pltpu.VMEM((count // GROUP, SLOTS, GROUP, NODES * NODES), BF16),
             pltpu.SemaphoreType.DMA((PLACES + 1,)),
             pltpu.SemaphoreType.DMA((ROW_PARTS,)),

time: 107 us -> 102 us (0.953)
  Pallas kernels: 52.8 us -> 47.6 us
    pallas_call x1, Pallas kernels: 22 us -> 17.8 us  [coarse_rows(): pl.pallas_call(compute_kernel, out_shape=jax.ShapeDtypeStruct((depth, PAC...]
where the time goes in v9:
time: 102 us
  blocking collectives  54.3 us (53%)
  Pallas kernels  47.6 us (47%)
    all_to_all x1, blocking collectives, shards(): taken = lax.all_to_all(send, 'gz', 0, 0, tiled=True)  54.3 us
    pallas_call x1, Pallas kernels, inner(): pl.pallas_call(inner_kernel, out_shape=[jax.ShapeDtypeStruct(shape, BF16)...  25 us
    pallas_call x1, Pallas kernels, coarse_rows(): pl.pallas_call(compute_kernel, out_shape=jax.ShapeDtypeStruct((depth, PAC...  17.8 us
    pallas_call x1, Pallas kernels, place_rows(): pl.pallas_call(place_kernel, out_shape=jax.ShapeDtypeStruct((SLOTS, count...  4.79 us

profile of v9, /device:TPU:0, one launch (start us, length us, event | category | flops | bytes accessed | tf_op | source)
XLA Modules:
  0.0 101.9 jit_solution(11307992056548365258)
XLA Ops:
  0.0 25.0 %inner.1 = (bf16[1536,128]{1,0:T(8,128)(2,1)}, bf16[1024,128]{1,0:T(8,128)(2,1)}, bf16[768,128]{1,0:T(8,128)(2,1)}, bf16[6,8,4096]{2,1,0:T(8,128)(2,1)}, bf16[4,...) custom-call(bf16[4,6,8,4096]{3,2,1,0:T(8,128)(2,1)} %prolong.1, ...), custom_call_target="tpu_custom_call" | custom-call | tf_op jit(solution)/shard_map/inner/pallas_call | solution.py:325
  25.0 17.8 %coarse_rows.1 = bf16[32,448,128]{2,1,0:T(8,128)(2,1)} custom-call(s32[6,4,8]{2,1,0:T(4,128)} %bitcast.6, s32[7,6,4,8]{3,2,1,0:T(4,128)} %bitcast.5, s32[24]{0:T(128)} %owner.1, bf16[1536,128]{1,0:T(8,128)(2,1)} %get-tuple-element.19.refs_0_, bf16[1024,128]{1,0:T(8,128)(2,1)} %get-tuple-element.20.refs_1_, bf16[768,128]{1,0:T(8,128)(2,1)} %get-tuple-element.21.refs_2_, ...), custom_call_target="tpu_custom_call" | custom-call | tf_op jit(solution)/shard_map/coarse_rows/pallas_call | solution.py:558
  42.8 54.3 %all_to_all.5.taken = bf16[32,448,128]{2,1,0:T(8,128)(2,1)} all-to-all(bf16[32,448,128]{2,1,0:T(8,128)(2,1)} %coarse_rows.1), channel_id=1, replica_groups=mesh['gx'=2,'gy'=2,'gz'=32] {'gz'}, dimensions={0} | all-to-all | bytes 7340032 | tf_op jit(solution)/shard_map/all_to_all | solution.py:683
  97.1 4.8 %place_rows.1 = bf16[7,64,4096]{2,1,0:T(8,128)(2,1)} custom-call(bf16[32,448,128]{2,1,0:T(8,128)(2,1)} %all_to_all.5.taken), custom_call_target="tpu_custom_call" | custom-call | tf_op jit(solution)/shard_map/place_rows/pallas_call | solution.py:652

commit v10 on v9

--- a/solution.py
+++ b/solution.py
@@ -123,13 +123,14 @@
     barrier = pltpu.get_barrier_semaphore()
     for target in ({"gx": 1 - gx}, {"gy": 1 - gy}, {"gz": next_z}, {"gz": previous_z}):
         pl.semaphore_signal(barrier, inc=1, device_id=target, device_id_type=MESH)
-    last_x, inner_x = pl.ds(BX - 1, 1), pl.ds(0, BX - 1)
+    last_x, inner_x, inner_y = pl.ds(BX - 1, 1), pl.ds(0, BX - 1), pl.ds(0, BY - 1)
     load_parts = (
         (prolong, in_p),
+        (a_face.at[1, :, BY - 1], in_f.at[1, :, BY - 1]),
+        (a_face.at[2], in_f.at[2]),
         (a_face.at[0, last_x], in_f.at[0, last_x]),
-        (a_face.at[1], in_f.at[1]),
-        (a_face.at[2], in_f.at[2]),
         (a_diag, in_d),
+        (a_face.at[1, :, inner_y], in_f.at[1, :, inner_y]),
         (a_face.at[0, inner_x], in_f.at[0, inner_x]),
     )
     loads = [pltpu.make_async_copy(*part, load_sems.at[k]) for k, part in enumerate(load_parts)]
@@ -137,7 +138,6 @@
         load.start()
     zero[...] = jnp.zeros_like(zero)
     zero_m[...] = jnp.zeros_like(zero_m)
-    pl.semaphore_wait(barrier, 4)
 
     def exchange(number, source, dest, target, sends, receives, blank):
         copy = pltpu.make_async_remote_copy(
@@ -181,32 +181,6 @@
 
     def pass_down(number, axis, source, dest, blank):
         return exchange(number, source, dest, to_line(axis, -1), has_line(axis, -1), has_line(axis, 1), blank)
-
-    ends = [
-        pass_down(0, "gy", prolong.at[:, 0], p_yp, zero.at[pl.ds(0, BX)]),
-        pass_down(1, "gx", prolong.at[0], p_xp, zero),
-    ]
-    loads[0].wait()
-
-    @pl.loop(0, BX)
-    def _(x):
-        low = lane_low((32, 128))
-        for y in range(BY):
-            line = x * BY + y
-            at = pl.ds(pl.multiple_of(line * 32, 32), 32)
-            natural = work_b.at[y]
-            spread_twice(in_p[x, y], natural)
-            even, odd = (natural[pl.ds(p, 32, stride=2), :] for p in range(2))
-            out_p_first[at, :] = jnp.where(low, even, odd).astype(BF16)
-            ra_z[pl.ds(pl.multiple_of(line * 288, 32), 32), :] = jnp.zeros((32, 128), BF16)
-            store_right(right, line, natural)
-            first_z[pl.ds(pl.multiple_of(line * 64, 64), 64), :] = natural[0:64, :].astype(BF16)
-            store_left(left, line, natural)
-
-    ends.append(pass_down(2, "gz", out_p_first, p_zp, zero_m.at[pl.ds(0, LINES * 32)]))
-    loads[1].wait()
-    loads[2].wait()
-    loads[3].wait()
 
     def outgoing(work, pair, line):
         blocks = []
@@ -220,11 +194,7 @@
     def side_by_side(first, second):
         return jnp.where(lane_low((64, 128)), first, pltpu.roll(second, 64, axis=1)).astype(BF16)
 
-    for f, count, out, line_of in (
-        (0, BY, out_mx, lambda k: (BX - 1) * BY + k),
-        (1, BX, out_my, lambda k: k * BY + BY - 1),
-    ):
-
+    def face(f, count, out, line_of):
         for row in range(count):
             line = line_of(row)
             work = work_a.at[row]
@@ -232,6 +202,37 @@
             for pair in range(4):
                 both = outgoing(work, pair, line)
                 out[row * 256 + pair * 64 : row * 256 + pair * 64 + 64, :] = side_by_side(both[0:64], both[64:128])
+
+    def factors(x, y, natural):
+        line = x * BY + y
+        at = pl.ds(pl.multiple_of(line * 32, 32), 32)
+        spread_twice(in_p[x, y], natural)
+        even, odd = (natural[pl.ds(p, 32, stride=2), :] for p in range(2))
+        out_p_first[at, :] = jnp.where(lane_low((32, 128)), even, odd).astype(BF16)
+        ra_z[pl.ds(pl.multiple_of(line * 288, 32), 32), :] = jnp.zeros((32, 128), BF16)
+        store_right(right, line, natural)
+        first_z[pl.ds(pl.multiple_of(line * 64, 64), 64), :] = natural[0:64, :].astype(BF16)
+        store_left(left, line, natural)
+
+    loads[0].wait()
+    for x in range(BX):
+        factors(x, BY - 1, work_b.at[x])
+    loads[1].wait()
+    face(1, BX, out_my, lambda k: k * BY + BY - 1)
+    pl.semaphore_wait(barrier, 4)
+    ends = [
+        pass_up(3, "gy", out_my, m_y, zero_m.at[pl.ds(0, BX * 256)]),
+        pass_down(0, "gy", prolong.at[:, 0], p_yp, zero.at[pl.ds(0, BX)]),
+        pass_down(1, "gx", prolong.at[0], p_xp, zero),
+    ]
+
+    @pl.loop(0, BX)
+    def _(x):
+        for y in range(BY - 1):
+            factors(x, y, work_b.at[y])
+
+    ends.append(pass_down(2, "gz", out_p_first, p_zp, zero_m.at[pl.ds(0, LINES * 32)]))
+    loads[2].wait()
 
     @pl.loop(0, BX)
     def _(x):
@@ -247,10 +248,12 @@
             at = pl.multiple_of((x * BY + y) * 32, 64)
             out_mz[pl.ds(at, 64), :] = side_by_side(*last)
 
-    for number, axis, source, dest in ((3, "gy", out_my, m_y), (4, "gz", out_mz, m_z), (5, "gx", out_mx, m_x)):
-        ends.append(pass_up(number, axis, source, dest, zero_m.at[pl.ds(0, source.shape[0])]))
-    loads[4].wait()
-    loads[5].wait()
+    ends.append(pass_up(4, "gz", out_mz, m_z, zero_m.at[pl.ds(0, LINES * 32)]))
+    loads[3].wait()
+    face(0, BY, out_mx, lambda k: (BX - 1) * BY + k)
+    ends.append(pass_up(5, "gx", out_mx, m_x, zero_m))
+    for load in loads[4:]:
+        load.wait()
 
     @pl.loop(0, BX)
     def _(x):
@@ -348,7 +351,7 @@
             pltpu.VMEM(((CELLS + BZ) * 64, 256), BF16),
             pltpu.VMEM((BY, 8 * STEP, 128), F32),
             pltpu.VMEM((BY, 8 * STEP_TWICE, 128), F32),
-            pltpu.SemaphoreType.DMA((6,)),
+            pltpu.SemaphoreType.DMA((7,)),
             pltpu.SemaphoreType.DMA((6,)),
             pltpu.SemaphoreType.DMA((6,)),
             pltpu.SemaphoreType.DMA((6,)),

time: 102 us -> 98.9 us (0.970)
  Pallas kernels: 47.6 us -> 44.2 us
    pallas_call x1, Pallas kernels: 25 us -> 21.6 us  [inner(): pl.pallas_call(inner_kernel, out_shape=[jax.ShapeDtypeStruct(shape, BF16)...]
where the time goes in v10:
time: 98.9 us; the launch traced here: 98.7 us
  blocking collectives  54.5 us (55%)
  Pallas kernels  44.2 us (45%)
    all_to_all x1, blocking collectives, shards(): taken = lax.all_to_all(send, 'gz', 0, 0, tiled=True)  54.5 us
    pallas_call x1, Pallas kernels, inner(): pl.pallas_call(inner_kernel, out_shape=[jax.ShapeDtypeStruct(shape, BF16)...  21.6 us
    pallas_call x1, Pallas kernels, coarse_rows(): pl.pallas_call(compute_kernel, out_shape=jax.ShapeDtypeStruct((depth, PAC...  17.8 us
    pallas_call x1, Pallas kernels, place_rows(): pl.pallas_call(place_kernel, out_shape=jax.ShapeDtypeStruct((SLOTS, count...  4.79 us

profile of v10, /device:TPU:0, one launch (start us, length us, event | category | flops | bytes accessed | tf_op | source)
XLA Modules:
  0.0 98.7 jit_solution(4700712615766423573)
XLA Ops:
  0.0 21.6 %inner.1 = (bf16[1536,128]{1,0:T(8,128)(2,1)}, bf16[1024,128]{1,0:T(8,128)(2,1)}, bf16[768,128]{1,0:T(8,128)(2,1)}, bf16[6,8,4096]{2,1,0:T(8,128)(2,1)}, bf16[4,...) custom-call(bf16[4,6,8,4096]{3,2,1,0:T(8,128)(2,1)} %prolong.1, ...), custom_call_target="tpu_custom_call" | custom-call | tf_op jit(solution)/shard_map/inner/pallas_call | solution.py:328
  21.6 17.8 %coarse_rows.1 = bf16[32,448,128]{2,1,0:T(8,128)(2,1)} custom-call(s32[6,4,8]{2,1,0:T(4,128)} %bitcast.6, s32[7,6,4,8]{3,2,1,0:T(4,128)} %bitcast.5, s32[24]{0:T(128)} %owner.1, bf16[1536,128]{1,0:T(8,128)(2,1)} %get-tuple-element.19.refs_0_, bf16[1024,128]{1,0:T(8,128)(2,1)} %get-tuple-element.20.refs_1_, bf16[768,128]{1,0:T(8,128)(2,1)} %get-tuple-element.21.refs_2_, ...), custom_call_target="tpu_custom_call" | custom-call | tf_op jit(solution)/shard_map/coarse_rows/pallas_call | solution.py:561
  39.4 54.5 %all_to_all.5.taken = bf16[32,448,128]{2,1,0:T(8,128)(2,1)} all-to-all(bf16[32,448,128]{2,1,0:T(8,128)(2,1)} %coarse_rows.1), channel_id=1, replica_groups=mesh['gx'=2,'gy'=2,'gz'=32] {'gz'}, dimensions={0} | all-to-all | bytes 7340032 | tf_op jit(solution)/shard_map/all_to_all | solution.py:686
  93.9 4.8 %place_rows.1 = bf16[7,64,4096]{2,1,0:T(8,128)(2,1)} custom-call(bf16[32,448,128]{2,1,0:T(8,128)(2,1)} %all_to_all.5.taken), custom_call_target="tpu_custom_call" | custom-call | tf_op jit(solution)/shard_map/place_rows/pallas_call | solution.py:655

commit v11 on v10

--- a/solution.py
+++ b/solution.py
@@ -55,22 +55,14 @@
 def couples(right, cell, stride, couple, blocks):
     low = lane_low((64, 128))
     zero = jnp.zeros((64, 128), BF16)
-    wide = jnp.zeros((128, 128), BF16)
-    columns = []
     for k in range(2):
         block = right[pl.ds(pl.multiple_of((cell + k * stride) * 64, 64), 64), :]
-        corner = jnp.concatenate([jnp.where(low, block, zero), jnp.where(low, zero, block)], axis=0)
-        columns.append(jnp.concatenate([corner, wide] if k == 0 else [wide, corner], axis=0))
-    weight = jnp.concatenate(columns, axis=1)
-    stack = [
-        jnp.concatenate([ref[pl.ds(pl.multiple_of(at, 32), 32), :] for at in ats], axis=1)
-        for _, ref, ats, _ in blocks
-    ]
-    stack = jnp.concatenate(stack, axis=0) if len(stack) > 1 else stack[0]
-    both = jnp.dot(stack, weight, preferred_element_type=F32)
-    for number, (f, _, _, cells) in enumerate(blocks):
-        for k in range(2):
-            part = both[number * 32 : number * 32 + 32, k * 128 : k * 128 + 128]
+        weight = jnp.concatenate([jnp.where(low, block, zero), jnp.where(low, zero, block)], axis=0)
+        stack = [ref[pl.ds(pl.multiple_of(ats[k], 32), 32), :] for _, ref, ats, _ in blocks]
+        stack = jnp.concatenate(stack, axis=0) if len(stack) > 1 else stack[0]
+        both = jnp.dot(stack, weight, preferred_element_type=F32)
+        for number, (f, _, _, cells) in enumerate(blocks):
+            part = both[number * 32 : number * 32 + 32]
             turned = pltpu.roll(part, 64, axis=1)
             side = f % 2 * 64
             for p in range(2):
@@ -125,8 +117,9 @@
         pl.semaphore_signal(barrier, inc=1, device_id=target, device_id_type=MESH)
     last_x, inner_x, inner_y = pl.ds(BX - 1, 1), pl.ds(0, BX - 1), pl.ds(0, BY - 1)
     load_parts = (
-        (prolong, in_p),
+        (prolong.at[:, BY - 1], in_p.at[:, BY - 1]),
         (a_face.at[1, :, BY - 1], in_f.at[1, :, BY - 1]),
+        (prolong.at[:, inner_y], in_p.at[:, inner_y]),
         (a_face.at[2], in_f.at[2]),
         (a_face.at[0, last_x], in_f.at[0, last_x]),
         (a_diag, in_d),
@@ -226,13 +219,15 @@
         pass_down(1, "gx", prolong.at[0], p_xp, zero),
     ]
 
+    loads[2].wait()
+
     @pl.loop(0, BX)
     def _(x):
         for y in range(BY - 1):
             factors(x, y, work_b.at[y])
 
     ends.append(pass_down(2, "gz", out_p_first, p_zp, zero_m.at[pl.ds(0, LINES * 32)]))
-    loads[2].wait()
+    loads[3].wait()
 
     @pl.loop(0, BX)
     def _(x):
@@ -249,10 +244,10 @@
             out_mz[pl.ds(at, 64), :] = side_by_side(*last)
 
     ends.append(pass_up(4, "gz", out_mz, m_z, zero_m.at[pl.ds(0, LINES * 32)]))
-    loads[3].wait()
+    loads[4].wait()
     face(0, BY, out_mx, lambda k: (BX - 1) * BY + k)
     ends.append(pass_up(5, "gx", out_mx, m_x, zero_m))
-    for load in loads[4:]:
+    for load in loads[5:]:
         load.wait()
 
     @pl.loop(0, BX)
@@ -351,7 +346,7 @@
             pltpu.VMEM(((CELLS + BZ) * 64, 256), BF16),
             pltpu.VMEM((BY, 8 * STEP, 128), F32),
             pltpu.VMEM((BY, 8 * STEP_TWICE, 128), F32),
-            pltpu.SemaphoreType.DMA((7,)),
+            pltpu.SemaphoreType.DMA((8,)),
             pltpu.SemaphoreType.DMA((6,)),
             pltpu.SemaphoreType.DMA((6,)),
             pltpu.SemaphoreType.DMA((6,)),
@@ -519,7 +514,7 @@
                 pair = jnp.where(low, b_low[at[0]], b_high[at[1]])
                 pair += pltpu.roll(jnp.where(low, b_low[at[1]], b_high[at[0]]), 64, axis=1)
                 blocks.append(pair)
-            flipped = jnp.concatenate(blocks, axis=0).T
+            flipped = jnp.concatenate(blocks, axis=0).astype(BF16).T.astype(F32)
             for k in range(s, min(s + 4, SLOTS)):
                 ref = f_low if k < s + 2 else f_high
                 ref[r * SLOTS + k] += flipped[k % 2 * 64 : k % 2 * 64 + 64]

time: 98.9 us -> 99.5 us (level)
  no operation moved by 1% of the time
where the time goes in v11:
time: 99.5 us; the launch traced here: 99.3 us
  blocking collectives  54.7 us (55%)
  Pallas kernels  44.5 us (45%)
    all_to_all x1, blocking collectives, shards(): taken = lax.all_to_all(send, 'gz', 0, 0, tiled=True)  54.7 us
    pallas_call x1, Pallas kernels, inner(): pl.pallas_call(inner_kernel, out_shape=[jax.ShapeDtypeStruct(shape, BF16)...  21.4 us
    pallas_call x1, Pallas kernels, coarse_rows(): pl.pallas_call(compute_kernel, out_shape=jax.ShapeDtypeStruct((depth, PAC...  18.4 us
    pallas_call x1, Pallas kernels, place_rows(): pl.pallas_call(place_kernel, out_shape=jax.ShapeDtypeStruct((SLOTS, count...  4.79 us

profile of v11, /device:TPU:0, one launch (start us, length us, event | category | flops | bytes accessed | tf_op | source)
XLA Modules:
  0.0 99.3 jit_solution(17639914836037151278)
XLA Ops:
  0.0 21.4 %inner.1 = (bf16[1536,128]{1,0:T(8,128)(2,1)}, bf16[1024,128]{1,0:T(8,128)(2,1)}, bf16[768,128]{1,0:T(8,128)(2,1)}, bf16[6,8,4096]{2,1,0:T(8,128)(2,1)}, bf16[4,...) custom-call(bf16[4,6,8,4096]{3,2,1,0:T(8,128)(2,1)} %prolong.1, ...), custom_call_target="tpu_custom_call" | custom-call | tf_op jit(solution)/shard_map/inner/pallas_call | solution.py:323
  21.4 18.4 %coarse_rows.1 = bf16[32,448,128]{2,1,0:T(8,128)(2,1)} custom-call(s32[6,4,8]{2,1,0:T(4,128)} %bitcast.6, s32[7,6,4,8]{3,2,1,0:T(4,128)} %bitcast.5, s32[24]{0:T(128)} %owner.1, bf16[1536,128]{1,0:T(8,128)(2,1)} %get-tuple-element.19.refs_0_, bf16[1024,128]{1,0:T(8,128)(2,1)} %get-tuple-element.20.refs_1_, bf16[768,128]{1,0:T(8,128)(2,1)} %get-tuple-element.21.refs_2_, ...), custom_call_target="tpu_custom_call" | custom-call | tf_op jit(solution)/shard_map/coarse_rows/pallas_call | solution.py:556
  39.7 54.7 %all_to_all.5.taken = bf16[32,448,128]{2,1,0:T(8,128)(2,1)} all-to-all(bf16[32,448,128]{2,1,0:T(8,128)(2,1)} %coarse_rows.1), channel_id=1, replica_groups=mesh['gx'=2,'gy'=2,'gz'=32] {'gz'}, dimensions={0} | all-to-all | bytes 7340032 | tf_op jit(solution)/shard_map/all_to_all | solution.py:681
  94.5 4.8 %place_rows.1 = bf16[7,64,4096]{2,1,0:T(8,128)(2,1)} custom-call(bf16[32,448,128]{2,1,0:T(8,128)(2,1)} %all_to_all.5.taken), custom_call_target="tpu_custom_call" | custom-call | tf_op jit(solution)/shard_map/place_rows/pallas_call | solution.py:650
